TPU v7x, 128 devices: a whole 4x4x4 slice. The times are simulated.
128 devices in a mesh: shot: 32 (over y, x_lo, z), slab: 4 (over x_hi, core).
Axes of the slice: x: 4 (x_hi: 2, x_lo: 2; x = x_hi * 2 + x_lo), y: 4, z: 4, core: 2. Of those that a mesh axis runs over, the one named last changes fastest.
Arguments:
- forward_state: float32 [32, 9, 32, 32, 128], P('shot', None, 'slab'), may hold values from -6 to 6
- adjoint_state: float32 [32, 9, 32, 32, 128], P('shot', None, 'slab'), may hold values from -6 to 6
- materials: float32 [10, 32, 32, 128], P(None, 'slab', 'shot'), may hold values from 0.1 to 2, as said below
- wavelet: float32 [4], replicated, may hold values from -4 to 4
- encoding: int32 [32, 16], P('shot'), may hold values from 0 to 1
- source_cells: int32 [32, 16], P('shot'), may hold values from 0 to 131071
- receiver_depth: int32 [32, 32], P('slab'), may hold values from 0 to 3
- receiver_data: float32 [32, 4, 32, 32], P('shot', None, 'slab'), may hold values from -6 to 6
Outputs:
- forward_out: float32 [32, 9, 32, 32, 128], P('shot', None, 'slab')
- adjoint_out: float32 [32, 9, 32, 32, 128], P('shot', None, 'slab')
- gradient: float32 [10, 32, 32, 128], P(None, 'slab', 'shot')
Inputs may be any that keep to these rules, and one draw needn't show every extreme that they name: `materials`: row 0 lies in 0.5 to 1; rows 1, 4, 6 in 1 to 2; rows 2, 3, 5 in 0.1 to 0.4; rows 7, 8, 9 in 0.3 to 1.
All inputs are finite; a program needn't handle non-finite values.
Results may differ from a plain program's by a relative error of at most 0.0001.
Values sent between devices are 32-bit elements; how exact they have to be, the bound alone decides.
No kernel may reach another device: no remote copies, remote signals or barrier semaphores. Data moves between devices by JAX's collectives and lax.ppermute only.
A program may use at most 64 MiB of HBM per device.

v0:
```python
import jax
import jax.numpy as jnp
from jax import lax
from jax.sharding import PartitionSpec as P

STEPS = 4


step_size = 0.25


def passed_along(value, axis, by):
    peers = lax.axis_size(axis)
    pairs = [(i, i + by) for i in range(peers) if 0 <= i + by < peers]
    return lax.ppermute(value, axis, pairs)


def in_blocks(value, dim, peers):
    shape = value.shape
    tiles = value.reshape(*shape[:dim], peers, shape[dim] // peers, *shape[dim + 1 :])
    return jnp.moveaxis(tiles, dim, 0)


def summed_on_arrival(value, axis, dim):
    peers = lax.axis_size(axis)
    tiles = lax.all_to_all(in_blocks(value, dim, peers), axis, 0, 0, tiled=True)
    return jnp.sum(tiles, axis=0)


def copy_for_each(value, axis):
    copies = jnp.broadcast_to(value, (lax.axis_size(axis), *value.shape))
    return lax.all_to_all(copies, axis, split_axis=0, concat_axis=0, tiled=True)


def in_order(tiles, dim):
    tiles = jnp.moveaxis(tiles, 0, dim)
    shape = tiles.shape
    return tiles.reshape(*shape[:dim], shape[dim] * shape[dim + 1], *shape[dim + 2 :])


def gather_directly(value, axis, dim):
    tiles = copy_for_each(value, axis)
    return in_order(tiles, dim)


def diff_up(values, direction):
    length = values.shape[direction]
    ahead = lax.slice_in_dim(values, 1, length, axis=direction)
    zero_layer = jnp.zeros_like(lax.slice_in_dim(values, 0, 1, axis=direction))
    return jnp.concatenate([ahead, zero_layer], axis=direction) - values


def diff_down(values, direction):
    length = values.shape[direction]
    behind = lax.slice_in_dim(values, 0, length - 1, axis=direction)
    zero_layer = jnp.zeros_like(lax.slice_in_dim(values, 0, 1, axis=direction))
    return values - jnp.concatenate([zero_layer, behind], axis=direction)


def rim_up(values, first_above):
    return jnp.concatenate([values[:, 1:], first_above[:, None]], axis=1) - values


def rim_down(values, last_below):
    return values - jnp.concatenate([last_below[:, None], values[:, :-1]], axis=1)


def rims(below_layers, above_layers):
    from_below = passed_along(below_layers, "slab", 1)
    from_above = passed_along(above_layers, "slab", -1)
    return (from_below, from_above)


def stress_rims(stress):
    below_layers = jnp.stack([stress[4][:, -1], stress[5][:, -1]])
    above_layers = stress[0][:, 0][None]
    from_below, from_above = rims(below_layers, above_layers)
    return (
        rim_up(stress[0], from_above[0]),
        rim_down(stress[5], from_below[1]),
        rim_down(stress[4], from_below[0]),
    )


def velocity_rims(velocity):
    below_layers = velocity[0][:, -1][None]
    above_layers = jnp.stack([velocity[1][:, 0], velocity[2][:, 0]])
    from_below, from_above = rims(below_layers, above_layers)
    return (
        rim_down(velocity[0], from_below[0]),
        rim_up(velocity[1], from_above[0]),
        rim_up(velocity[2], from_above[1]),
    )


def correlate_list(buoy_grad, strain, halfway):
    forward = [part[:halfway] for part in strain]
    adjoint = [part[halfway:] for part in strain]
    pairs = [(0, 0), (0, 1), (0, 2), (1, 1), (1, 2), (2, 2), (3, 3), (4, 4), (5, 5)]
    terms = [buoy_grad]
    for first, second in pairs:
        product = forward[first] * adjoint[second]
        if first != second:
            product = product + forward[second] * adjoint[first]
        terms.append(jnp.sum(product, axis=0))
    return terms


def make_sources(encoding, source_cells, start_cell, row_count, y_rows, z_rows):
    shot_count = source_cells.shape[0]
    span = row_count * y_rows * z_rows
    local_cell = source_cells - start_cell
    inside = (local_cell >= 0) & (local_cell < span)
    shot_base = lax.broadcasted_iota(jnp.int32, source_cells.shape, 0) * span
    target_cell = jnp.where(inside, local_cell + shot_base, shot_count * span)
    sign_values = (2 * encoding - 1).astype(jnp.float32)
    return (
        jnp.zeros((shot_count * span,), jnp.float32)
        .at[target_cell.reshape(-1)]
        .add(sign_values.reshape(-1), mode="drop")
        .reshape(shot_count, row_count, y_rows, z_rows)
    )


def run_tile(
    fields,
    buoyancy,
    stiffness,
    source_image,
    step_data,
    probe,
    wavelet,
    stress_edges,
    velocity_edges,
    keep_rows,
    shot_count,
):
    velocity = fields[0:3]
    stress = fields[3:9]
    y_rows, z_rows = (fields[0].shape[2], fields[0].shape[3])
    local_sum = [jnp.zeros((keep_rows, y_rows, z_rows), jnp.float32) for slot in range(10)]
    for step_index in range(STEPS):
        dx_sxx, dx_sxy, dx_sxz = stress_edges(stress)
        force_x = dx_sxx + diff_down(stress[5], 2) + diff_down(stress[4], 3)
        force_y = dx_sxy + diff_up(stress[1], 2) + diff_down(stress[3], 3)
        force_z = dx_sxz + diff_down(stress[3], 2) + diff_up(stress[2], 3)
        forces = [force_x, force_y, force_z]
        buoy_grad = jnp.sum(
            force_x[:shot_count] * velocity[0][shot_count:]
            + force_y[:shot_count] * velocity[1][shot_count:]
            + force_z[:shot_count] * velocity[2][shot_count:],
            axis=0,
        )
        velocity = [velocity[comp] + step_size * buoyancy * forces[comp] for comp in range(3)]
        dx_vx, dx_vy, dx_vz = velocity_edges(velocity)
        strain_yy = diff_down(velocity[1], 2)
        strain_zz = diff_down(velocity[2], 3)
        strain_yz = diff_up(velocity[1], 3) + diff_up(velocity[2], 2)
        strain_xz = diff_up(velocity[0], 3) + dx_vz
        strain_xy = diff_up(velocity[0], 2) + dx_vy
        strain = [dx_vx, strain_yy, strain_zz, strain_yz, strain_xz, strain_xy]
        inject = jnp.concatenate(
            [
                wavelet[step_index] * source_image,
                step_data[:, step_index][:, :, :, None] * probe[None],
            ],
            axis=0,
        )
        stress = [
            stress[0]
            + step_size
            * (stiffness[0] * dx_vx + stiffness[1] * strain_yy + stiffness[2] * strain_zz),
            stress[1]
            + step_size
            * (stiffness[1] * dx_vx + stiffness[3] * strain_yy + stiffness[4] * strain_zz),
            stress[2]
            + step_size
            * (stiffness[2] * dx_vx + stiffness[4] * strain_yy + stiffness[5] * strain_zz)
            + inject,
            stress[3] + step_size * stiffness[6] * strain_yz,
            stress[4] + step_size * stiffness[7] * strain_xz,
            stress[5] + step_size * stiffness[8] * strain_xy,
        ]
        kept_strain = [part for part in strain]
        terms = correlate_list(buoy_grad, kept_strain, shot_count)
        local_sum = [local_sum[slot] + terms[slot] for slot in range(10)]
    summed = summed_on_arrival(jnp.stack(local_sum), "shot", 2)
    final_fields = [part for part in velocity + stress]
    return (final_fields, summed)


def body(
    forward_state,
    adjoint_state,
    materials,
    wavelet,
    encoding,
    source_cells,
    receiver_depth,
    receiver_data,
):
    shot_count, comp_count, x_rows, y_rows, z_rows = forward_state.shape
    cell_count = x_rows * y_rows * z_rows
    buoyancy = gather_directly(materials[0:1], "shot", 2)[0]
    stiffness = gather_directly(materials[1:10], "shot", 2)
    probe = (
        lax.broadcasted_iota(jnp.int32, (x_rows, y_rows, z_rows), 2) == receiver_depth[:, :, None]
    ).astype(jnp.float32)
    fields = [
        jnp.concatenate([forward_state[:, comp], adjoint_state[:, comp]], axis=0)
        for comp in range(9)
    ]
    slab_start = lax.axis_index("slab") * cell_count
    source_image = make_sources(encoding, source_cells, slab_start, x_rows, y_rows, z_rows)
    final_fields, summed = run_tile(
        fields,
        buoyancy,
        stiffness,
        source_image,
        receiver_data,
        probe,
        wavelet,
        stress_rims,
        velocity_rims,
        x_rows,
        shot_count,
    )
    total_shots = shot_count * lax.axis_size("shot")
    gradient = summed * float(total_shots * STEPS) ** (-0.5)
    forward_out = jnp.stack([part[:shot_count] for part in final_fields], axis=1)
    adjoint_out = jnp.stack([part[shot_count:] for part in final_fields], axis=1)
    return (forward_out, adjoint_out, gradient)


def solution(mesh):
    return jax.shard_map(
        body,
        mesh=mesh,
        in_specs=(
            P("shot", None, "slab", None, None),
            P("shot", None, "slab", None, None),
            P(None, "slab", "shot", None),
            P(),
            P("shot", None),
            P("shot", None),
            P("slab", None),
            P("shot", None, "slab", None),
        ),
        out_specs=(
            P("shot", None, "slab", None, None),
            P("shot", None, "slab", None, None),
            P(None, "slab", "shot", None),
        ),
        check_vma=False,
    )
```

profile of v0, /device:TPU:1, one launch (start us, length us, event | category | flops | bytes accessed | tf_op | source)
XLA Modules:
  0.0 165.6 jit_solution(11110880464510325727)
XLA Ops:
  2.0 9.8 %all-to-all-start = ((f32[32,1,8,1,128]{4,2,3,1,0:T(8,128)}), f32[32,1,8,1,128]{4,2,3,1,0:T(8,128)S(1)}, u32[]{:S(2)}, u32[]{:S(2)}) async-start(f32[32,1,8,1,128]{4,2,3,1,0:T(8,128)} %broadcast_in_dim.8), calls=%async_computation | async-start | bytes 262144 | tf_op jit(solution)/shard_map/all_to_all | solution.py:32
  11.8 2.2 %slice_bitcast_fusion.31 = (f32[1,8,32,128]{3,2,0,1:T(8,128)S(1)}, f32[1,8,32,128]{3,2,0,1:T(8,128)S(1)}, f32[1,8,32,128]{3,2,0,1:T(8,128)}, f32[1,8,32,128]{3,2...) fusion(f32[1,9,8,32,128]{4,3,2,1,0:T(8,128)} %param.8), kind=kLoop, calls=%fused_computation.275 | loop fusion | bytes 2359296 | tf_op jit(solution)/shard_map/squeeze | solution.py:210
  14.0 0.8 slice_bitcast_fusion.30
  15.5 2.9 %collective-permute-start = (f32[1,2,32,128]{3,2,1,0:T(8,128)}, f32[1,2,32,128]{3,2,1,0:T(8,128)}, u32[]{:S(2)}, u32[]{:S(2)}) collective-permute-start(f32[1,2,32,128]{3,2,1,0:T(8,128)} %fusion.85), channel_id=1, source_target_pairs={{1,0},{2,1},{3,2},{5,4},{6,5},{7,6},{9,8},{10,9},{11,10},{13,12},{... | collective-permute-start | bytes 98312 | tf_op jit(solution)/shard_map/ppermute | solution.py:15
  18.5 4.3 %collective-permute-start.2 = (f32[2,2,32,128]{3,2,1,0:T(8,128)S(1)}, f32[2,2,32,128]{3,2,1,0:T(8,128)S(1)}, u32[]{:S(2)}, u32[]{:S(2)}) collective-permute-start(f32[2,2,32,128]{3,2,1,0:T(8,128)S(1)} %pad_maximum_fusion.6), channel_id=1, source_target_pairs={{0,1},{1,2},{2,3},{4,5},{5,6},{6,7},{8,9},{9,10},{10,11},{12,13},{... | collective-permute-start | bytes 196616 | tf_op jit(solution)/shard_map/ppermute | solution.py:15
  22.7 0.8 fusion.4
  24.2 0.8 fusion.37
  25.7 0.8 fusion.1
  26.5 0.9 fusion
  28.1 3.4 %broadcast_multiply_fusion.2 = (f32[32768]{0:T(1024)}, f32[32768]{0:T(1024)}, f32[32768]{0:T(1024)}, f32[32768]{0:T(1024)}) fusion(f32[32768]{0:T(1024)S(1)} %scatter_custom_fusion, f32[]{:T(128)} %bitcast.94, f32[]{:T(128)} %bitcast.86, f32[]{:T(128)} %bitcast.70, f32[]{:T(128)} %bitcast.52), kind=kLoop, calls=%fused_computation.297 | loop fusion | flops 131072 | bytes 655376 | tf_op jit(solution)/shard_map/mul | solution.py:164
  31.4 1.0 fusion.78
  33.8 1.1 broadcast_in_dim.9
  34.9 7.7 %all-to-all-start.1 = ((f32[32,9,8,1,128]{4,2,3,1,0:T(8,128)}), f32[32,9,8,1,128]{4,2,3,1,0:T(8,128)S(1)}, u32[]{:S(2)}, u32[]{:S(2)}) async-start(f32[32,9,8,1,128]{4,2,3,1,0:T(8,128)} %broadcast_in_dim.9), calls=%async_computation.1 | async-start | bytes 2359296 | tf_op jit(solution)/shard_map/all_to_all | solution.py:32
  42.7 2.1 %maximum_add_fusion.1 = (f32[2,8,32,128]{3,2,0,1:T(8,128)S(1)}, f32[2,8,32,128]{3,2,0,1:T(8,128)}) fusion(f32[1,8,32,128]{3,2,0,1:T(8,128)} %get-tuple-element.86, f32[1,8,32,128]{3,2,0,1:T(8,128)} %get-tuple-element.77, f32[8,32,128]{2,1,0:T(8,128)S(1)} %copy.66, f32[2,8,32,127]{3,2,0,1:T(8,128)} %get-tuple-element.185, ...), kind=kLoop, calls=%fused_computation.42 | loop fusion | flops 786432 | bytes 2480128 | tf_op jit(solution)/shard_map/add | solution.py:154
  44.9 0.9 maximum_add_fusion.2
  45.9 1.9 %collective-permute-start.4 = (f32[2,2,32,128]{3,2,1,0:T(8,128)S(1)}, f32[2,2,32,128]{3,2,1,0:T(8,128)S(1)}, u32[]{:S(2)}, u32[]{:S(2)}) collective-permute-start(f32[2,2,32,128]{3,2,1,0:T(8,128)S(1)} %pad_maximum_fusion.7), channel_id=1, source_target_pairs={{1,0},{2,1},{3,2},{5,4},{6,5},{7,6},{9,8},{10,9},{11,10},{13,12},{... | collective-permute-start | bytes 196616 | tf_op jit(solution)/shard_map/ppermute | solution.py:15
  47.8 1.7 %maximum_add_fusion = (f32[2,8,32,128]{3,2,0,1:T(8,128)S(1)}, f32[2,8,32,128]{3,2,0,1:T(8,128)}) fusion(f32[1,8,32,128]{3,2,0,1:T(8,128)S(1)} %copy-done.26, f32[1,8,32,128]{3,2,0,1:T(8,128)S(1)} %copy-done.25, f32[8,32,128]{2,1,0:T(8,128)S(1)} %copy.66, f32[2,8,32,127]{3,2,0,1:T(8,128)S(1)} %copy-done.7, f32[1,8,32,128]{3,2,0,1:T(8,128)S(1)} %get-tuple-element.87, ...), kind=kLoop, calls=%fused_computation.37 | loop fusion | flops 786432 | bytes 2480128 | tf_op jit(solution)/shard_map/add | solution.py:154
  50.9 0.9 slice.1041
  51.7 0.8 slice.1034
  53.9 0.8 slice.1055
  54.8 0.7 slice.1056
  55.5 5.1 %collective-permute-start.1 = (f32[1,2,32,128]{3,2,1,0:T(8,128)}, f32[1,2,32,128]{3,2,1,0:T(8,128)}, u32[]{:S(2)}, u32[]{:S(2)}) collective-permute-start(f32[1,2,32,128]{3,2,1,0:T(8,128)} %slice_bitcast_fusion.75), channel_id=1, source_target_pairs={{0,1},{1,2},{2,3},{4,5},{5,6},{6,7},{8,9},{9,10},{10,11},{12,13},{... | collective-permute-start | bytes 98312 | tf_op jit(solution)/shard_map/ppermute | solution.py:15
  61.5 0.7 copy-done.5
  63.1 2.3 %collective-permute-start.6 = (f32[2,2,32,128]{3,2,1,0:T(8,128)S(1)}, f32[2,2,32,128]{3,2,1,0:T(8,128)S(1)}, u32[]{:S(2)}, u32[]{:S(2)}) collective-permute-start(f32[2,2,32,128]{3,2,1,0:T(8,128)S(1)} %pad_maximum_fusion.8), channel_id=1, source_target_pairs={{0,1},{1,2},{2,3},{4,5},{5,6},{6,7},{8,9},{9,10},{10,11},{12,13},{... | collective-permute-start | bytes 196616 | tf_op jit(solution)/shard_map/ppermute | solution.py:15
  65.5 1.2 multiply_add_fusion.16
  67.1 2.0 %collective-permute-start.3 = (f32[1,2,32,128]{3,2,1,0:T(8,128)S(1)}, f32[1,2,32,128]{3,2,1,0:T(8,128)S(1)}, u32[]{:S(2)}, u32[]{:S(2)}) collective-permute-start(f32[1,2,32,128]{3,2,1,0:T(8,128)S(1)} %slice_bitcast_fusion.72), channel_id=1, source_target_pairs={{1,0},{2,1},{3,2},{5,4},{6,5},{7,6},{9,8},{10,9},{11,10},{13,12},{... | collective-permute-start | bytes 98312 | tf_op jit(solution)/shard_map/ppermute | solution.py:15
  69.2 4.6 %collective-permute-done.3 = f32[1,2,32,128]{3,2,1,0:T(8,128)S(1)} collective-permute-done((f32[1,2,32,128]{3,2,1,0:T(8,128)S(1)}, f32[1,2,32,128]{3,2,1,0:T(8,128)S(1)}, u32[]{:S(2)}, u32[]{:S(2)}) %collective-permute-start.3) | collective-permute-done | bytes 32800 | tf_op jit(solution)/shard_map/ppermute | solution.py:15
  74.8 1.9 %collective-permute-start.5 = (f32[1,2,32,128]{3,2,1,0:T(8,128)S(1)}, f32[1,2,32,128]{3,2,1,0:T(8,128)S(1)}, u32[]{:S(2)}, u32[]{:S(2)}) collective-permute-start(f32[1,2,32,128]{3,2,1,0:T(8,128)S(1)} %slice_bitcast_fusion.67), channel_id=1, source_target_pairs={{0,1},{1,2},{2,3},{4,5},{5,6},{6,7},{8,9},{9,10},{10,11},{12,13},{... | collective-permute-start | bytes 98312 | tf_op jit(solution)/shard_map/ppermute | solution.py:15
  76.7 2.4 %collective-permute-start.8 = (f32[2,2,32,128]{3,2,1,0:T(8,128)S(1)}, f32[2,2,32,128]{3,2,1,0:T(8,128)S(1)}, u32[]{:S(2)}, u32[]{:S(2)}) collective-permute-start(f32[2,2,32,128]{3,2,1,0:T(8,128)S(1)} %pad_maximum_fusion.9), channel_id=1, source_target_pairs={{1,0},{2,1},{3,2},{5,4},{6,5},{7,6},{9,8},{10,9},{11,10},{13,12},{... | collective-permute-start | bytes 196616 | tf_op jit(solution)/shard_map/ppermute | solution.py:15
  79.2 1.2 fusion.63
  82.0 1.9 %collective-permute-start.7 = (f32[1,2,32,128]{3,2,1,0:T(8,128)S(1)}, f32[1,2,32,128]{3,2,1,0:T(8,128)S(1)}, u32[]{:S(2)}, u32[]{:S(2)}) collective-permute-start(f32[1,2,32,128]{3,2,1,0:T(8,128)S(1)} %slice_bitcast_fusion.62), channel_id=1, source_target_pairs={{1,0},{2,1},{3,2},{5,4},{6,5},{7,6},{9,8},{10,9},{11,10},{13,12},{... | collective-permute-start | bytes 98312 | tf_op jit(solution)/shard_map/ppermute | solution.py:15
  84.5 5.1 %collective-permute-start.10 = (f32[2,2,32,128]{3,2,1,0:T(8,128)S(1)}, f32[2,2,32,128]{3,2,1,0:T(8,128)S(1)}, u32[]{:S(2)}, u32[]{:S(2)}) collective-permute-start(f32[2,2,32,128]{3,2,1,0:T(8,128)S(1)} %pad_maximum_fusion.10), channel_id=1, source_target_pairs={{0,1},{1,2},{2,3},{4,5},{5,6},{6,7},{8,9},{9,10},{10,11},{12,13},{... | collective-permute-start | bytes 196616 | tf_op jit(solution)/shard_map/ppermute | solution.py:15
  89.8 1.2 collective-permute-done.10
  91.8 1.9 %collective-permute-start.12 = (f32[2,2,32,128]{3,2,1,0:T(8,128)S(1)}, f32[2,2,32,128]{3,2,1,0:T(8,128)S(1)}, u32[]{:S(2)}, u32[]{:S(2)}) collective-permute-start(f32[2,2,32,128]{3,2,1,0:T(8,128)S(1)} %pad_maximum_fusion.11), channel_id=1, source_target_pairs={{1,0},{2,1},{3,2},{5,4},{6,5},{7,6},{9,8},{10,9},{11,10},{13,12},{... | collective-permute-start | bytes 196616 | tf_op jit(solution)/shard_map/ppermute | solution.py:15
  94.3 5.8 %collective-permute-start.9 = (f32[1,2,32,128]{3,2,1,0:T(8,128)S(1)}, f32[1,2,32,128]{3,2,1,0:T(8,128)S(1)}, u32[]{:S(2)}, u32[]{:S(2)}) collective-permute-start(f32[1,2,32,128]{3,2,1,0:T(8,128)S(1)} %slice_bitcast_fusion.57), channel_id=1, source_target_pairs={{0,1},{1,2},{2,3},{4,5},{5,6},{6,7},{8,9},{9,10},{10,11},{12,13},{... | collective-permute-start | bytes 98312 | tf_op jit(solution)/shard_map/ppermute | solution.py:15
  100.1 1.0 collective-permute-done.9
  101.6 0.8 copy_add_fusion.5
  102.4 5.7 %collective-permute-start.13 = (f32[2,2,32,128]{3,2,1,0:T(8,128)S(1)}, f32[2,2,32,128]{3,2,1,0:T(8,128)S(1)}, u32[]{:S(2)}, u32[]{:S(2)}) collective-permute-start(f32[2,2,32,128]{3,2,1,0:T(8,128)S(1)} %pad_maximum_fusion.12), channel_id=1, source_target_pairs={{0,1},{1,2},{2,3},{4,5},{5,6},{6,7},{8,9},{9,10},{10,11},{12,13},{... | collective-permute-start | bytes 196616 | tf_op jit(solution)/shard_map/ppermute | solution.py:15
  108.7 2.1 %collective-permute-start.11 = (f32[1,2,32,128]{3,2,1,0:T(8,128)S(1)}, f32[1,2,32,128]{3,2,1,0:T(8,128)S(1)}, u32[]{:S(2)}, u32[]{:S(2)}) collective-permute-start(f32[1,2,32,128]{3,2,1,0:T(8,128)S(1)} %slice_bitcast_fusion.52), channel_id=1, source_target_pairs={{1,0},{2,1},{3,2},{5,4},{6,5},{7,6},{9,8},{10,9},{11,10},{13,12},{... | collective-permute-start | bytes 98312 | tf_op jit(solution)/shard_map/ppermute | solution.py:15
  111.2 4.2 %collective-permute-done.11 = f32[1,2,32,128]{3,2,1,0:T(8,128)S(1)} collective-permute-done((f32[1,2,32,128]{3,2,1,0:T(8,128)S(1)}, f32[1,2,32,128]{3,2,1,0:T(8,128)S(1)}, u32[]{:S(2)}, u32[]{:S(2)}) %collective-permute-start.11) | collective-permute-done | bytes 32800 | tf_op jit(solution)/shard_map/ppermute | solution.py:15
  116.2 1.9 %collective-permute-start.15 = (f32[2,2,32,128]{3,2,1,0:T(8,128)S(1)}, f32[2,2,32,128]{3,2,1,0:T(8,128)S(1)}, u32[]{:S(2)}, u32[]{:S(2)}) collective-permute-start(f32[2,2,32,128]{3,2,1,0:T(8,128)S(1)} %pad_maximum_fusion.13), channel_id=1, source_target_pairs={{1,0},{2,1},{3,2},{5,4},{6,5},{7,6},{9,8},{10,9},{11,10},{13,12},{... | collective-permute-start | bytes 196616 | tf_op jit(solution)/shard_map/ppermute | solution.py:15
  118.2 0.7 copy_dynamic-update-slice_fusion.10
  119.1 0.7 copy_dynamic-update-slice_fusion.9
  120.5 1.0 fusion.57
  121.9 5.1 %collective-permute-start.14 = (f32[1,2,32,128]{3,2,1,0:T(8,128)S(1)}, f32[1,2,32,128]{3,2,1,0:T(8,128)S(1)}, u32[]{:S(2)}, u32[]{:S(2)}) collective-permute-start(f32[1,2,32,128]{3,2,1,0:T(8,128)S(1)} %slice_bitcast_fusion.45), channel_id=1, source_target_pairs={{0,1},{1,2},{2,3},{4,5},{5,6},{6,7},{8,9},{9,10},{10,11},{12,13},{... | collective-permute-start | bytes 98312 | tf_op jit(solution)/shard_map/ppermute | solution.py:15
  127.1 1.0 collective-permute-done.14
  128.9 0.9 multiply_add_fusion.1
  131.1 1.2 copy_add_fusion
  132.3 0.7 copy_dynamic-update-slice_fusion.5
  133.1 0.8 copy_dynamic-update-slice_fusion.4
  133.8 0.7 copy_dynamic-update-slice_fusion.3
  134.6 0.8 copy_dynamic-update-slice_fusion.2
  135.3 0.8 copy_dynamic-update-slice_fusion.1
  136.1 0.8 copy_dynamic-update-slice_fusion
  136.9 1.1 multiply_add_fusion
  138.0 0.8 fusion.51
  138.7 0.8 fusion.46
  139.5 0.8 fusion.41
  140.3 7.3 %all-to-all-start.2 = ((f32[32,10,8,1,128]{4,2,1,3,0:T(8,128)}), f32[32,10,8,1,128]{4,2,1,3,0:T(8,128)S(1)}, u32[]{:S(2)}, u32[]{:S(2)}) async-start(f32[32,10,8,1,128]{4,2,1,3,0:T(8,128)} %bitcast.119), calls=%async_computation.2 | async-start | bytes 2621440 | tf_op jit(solution)/shard_map/all_to_all | solution.py:26
  147.6 1.0 slice_bitcast_fusion.5
  148.7 0.7 copy_dynamic-update-slice_fusion.8
  153.4 2.5 %copy.145 = f32[1,9,8,32,128]{4,3,2,1,0:T(8,128)} copy(f32[1,9,8,32,128]{4,2,3,1,0:T(8,128)} %get-tuple-element.117) | data formatting | bytes 2359296
  155.9 1.2 copy.144
  157.1 7.7 %all-to-all-done.2 = f32[32,10,8,1,128]{4,2,1,3,0:T(8,128)S(1)} async-done(((f32[32,10,8,1,128]{4,2,1,3,0:T(8,128)}), f32[32,10,8,1,128]{4,2,1,3,0:T(8,128)S(1)}, u32[]{:S(2)}, u32[]{:S(2)}) %all-to-all-start.2) | async-done | bytes 1310752 | tf_op jit(solution)/shard_map/all_to_all | solution.py:26
  (255 shorter events, 24.8 us)
Async XLA Ops:
  2.0 31.8 %all-to-all-start = ((f32[32,1,8,1,128]{4,2,3,1,0:T(8,128)}), f32[32,1,8,1,128]{4,2,3,1,0:T(8,128)S(1)}, u32[]{:S(2)}, u32[]{:S(2)}) async-start(f32[32,1,8,1,128]{4,2,3,1,0:T(8,128)} %broadcast_in_dim.8), calls=%async_computation | async-start | bytes 262144 | tf_op jit(solution)/shard_map/all_to_all | solution.py:32
  11.8 2.2 %copy-start.2 = (f32[1,9,8,32,128]{4,3,2,1,0:T(8,128)S(1)}, f32[1,9,8,32,128]{4,3,2,1,0:T(8,128)}, u32[]{:S(2)}) copy-start(f32[1,9,8,32,128]{4,3,2,1,0:T(8,128)} %param.9) | copy-start | bytes 3538948
  14.9 30.0 %copy-start.3 = (f32[1,8,32,128]{3,2,0,1:T(8,128)}, f32[1,8,32,128]{3,2,0,1:T(8,128)S(1)}, u32[]{:S(2)}) copy-start(f32[1,8,32,128]{3,2,0,1:T(8,128)S(1)} %get-tuple-element.91) | copy-start | bytes 393220
  15.5 32.3 %collective-permute-start = (f32[1,2,32,128]{3,2,1,0:T(8,128)}, f32[1,2,32,128]{3,2,1,0:T(8,128)}, u32[]{:S(2)}, u32[]{:S(2)}) collective-permute-start(f32[1,2,32,128]{3,2,1,0:T(8,128)} %fusion.85), channel_id=1, source_target_pairs={{1,0},{2,1},{3,2},{5,4},{6,5},{7,6},{9,8},{10,9},{11,10},{13,12},{... | collective-permute-start | bytes 98312 | tf_op jit(solution)/shard_map/ppermute | solution.py:15
  18.4 6.6 %copy-start.41 = (s32[1,16]{1,0:T(1,128)S(1)}, s32[1,16]{1,0:T(1,128)}, u32[]{:S(2)}) copy-start(s32[1,16]{1,0:T(1,128)} %param.12) | copy-start | bytes 196
  18.4 6.6 %copy-start.39 = (f32[4]{0:T(128)S(1)}, f32[4]{0:T(128)}, u32[]{:S(2)}) copy-start(f32[4]{0:T(128)} %param.11) | copy-start | bytes 52
  18.4 7.3 %copy-start.38 = (f32[1,4,8,32]{3,2,1,0:T(8,128)S(1)}, f32[1,4,8,32]{3,2,1,0:T(8,128)}, u32[]{:S(2)}) copy-start(f32[1,4,8,32]{3,2,1,0:T(8,128)} %param.15) | copy-start | bytes 12292
  18.4 7.3 %copy-start.42 = (s32[1,16]{1,0:T(1,128)S(1)}, s32[1,16]{1,0:T(1,128)}, u32[]{:S(2)}) copy-start(s32[1,16]{1,0:T(1,128)} %param.13) | copy-start | bytes 196
  18.5 14.7 %collective-permute-start.2 = (f32[2,2,32,128]{3,2,1,0:T(8,128)S(1)}, f32[2,2,32,128]{3,2,1,0:T(8,128)S(1)}, u32[]{:S(2)}, u32[]{:S(2)}) collective-permute-start(f32[2,2,32,128]{3,2,1,0:T(8,128)S(1)} %pad_maximum_fusion.6), channel_id=1, source_target_pairs={{0,1},{1,2},{2,3},{4,5},{5,6},{6,7},{8,9},{9,10},{10,11},{12,13},{... | collective-permute-start | bytes 196616 | tf_op jit(solution)/shard_map/ppermute | solution.py:15
  26.5 4.9 %copy-start.40 = (s32[8,32]{1,0:T(8,128)S(1)}, s32[8,32]{1,0:T(8,128)}, u32[]{:S(2)}) copy-start(s32[8,32]{1,0:T(8,128)} %param.14) | copy-start | bytes 3076
  27.4 6.4 %slice-start.1 = ((f32[10,8,1,128]{3,2,1,0:T(1,128)}), f32[9,8,1,128]{3,2,1,0:T(1,128)S(1)}, s32[]{:S(2)}) async-start(f32[10,8,1,128]{3,2,1,0:T(1,128)} %param.10), calls=%async_computation.4 | async-start | bytes 73728 | tf_op jit(solution)/shard_map/slice | solution.py:205
  34.9 26.4 %all-to-all-start.1 = ((f32[32,9,8,1,128]{4,2,3,1,0:T(8,128)}), f32[32,9,8,1,128]{4,2,3,1,0:T(8,128)S(1)}, u32[]{:S(2)}, u32[]{:S(2)}) async-start(f32[32,9,8,1,128]{4,2,3,1,0:T(8,128)} %broadcast_in_dim.9), calls=%async_computation.1 | async-start | bytes 2359296 | tf_op jit(solution)/shard_map/all_to_all | solution.py:32
  42.6 2.2 %copy-start.12 = (f32[2,8,31,128]{3,2,0,1:T(8,128)S(1)}, f32[2,8,31,128]{3,2,0,1:T(8,128)}, u32[]{:S(2)}) copy-start(f32[2,8,31,128]{3,2,0,1:T(8,128)} %get-tuple-element.187) | copy-start | bytes 761860
  42.6 2.2 %copy-start.13 = (f32[2,8,32,127]{3,2,0,1:T(8,128)S(1)}, f32[2,8,32,127]{3,2,0,1:T(8,128)}, u32[]{:S(2)}) copy-start(f32[2,8,32,127]{3,2,0,1:T(8,128)} %get-tuple-element.184) | copy-start | bytes 780292
  42.7 2.2 %copy-start.18 = (f32[2,7,32,128]{3,2,0,1:T(8,128)S(1)}, f32[2,7,32,128]{3,2,0,1:T(8,128)}, u32[]{:S(2)}) copy-start(f32[2,7,32,128]{3,2,0,1:T(8,128)} %get-tuple-element.189) | copy-start | bytes 688132
  42.7 2.2 %copy-start.27 = (f32[1,8,32,128]{3,2,0,1:T(8,128)S(1)}, f32[1,8,32,128]{3,2,0,1:T(8,128)}, u32[]{:S(2)}) copy-start(f32[1,8,32,128]{3,2,0,1:T(8,128)} %get-tuple-element.92) | copy-start | bytes 393220
  42.7 2.2 %copy-start.35 = (f32[2,1,32,128]{3,2,0,1:T(8,128)S(1)}, f32[2,1,32,128]{3,2,0,1:T(8,128)}, u32[]{:S(2)}) copy-start(f32[2,1,32,128]{3,2,0,1:T(8,128)} %get-tuple-element.171) | copy-start | bytes 98308
  44.9 2.9 %copy-start.7 = (f32[2,8,32,127]{3,2,0,1:T(8,128)S(1)}, f32[2,8,32,127]{3,2,0,1:T(8,128)}, u32[]{:S(2)}) copy-start(f32[2,8,32,127]{3,2,0,1:T(8,128)} %fusion.4) | copy-start | bytes 780292
  44.9 2.9 %copy-start.8 = (f32[2,8,31,128]{3,2,0,1:T(8,128)S(1)}, f32[2,8,31,128]{3,2,0,1:T(8,128)}, u32[]{:S(2)}) copy-start(f32[2,8,31,128]{3,2,0,1:T(8,128)} %fusion.5) | copy-start | bytes 761860
  44.9 2.9 %copy-start.17 = (f32[2,7,32,128]{3,2,0,1:T(8,128)S(1)}, f32[2,7,32,128]{3,2,0,1:T(8,128)}, u32[]{:S(2)}) copy-start(f32[2,7,32,128]{3,2,0,1:T(8,128)} %get-tuple-element.188) | copy-start | bytes 688132
  44.9 2.9 %copy-start.25 = (f32[1,8,32,128]{3,2,0,1:T(8,128)S(1)}, f32[1,8,32,128]{3,2,0,1:T(8,128)}, u32[]{:S(2)}) copy-start(f32[1,8,32,128]{3,2,0,1:T(8,128)} %get-tuple-element.81) | copy-start | bytes 393220
  44.9 2.9 %copy-start.26 = (f32[1,8,32,128]{3,2,0,1:T(8,128)S(1)}, f32[1,8,32,128]{3,2,0,1:T(8,128)}, u32[]{:S(2)}) copy-start(f32[1,8,32,128]{3,2,0,1:T(8,128)} %get-tuple-element.90) | copy-start | bytes 393220
  45.9 14.8 %collective-permute-start.4 = (f32[2,2,32,128]{3,2,1,0:T(8,128)S(1)}, f32[2,2,32,128]{3,2,1,0:T(8,128)S(1)}, u32[]{:S(2)}, u32[]{:S(2)}) collective-permute-start(f32[2,2,32,128]{3,2,1,0:T(8,128)S(1)} %pad_maximum_fusion.7), channel_id=1, source_target_pairs={{1,0},{2,1},{3,2},{5,4},{6,5},{7,6},{9,8},{10,9},{11,10},{13,12},{... | collective-permute-start | bytes 196616 | tf_op jit(solution)/shard_map/ppermute | solution.py:15
  55.5 9.9 %collective-permute-start.1 = (f32[1,2,32,128]{3,2,1,0:T(8,128)}, f32[1,2,32,128]{3,2,1,0:T(8,128)}, u32[]{:S(2)}, u32[]{:S(2)}) collective-permute-start(f32[1,2,32,128]{3,2,1,0:T(8,128)} %slice_bitcast_fusion.75), channel_id=1, source_target_pairs={{0,1},{1,2},{2,3},{4,5},{5,6},{6,7},{8,9},{9,10},{10,11},{12,13},{... | collective-permute-start | bytes 98312 | tf_op jit(solution)/shard_map/ppermute | solution.py:15
  61.3 1.0 copy-start.5
  61.3 1.0 copy-start.6
  61.3 1.1 copy-start.15
  61.3 1.2 copy-start.16
  61.3 1.1 copy-start.36
  61.3 1.1 copy-start.37
  62.8 2.7 %copy-start.9 = (f32[2,8,32,127]{3,2,0,1:T(8,128)S(1)}, f32[2,8,32,127]{3,2,0,1:T(8,128)}, u32[]{:S(2)}) copy-start(f32[2,8,32,127]{3,2,0,1:T(8,128)} %slice.1055) | copy-start | bytes 780292
  62.8 2.7 %copy-start.10 = (f32[2,8,31,128]{3,2,0,1:T(8,128)S(1)}, f32[2,8,31,128]{3,2,0,1:T(8,128)}, u32[]{:S(2)}) copy-start(f32[2,8,31,128]{3,2,0,1:T(8,128)} %slice.1056) | copy-start | bytes 761860
  62.8 2.7 %copy-start.19 = (f32[2,7,32,128]{3,2,0,1:T(8,128)S(1)}, f32[2,7,32,128]{3,2,0,1:T(8,128)}, u32[]{:S(2)}) copy-start(f32[2,7,32,128]{3,2,0,1:T(8,128)} %slice.1008) | copy-start | bytes 688132
  63.1 6.1 %collective-permute-start.6 = (f32[2,2,32,128]{3,2,1,0:T(8,128)S(1)}, f32[2,2,32,128]{3,2,1,0:T(8,128)S(1)}, u32[]{:S(2)}, u32[]{:S(2)}) collective-permute-start(f32[2,2,32,128]{3,2,1,0:T(8,128)S(1)} %pad_maximum_fusion.8), channel_id=1, source_target_pairs={{0,1},{1,2},{2,3},{4,5},{5,6},{6,7},{8,9},{9,10},{10,11},{12,13},{... | collective-permute-start | bytes 196616 | tf_op jit(solution)/shard_map/ppermute | solution.py:15
  65.5 1.2 copy-start.4
  65.5 1.2 copy-start.32
  65.5 1.2 copy-start.34
  67.1 6.7 %collective-permute-start.3 = (f32[1,2,32,128]{3,2,1,0:T(8,128)S(1)}, f32[1,2,32,128]{3,2,1,0:T(8,128)S(1)}, u32[]{:S(2)}, u32[]{:S(2)}) collective-permute-start(f32[1,2,32,128]{3,2,1,0:T(8,128)S(1)} %slice_bitcast_fusion.72), channel_id=1, source_target_pairs={{1,0},{2,1},{3,2},{5,4},{6,5},{7,6},{9,8},{10,9},{11,10},{13,12},{... | collective-permute-start | bytes 98312 | tf_op jit(solution)/shard_map/ppermute | solution.py:15
  74.4 4.8 %copy-start.20 = (f32[2,8,32,128]{3,2,0,1:T(8,128)S(1)}, f32[2,8,32,128]{3,2,0,1:T(8,128)}, u32[]{:S(2)}) copy-start(f32[2,8,32,128]{3,2,0,1:T(8,128)} %get-tuple-element.61) | copy-start | bytes 786436
  74.4 4.8 %copy-start.21 = (f32[2,8,32,128]{3,2,0,1:T(8,128)S(1)}, f32[2,8,32,128]{3,2,0,1:T(8,128)}, u32[]{:S(2)}) copy-start(f32[2,8,32,128]{3,2,0,1:T(8,128)} %get-tuple-element.63) | copy-start | bytes 786436
  74.4 4.8 %copy-start.22 = (f32[2,8,32,128]{3,2,0,1:T(8,128)S(1)}, f32[2,8,32,128]{3,2,0,1:T(8,128)}, u32[]{:S(2)}) copy-start(f32[2,8,32,128]{3,2,0,1:T(8,128)} %get-tuple-element.65) | copy-start | bytes 786436
  74.8 6.0 %collective-permute-start.5 = (f32[1,2,32,128]{3,2,1,0:T(8,128)S(1)}, f32[1,2,32,128]{3,2,1,0:T(8,128)S(1)}, u32[]{:S(2)}, u32[]{:S(2)}) collective-permute-start(f32[1,2,32,128]{3,2,1,0:T(8,128)S(1)} %slice_bitcast_fusion.67), channel_id=1, source_target_pairs={{0,1},{1,2},{2,3},{4,5},{5,6},{6,7},{8,9},{9,10},{10,11},{12,13},{... | collective-permute-start | bytes 98312 | tf_op jit(solution)/shard_map/ppermute | solution.py:15
  76.7 7.4 %collective-permute-start.8 = (f32[2,2,32,128]{3,2,1,0:T(8,128)S(1)}, f32[2,2,32,128]{3,2,1,0:T(8,128)S(1)}, u32[]{:S(2)}, u32[]{:S(2)}) collective-permute-start(f32[2,2,32,128]{3,2,1,0:T(8,128)S(1)} %pad_maximum_fusion.9), channel_id=1, source_target_pairs={{1,0},{2,1},{3,2},{5,4},{6,5},{7,6},{9,8},{10,9},{11,10},{13,12},{... | collective-permute-start | bytes 196616 | tf_op jit(solution)/shard_map/ppermute | solution.py:15
  80.7 0.9 copy-start.31
  80.7 1.0 copy-start.33
  82.0 9.5 %collective-permute-start.7 = (f32[1,2,32,128]{3,2,1,0:T(8,128)S(1)}, f32[1,2,32,128]{3,2,1,0:T(8,128)S(1)}, u32[]{:S(2)}, u32[]{:S(2)}) collective-permute-start(f32[1,2,32,128]{3,2,1,0:T(8,128)S(1)} %slice_bitcast_fusion.62), channel_id=1, source_target_pairs={{1,0},{2,1},{3,2},{5,4},{6,5},{7,6},{9,8},{10,9},{11,10},{13,12},{... | collective-permute-start | bytes 98312 | tf_op jit(solution)/shard_map/ppermute | solution.py:15
  84.5 6.5 %collective-permute-start.10 = (f32[2,2,32,128]{3,2,1,0:T(8,128)S(1)}, f32[2,2,32,128]{3,2,1,0:T(8,128)S(1)}, u32[]{:S(2)}, u32[]{:S(2)}) collective-permute-start(f32[2,2,32,128]{3,2,1,0:T(8,128)S(1)} %pad_maximum_fusion.10), channel_id=1, source_target_pairs={{0,1},{1,2},{2,3},{4,5},{5,6},{6,7},{8,9},{9,10},{10,11},{12,13},{... | collective-permute-start | bytes 196616 | tf_op jit(solution)/shard_map/ppermute | solution.py:15
  91.8 8.3 %collective-permute-start.12 = (f32[2,2,32,128]{3,2,1,0:T(8,128)S(1)}, f32[2,2,32,128]{3,2,1,0:T(8,128)S(1)}, u32[]{:S(2)}, u32[]{:S(2)}) collective-permute-start(f32[2,2,32,128]{3,2,1,0:T(8,128)S(1)} %pad_maximum_fusion.11), channel_id=1, source_target_pairs={{1,0},{2,1},{3,2},{5,4},{6,5},{7,6},{9,8},{10,9},{11,10},{13,12},{... | collective-permute-start | bytes 196616 | tf_op jit(solution)/shard_map/ppermute | solution.py:15
  94.0 7.0 %copy-start.24 = (f32[32768]{0:T(1024)S(1)}, f32[32768]{0:T(1024)}, u32[]{:S(2)}) copy-start(f32[32768]{0:T(1024)} %get-tuple-element.152) | copy-start | bytes 393220
  94.0 7.0 %copy-start.29 = (f32[1,8,32,128]{3,2,0,1:T(8,128)S(1)}, f32[1,8,32,128]{3,2,0,1:T(8,128)}, u32[]{:S(2)}) copy-start(f32[1,8,32,128]{3,2,0,1:T(8,128)} %get-tuple-element.177) | copy-start | bytes 393220
  94.3 6.8 %collective-permute-start.9 = (f32[1,2,32,128]{3,2,1,0:T(8,128)S(1)}, f32[1,2,32,128]{3,2,1,0:T(8,128)S(1)}, u32[]{:S(2)}, u32[]{:S(2)}) collective-permute-start(f32[1,2,32,128]{3,2,1,0:T(8,128)S(1)} %slice_bitcast_fusion.57), channel_id=1, source_target_pairs={{0,1},{1,2},{2,3},{4,5},{5,6},{6,7},{8,9},{9,10},{10,11},{12,13},{... | collective-permute-start | bytes 98312 | tf_op jit(solution)/shard_map/ppermute | solution.py:15
  102.4 8.5 %collective-permute-start.13 = (f32[2,2,32,128]{3,2,1,0:T(8,128)S(1)}, f32[2,2,32,128]{3,2,1,0:T(8,128)S(1)}, u32[]{:S(2)}, u32[]{:S(2)}) collective-permute-start(f32[2,2,32,128]{3,2,1,0:T(8,128)S(1)} %pad_maximum_fusion.12), channel_id=1, source_target_pairs={{0,1},{1,2},{2,3},{4,5},{5,6},{6,7},{8,9},{9,10},{10,11},{12,13},{... | collective-permute-start | bytes 196616 | tf_op jit(solution)/shard_map/ppermute | solution.py:15
  108.7 6.7 %collective-permute-start.11 = (f32[1,2,32,128]{3,2,1,0:T(8,128)S(1)}, f32[1,2,32,128]{3,2,1,0:T(8,128)S(1)}, u32[]{:S(2)}, u32[]{:S(2)}) collective-permute-start(f32[1,2,32,128]{3,2,1,0:T(8,128)S(1)} %slice_bitcast_fusion.52), channel_id=1, source_target_pairs={{1,0},{2,1},{3,2},{5,4},{6,5},{7,6},{9,8},{10,9},{11,10},{13,12},{... | collective-permute-start | bytes 98312 | tf_op jit(solution)/shard_map/ppermute | solution.py:15
  116.1 12.0 %copy-start = (f32[2,8,32,128]{3,1,2,0:T(8,128)}, f32[2,8,32,128]{3,1,2,0:T(8,128)S(1)}, u32[]{:S(2)}) copy-start(f32[2,8,32,128]{3,1,2,0:T(8,128)S(1)} %copy_add_fusion.4) | copy-start | bytes 786436
  116.2 10.9 %collective-permute-start.15 = (f32[2,2,32,128]{3,2,1,0:T(8,128)S(1)}, f32[2,2,32,128]{3,2,1,0:T(8,128)S(1)}, u32[]{:S(2)}, u32[]{:S(2)}) collective-permute-start(f32[2,2,32,128]{3,2,1,0:T(8,128)S(1)} %pad_maximum_fusion.13), channel_id=1, source_target_pairs={{1,0},{2,1},{3,2},{5,4},{6,5},{7,6},{9,8},{10,9},{11,10},{13,12},{... | collective-permute-start | bytes 196616 | tf_op jit(solution)/shard_map/ppermute | solution.py:15
  121.6 6.5 %copy-start.23 = (f32[32768]{0:T(1024)S(1)}, f32[32768]{0:T(1024)}, u32[]{:S(2)}) copy-start(f32[32768]{0:T(1024)} %get-tuple-element.151) | copy-start | bytes 393220
  121.6 6.5 %copy-start.28 = (f32[1,8,32,128]{3,2,0,1:T(8,128)S(1)}, f32[1,8,32,128]{3,2,0,1:T(8,128)}, u32[]{:S(2)}) copy-start(f32[1,8,32,128]{3,2,0,1:T(8,128)} %get-tuple-element.176) | copy-start | bytes 393220
  121.9 6.2 %collective-permute-start.14 = (f32[1,2,32,128]{3,2,1,0:T(8,128)S(1)}, f32[1,2,32,128]{3,2,1,0:T(8,128)S(1)}, u32[]{:S(2)}, u32[]{:S(2)}) collective-permute-start(f32[1,2,32,128]{3,2,1,0:T(8,128)S(1)} %slice_bitcast_fusion.45), channel_id=1, source_target_pairs={{0,1},{1,2},{2,3},{4,5},{5,6},{6,7},{8,9},{9,10},{10,11},{12,13},{... | collective-permute-start | bytes 98312 | tf_op jit(solution)/shard_map/ppermute | solution.py:15
  131.1 5.7 %copy-start.1 = (f32[2,8,32,128]{3,1,2,0:T(8,128)S(1)}, f32[2,8,32,128]{3,1,2,0:T(8,128)}, u32[]{:S(2)}) copy-start(f32[2,8,32,128]{3,1,2,0:T(8,128)} %copy-done) | copy-start | bytes 786436
  131.1 5.7 %slice-start = ((f32[2,8,32,128]{3,1,2,0:T(8,128)}), f32[2,8,31,128]{3,1,2,0:T(8,128)S(1)}, s32[]{:S(2)}) async-start(f32[2,8,32,128]{3,1,2,0:T(8,128)} %copy-done), calls=%async_computation.3 | async-start | bytes 507904 | tf_op jit(solution)/shard_map/slice | solution.py:48
  140.3 24.6 %all-to-all-start.2 = ((f32[32,10,8,1,128]{4,2,1,3,0:T(8,128)}), f32[32,10,8,1,128]{4,2,1,3,0:T(8,128)S(1)}, u32[]{:S(2)}, u32[]{:S(2)}) async-start(f32[32,10,8,1,128]{4,2,1,3,0:T(8,128)} %bitcast.119), calls=%async_computation.2 | async-start | bytes 2621440 | tf_op jit(solution)/shard_map/all_to_all | solution.py:26
  147.6 1.8 %copy-start.30 = (f32[1,1,8,32,128]{4,3,2,1,0:T(8,128)S(1)}, f32[1,1,8,32,128]{4,3,2,1,0:T(8,128)}, u32[]{:S(2)}) copy-start(f32[1,1,8,32,128]{4,3,2,1,0:T(8,128)} %get-tuple-element.125) | copy-start | bytes 393220
  147.6 3.5 %copy-start.11 = (f32[2,8,32,128]{3,1,2,0:T(8,128)S(1)}, f32[2,8,32,128]{3,1,2,0:T(8,128)}, u32[]{:S(2)}) copy-start(f32[2,8,32,128]{3,1,2,0:T(8,128)} %get-tuple-element.8) | copy-start | bytes 786436
  151.2 1.6 copy-start.14
where the time goes:
time: 167 us; the launch traced here: 166 us
  starting transfers between devices  77.3 us (46%)
  local copies, waits for them, and re-layouts  34.2 us (20%)
  other arithmetic  32.1 us (19%)
  waiting for transfers between devices  19.7 us (12%)
  between operations  2.26 us (1%)
    ppermute x16, starting transfers between devices, passed_along(): return lax.ppermute(value, axis, pairs)  52.5 us
    all_to_all x2, starting transfers between devices, copy_for_each(): return lax.all_to_all(copies, axis, split_axis=0, concat_axis=0, tiled=True)  17.5 us
    unnamed x108, local copies, waits for them, and re-layouts  16.1 us
    ppermute x16, waiting for transfers between devices, passed_along(): return lax.ppermute(value, axis, pairs)  12 us
    all_to_all x1, waiting for transfers between devices, summed_on_arrival(): tiles = lax.all_to_all(in_blocks(value, dim, peers), axis, 0, 0, tiled=True)  7.74 us
    all_to_all x1, starting transfers between devices, summed_on_arrival(): tiles = lax.all_to_all(in_blocks(value, dim, peers), axis, 0, 0, tiled=True)  7.3 us
    add x9, other arithmetic, run_tile(): velocity[comp] + step_size * buoyancy * forces[comp]  6.5 us
    concatenate x6, other arithmetic, body(): jnp.concatenate([forward_state[:, comp], adjoint_state[:, comp]], axis=0)  4.64 us
  transfers between devices with their start and end apart: 19, of which 6 were waited for; matrix products, arithmetic and copies ran while one was open for 28% of the time, Pallas kernels for 0%

commit v1 on v0

v1 whole, which is shorter than its diff:
```python
import functools

import jax
import jax.numpy as jnp
from jax import lax
from jax.experimental import pallas as pl
from jax.experimental.pallas import tpu as pltpu
from jax.sharding import PartitionSpec as P

STEPS = 4
DEPTH = 2
OWN = 8
VX, VY, VZ, SXX, SYY, SZZ, SYZ, SXZ, SXY = range(9)
step_size = 0.25
VMEM = pltpu.VMEM
SMEM = pltpu.SMEM


def phase_kernel(depth, y_rows, z_rows, steps, first, last, *refs):
    refs = list(refs)
    wavelet, state_in = refs.pop(0), refs.pop(0)
    if first:
        own_rows, rim_rows = refs.pop(0), refs.pop(0)
    else:
        halo_lo, halo_hi, mats, acc_in = (refs.pop(0) for slot in range(4))
    image, data = refs.pop(0), refs.pop(0)
    state, acc = refs.pop(0), refs.pop(0)
    if first:
        mats = refs.pop(0)
    if last:
        packed = refs.pop(0)
    else:
        send_dn, send_up = refs.pop(0), refs.pop(0)

    length = OWN + 2 * depth
    chunks = y_rows // 8
    row = lax.broadcasted_iota(jnp.int32, (8, z_rows), 0)
    lane = lax.broadcasted_iota(jnp.int32, (8, z_rows), 1)
    row_first, row_last = row == 0, row == 7
    lane_first, lane_last = lane == 0, lane == z_rows - 1
    nought = jnp.zeros((8, z_rows), jnp.float32)

    def rows_of(c):
        return pl.ds(8 * c, 8)

    if first:
        own_count, rim_count = 10 * OWN, rim_rows.shape[0] // y_rows
        side = depth + 9 * (depth - 1)

        def take(source, count, r, c):
            return step_size * source[pl.ds(r + 8 * c * count, 8, stride=count), :]

        for c in range(chunks):
            for r in range(own_count):
                mats[r // OWN, depth + r % OWN, rows_of(c), :] = take(own_rows, own_count, r, c)
            for base, buoy_at, stiff_at in ((0, 0, 1), (side, depth + OWN, depth + OWN)):
                for j in range(depth):
                    mats[0, buoy_at + j, rows_of(c), :] = take(rim_rows, rim_count, base + j, c)
                for m in range(9):
                    for j in range(depth - 1):
                        r = base + depth + m * (depth - 1) + j
                        mats[1 + m, stiff_at + j, rows_of(c), :] = take(rim_rows, rim_count, r, c)
    else:
        for f in range(18):
            for j in range(depth):
                state[f, j] = halo_lo[f, j]
                state[f, depth + OWN + j] = halo_hi[f, j]

    def at(f, i, c):
        return state[f, i, rows_of(c), :]

    def up_y(f, i, c, a):
        b = at(f, i, c + 1) if c + 1 < chunks else nought
        return pltpu.roll(jnp.where(row_first, b, a), 7, 0) - a

    def down_y(f, i, c, a):
        b = at(f, i, c - 1) if c > 0 else nought
        return a - pltpu.roll(jnp.where(row_last, b, a), 1, 0)

    def up_z(a):
        return pltpu.roll(jnp.where(lane_first, 0.0, a), z_rows - 1, 1) - a

    def down_z(a):
        return a - pltpu.roll(jnp.where(lane_last, 0.0, a), 1, 1)

    def force(s, i, c, which):
        sxy, sxz = at(s + SXY, i, c), at(s + SXZ, i, c)
        out = [None] * 3
        if 0 in which:
            up_x = at(s + SXX, i + 1, c) - at(s + SXX, i, c)
            out[0] = up_x + down_y(s + SXY, i, c, sxy) + down_z(sxz)
        if 1 in which:
            syz = at(s + SYZ, i, c)
            syy, szz = at(s + SYY, i, c), at(s + SZZ, i, c)
            down_sxy = sxy - at(s + SXY, i - 1, c)
            down_sxz = sxz - at(s + SXZ, i - 1, c)
            out[1] = down_sxy + up_y(s + SYY, i, c, syy) + down_z(syz)
            out[2] = down_sxz + down_y(s + SYZ, i, c, syz) + up_z(szz)
        return out

    def velocity_plane(i, which, slot=None, fresh=False):
        for c in range(chunks):
            buoyancy = mats[0, i, rows_of(c), :]
            term = None
            both = [force(s, i, c, which) for s in (0, 9)]
            old = [[at(s + d, i, c) for d in range(3)] for s in (0, 9)]
            for d in which:
                for side_at, s in enumerate((0, 9)):
                    state[s + d, i, rows_of(c), :] = old[side_at][d] + buoyancy * both[side_at][d]
            if slot is not None:
                term = both[0][0] * old[1][0] + both[0][1] * old[1][1] + both[0][2] * old[1][2]
                if not fresh:
                    term = acc[0, slot, rows_of(c), :] + term
                acc[0, slot, rows_of(c), :] = term

    def strain(s, i, c):
        vx, vy, vz = at(s + VX, i, c), at(s + VY, i, c), at(s + VZ, i, c)
        return [
            vx - at(s + VX, i - 1, c),
            down_y(s + VY, i, c, vy),
            down_z(vz),
            up_z(vy) + up_y(s + VZ, i, c, vz),
            up_z(vx) + (at(s + VZ, i + 1, c) - vz),
            up_y(s + VX, i, c, vx) + (at(s + VY, i + 1, c) - vy),
        ]

    def stress_plane(i, step, slot=None, fresh=False, final=False):
        for c in range(chunks):
            m = [None] + [mats[k, i, rows_of(c), :] for k in range(1, 10)]
            both = []
            for s in (0, 9):
                e = strain(s, i, c)
                both.append(e)
                if s == 0:
                    inject = wavelet[step] * image[i, rows_of(c), :]
                else:
                    inject = data[step, i, rows_of(c), :]
                rates = [
                    m[1] * e[0] + m[2] * e[1] + m[3] * e[2],
                    m[2] * e[0] + m[4] * e[1] + m[5] * e[2],
                    m[3] * e[0] + m[5] * e[1] + m[6] * e[2] + inject,
                    m[7] * e[3],
                    m[8] * e[4],
                    m[9] * e[5],
                ]
                for f, rate in enumerate(rates):
                    state[s + SXX + f, i, rows_of(c), :] = at(s + SXX + f, i, c) + rate
            if slot is None:
                continue
            f, a = both
            terms = [
                f[0] * a[0],
                f[0] * a[1] + f[1] * a[0],
                f[0] * a[2] + f[2] * a[0],
                f[1] * a[1],
                f[1] * a[2] + f[2] * a[1],
                f[2] * a[2],
                f[3] * a[3],
                f[4] * a[4],
                f[5] * a[5],
            ]
            for n, term in enumerate(terms):
                if not fresh:
                    term = acc[1 + n, slot, rows_of(c), :] + term
                if final:
                    packed[pl.ds((1 + n) * OWN + slot + 8 * c * 10 * OWN, 8, stride=10 * OWN), :] = term
                else:
                    acc[1 + n, slot, rows_of(c), :] = term
            if final:
                packed[pl.ds(slot + 8 * c * 10 * OWN, 8, stride=10 * OWN), :] = acc[0, slot, rows_of(c), :]

    for at_step, step in enumerate(steps):
        shrink = at_step + 1
        fresh = first and at_step == 0
        final = last and shrink == depth
        velocity_plane(shrink - 1, (0,))
        for i in range(shrink, depth):
            velocity_plane(i, (0, 1, 2))

        def velocity_own(x, carry):
            velocity_plane(depth + x, (0, 1, 2), x, fresh)
            return carry

        lax.fori_loop(0, OWN, velocity_own, 0)
        for i in range(depth + OWN, length - shrink):
            velocity_plane(i, (0, 1, 2))
        velocity_plane(length - shrink, (1, 2))
        for i in range(shrink, depth):
            stress_plane(i, step)

        def stress_own(x, carry):
            stress_plane(depth + x, step, x, fresh, final)
            return carry

        lax.fori_loop(0, OWN, stress_own, 0)
        for i in range(depth + OWN, length - shrink):
            stress_plane(i, step)

    if not last:
        for f in range(18):
            for j in range(depth):
                send_dn[f, j] = state[f, depth + j]
                send_up[f, j] = state[f, OWN + j]


def run_phase(steps, first, last, wavelet, state, extra, image, data):
    fields, length, y_rows, z_rows = state.shape
    depth = (length - OWN) // 2
    whole = pl.BlockSpec(memory_space=VMEM)
    outs = [
        VMEM(state.shape, jnp.float32),
        VMEM((10, OWN, y_rows, z_rows), jnp.float32),
    ]
    aliases = {1: 0}
    if first:
        outs.append(VMEM((10, length, y_rows, z_rows), jnp.float32))
    else:
        aliases[5] = 1
    if last:
        outs.append(VMEM((y_rows * 10 * OWN, z_rows), jnp.float32))
    else:
        outs += [VMEM((fields, depth, y_rows, z_rows), jnp.float32)] * 2
    cells = (OWN + depth) * y_rows * z_rows * len(steps)
    return pl.pallas_call(
        functools.partial(phase_kernel, depth, y_rows, z_rows, steps, first, last),
        out_shape=tuple(outs),
        in_specs=[pl.BlockSpec(memory_space=SMEM)] + [whole] * (3 + len(extra)),
        out_specs=tuple([whole] * len(outs)),
        input_output_aliases=aliases,
        cost_estimate=pl.CostEstimate(flops=160 * cells, bytes_accessed=8 * cells, transcendentals=0),
        compiler_params=pltpu.CompilerParams(vmem_limit_bytes=4 << 20),
        name="phase",
    )(wavelet, *[pltpu.with_memory_space_constraint(x, VMEM) for x in (state, *extra, image, data)])


def to_next(value):
    peers = lax.axis_size("slab")
    return lax.ppermute(value, "slab", [(i, i + 1) for i in range(peers - 1)])


def to_previous(value):
    peers = lax.axis_size("slab")
    return lax.ppermute(value, "slab", [(i + 1, i) for i in range(peers - 1)])


def gather_rows(rows):
    copies = jnp.broadcast_to(rows, (lax.axis_size("shot"), *rows.shape))
    return lax.all_to_all(copies, "shot", split_axis=0, concat_axis=0, tiled=True)


def make_image(encoding, source_cells, start_cell, layers, y_rows, z_rows):
    span = layers * y_rows * z_rows
    local_cell = source_cells - start_cell
    inside = (local_cell >= 0) & (local_cell < span)
    target = jnp.where(inside, local_cell, span)
    signs = (2 * encoding - 1).astype(jnp.float32)
    image = jnp.zeros((span,), jnp.float32).at[target].add(signs, mode="drop")
    return image.reshape(layers, y_rows, z_rows)


def body(
    forward_state,
    adjoint_state,
    materials,
    wavelet,
    encoding,
    source_cells,
    receiver_depth,
    receiver_data,
):
    _, comps, own, y_rows, z_rows = forward_state.shape
    k = DEPTH
    length = own + 2 * k
    mats = materials.reshape(10, own, z_rows)
    own_rows = gather_rows(mats.reshape(10 * own, z_rows))

    recv = jnp.concatenate([receiver_data[0], receiver_depth.astype(jnp.float32)[None]], axis=0)
    tail = -(-5 * k * y_rows // z_rows)

    def rim_of(buoy_from, stiff_from):
        buoy = mats[0, buoy_from : buoy_from + k]
        stiff = mats[1:, stiff_from : stiff_from + k - 1].reshape(9 * (k - 1), z_rows)
        line = recv[:, buoy_from : buoy_from + k].reshape(-1)
        line = jnp.pad(line, (0, tail * z_rows - line.shape[0])).reshape(tail, z_rows)
        return jnp.concatenate([buoy, stiff, line], axis=0)

    side = k + 9 * (k - 1)
    rim_lo = to_next(rim_of(own - k, own - k + 1))
    rim_hi = to_previous(rim_of(0, 0))
    rim_rows = jnp.concatenate([rim_lo[:side], rim_hi[:side]], axis=0)
    rim_rows = jnp.pad(rim_rows, ((0, -2 * side % 8), (0, 0)))
    rim_rows = gather_rows(rim_rows)

    def recv_of(rim):
        return rim[side:].reshape(-1)[: 5 * k * y_rows].reshape(5, k, y_rows)

    recv = jnp.concatenate([recv_of(rim_lo), recv, recv_of(rim_hi)], axis=1)
    z_at = lax.broadcasted_iota(jnp.int32, (1, length, y_rows, z_rows), 3).astype(jnp.float32)
    data = jnp.where(z_at == recv[4:5, :, :, None], recv[:4, :, :, None], 0.0)
    start_cell = (lax.axis_index("slab") * own - k) * (y_rows * z_rows)
    image = make_image(encoding[0], source_cells[0], start_cell, length, y_rows, z_rows)

    both = [forward_state[0], adjoint_state[0]]
    halo_lo = to_next(jnp.concatenate([part[:, own - k :] for part in both], axis=0))
    halo_hi = to_previous(jnp.concatenate([part[:, :k] for part in both], axis=0))
    state = jnp.concatenate([halo_lo, jnp.concatenate(both, axis=0), halo_hi], axis=1)

    def flat(rows):
        return rows.reshape(-1, z_rows)

    phases = STEPS // k
    extra = (flat(own_rows), flat(rim_rows))
    for p in range(phases):
        first, last = p == 0, p == phases - 1
        steps = tuple(range(p * k, p * k + k))
        outs = list(run_phase(steps, first, last, wavelet, state, extra, image, data))
        state, acc = outs.pop(0), outs.pop(0)
        if first:
            stored = outs.pop(0)
        if last:
            packed = outs.pop(0)
        else:
            extra = (to_next(outs.pop(1)), to_previous(outs.pop(0)), stored, acc)

    packed = packed.reshape(y_rows, 10 * own, z_rows)
    tiles = lax.all_to_all(packed, "shot", 0, 0, tiled=True)
    shots = lax.axis_size("shot")
    gradient = jnp.sum(tiles, axis=0) * float(shots * STEPS) ** (-0.5)
    gradient = gradient.reshape(10, own, 1, z_rows)
    forward_out = state[None, :comps, k : k + own]
    adjoint_out = state[None, comps:, k : k + own]
    return forward_out, adjoint_out, gradient


def solution(mesh):
    state_spec = P("shot", None, "slab", None, None)
    return jax.shard_map(
        body,
        mesh=mesh,
        in_specs=(
            state_spec,
            state_spec,
            P(None, "slab", "shot", None),
            P(),
            P("shot", None),
            P("shot", None),
            P("slab", None),
            P("shot", None, "slab", None),
        ),
        out_specs=(state_spec, state_spec, P(None, "slab", "shot", None)),
        check_vma=False,
    )
```

time: 167 us -> 111 us (0.66)
  starting transfers between devices: 77.3 us -> 44.7 us
  other arithmetic: 32.1 us -> 8.72 us
  local copies, waits for them, and re-layouts: 34.2 us -> 11.8 us
  waiting for transfers between devices: 19.7 us -> 33.6 us
  Pallas kernels: 0 us -> 9.99 us
    ppermute x16 -> x6, starting transfers between devices: 52.5 us -> 23.3 us  [the longest x3 16.1 us: to_next(): return lax.ppermute(value, 'slab', [(i, i + 1) for i in range(peers - 1)])]
    add x35 -> x0, other arithmetic: 16.6 us -> none  [the longest x9 6.5 us: run_tile(): velocity[comp] + step_size * buoyancy * forces[comp]]
    all_to_all x3, waiting for transfers between devices: 7.75 us -> 22 us  [the longest x1 11.1 us: body(): tiles = lax.all_to_all(packed, 'shot', 0, 0, tiled=True)]
    unnamed x108 -> x30, local copies, waits for them, and re-layouts: 16.1 us -> 4.97 us
    pallas_call x0 -> x2, Pallas kernels: none -> 9.99 us  [run_phase(): pl.pallas_call(functools.partial(phase_kernel, depth, y_rows, z_rows, ste...]
    slice x50 -> x8, local copies, waits for them, and re-layouts: 8.35 us -> 2.2 us  [the longest x1 1.16 us: body(): part[:, own - k:]]
    mul x8 -> x1, other arithmetic: 5.55 us -> 0.62 us  [body(): gradient = jnp.sum(tiles, axis=0) * float(shots * STEPS) ** (-0.5)]
    another operation x34 -> x0, local copies, waits for them, and re-layouts: 4.43 us -> none  [the longest x6 2.45 us: body(): jnp.stack([part[shot_count:] for part in final_fields], axis=1)]
  transfers between devices with their start and end apart: 19 -> 9, of which waited for: 6 -> 5; matrix products, arithmetic and copies ran while one was open for 28% -> 9% of each run, Pallas kernels for 0% -> 0%
where the time goes in v1:
time: 111 us; the launch traced here: 110 us
  starting transfers between devices  44.7 us (40%)
  waiting for transfers between devices  33.6 us (30%)
  local copies, waits for them, and re-layouts  11.8 us (11%)
  Pallas kernels  9.99 us (9%)
  other arithmetic  8.72 us (8%)
    all_to_all x2, starting transfers between devices, gather_rows(): lax.all_to_all(copies, 'shot', split_axis=0, concat_axis=0, tiled=True)  16.6 us
    ppermute x3, starting transfers between devices, to_next(): return lax.ppermute(value, 'slab', [(i, i + 1) for i in range(peers - 1)])  16.1 us
    all_to_all x1, waiting for transfers between devices, body(): tiles = lax.all_to_all(packed, 'shot', 0, 0, tiled=True)  11.1 us
    all_to_all x2, waiting for transfers between devices, gather_rows(): lax.all_to_all(copies, 'shot', split_axis=0, concat_axis=0, tiled=True)  11 us
    pallas_call x2, Pallas kernels, run_phase(): pl.pallas_call(functools.partial(phase_kernel, depth, y_rows, z_rows, ste...  9.99 us
    ppermute x3, starting transfers between devices, to_previous(): return lax.ppermute(value, 'slab', [(i + 1, i) for i in range(peers - 1)])  7.13 us
    ppermute x3, waiting for transfers between devices, to_previous(): return lax.ppermute(value, 'slab', [(i + 1, i) for i in range(peers - 1)])  5.91 us
    ppermute x3, waiting for transfers between devices, to_next(): return lax.ppermute(value, 'slab', [(i, i + 1) for i in range(peers - 1)])  5.64 us
  transfers between devices with their start and end apart: 9, of which 5 were waited for; matrix products, arithmetic and copies ran while one was open for 9% of the time, Pallas kernels for 0%

profile of v1, /device:TPU:1, one launch (start us, length us, event | category | flops | bytes accessed | tf_op | source)
XLA Modules:
  0.0 109.7 jit_solution(8512236108150415717)
XLA Ops:
  0.6 0.0 copy-start.8
  0.6 0.8 slice_bitcast_fusion.3
  1.4 0.8 fusion.5
  2.3 0.7 convert_bitcast_fusion
  3.0 0.8 pad_maximum_fusion.9
  3.8 0.1 reshape.110
  3.9 3.3 %collective-permute-start.3 = (f32[14,128]{1,0:T(8,128)S(1)}, f32[14,128]{1,0:T(8,128)S(1)}, u32[]{:S(2)}, u32[]{:S(2)}) collective-permute-start(f32[14,128]{1,0:T(8,128)S(1)} %pad_maximum_fusion.7), channel_id=1, source_target_pairs={{1,0},{2,1},{3,2},{5,4},{6,5},{7,6},{9,8},{10,9},{11,10},{13,12},{... | collective-permute-start | bytes 21512 | tf_op jit(solution)/shard_map/ppermute | solution.py:243
  7.2 0.1 reshape.107
  7.3 4.7 %collective-permute-start.2 = (f32[14,128]{1,0:T(8,128)S(1)}, f32[14,128]{1,0:T(8,128)S(1)}, u32[]{:S(2)}, u32[]{:S(2)}) collective-permute-start(f32[14,128]{1,0:T(8,128)S(1)} %pad_maximum_fusion.6), channel_id=1, source_target_pairs={{0,1},{1,2},{2,3},{4,5},{5,6},{6,7},{8,9},{9,10},{10,11},{12,13},{... | collective-permute-start | bytes 21512 | tf_op jit(solution)/shard_map/ppermute | solution.py:238
  12.0 0.0 collective-permute-done.3
  12.0 0.8 collective-permute-done.2
  12.7 0.8 broadcast_in_dim.45
  13.5 8.9 %all-to-all-start.1 = ((f32[32,24,128]{2,1,0:T(8,128)}), f32[32,24,128]{2,1,0:T(8,128)S(1)}, u32[]{:S(2)}, u32[]{:S(2)}) async-start(f32[32,24,128]{2,1,0:T(8,128)} %broadcast_in_dim.45), calls=%async_computation.1 | async-start | bytes 786432 | tf_op jit(solution)/shard_map/all_to_all | solution.py:248
  22.4 0.0 copy-done.8
  22.4 1.2 %fusion.3 = (f32[9,2,32,128]{3,2,1,0:T(8,128)S(1)}, f32[9,2,32,128]{3,2,1,0:T(8,128)S(1)}, f32[9,2,32,128]{3,2,1,0:T(8,128)S(1)}, f32[9,2,32,128]{3,2,1,0:T(8,128)S(1)}) fusion(f32[9,8,32,128]{3,2,1,0:T(8,128)S(1)} %bitcast.45, f32[9,8,32,128]{3,2,1,0:T(8,128)} %bitcast.46), kind=kLoop, calls=%fused_computation.33 | loop fusion | bytes 2359296 | tf_op jit(solution)/shard_map/slice | solution.py:304
  23.6 0.0 copy-start.11
  23.7 1.9 %collective-permute-start.1 = (f32[18,2,32,128]{3,2,1,0:T(8,128)S(1)}, f32[18,2,32,128]{3,2,1,0:T(8,128)S(1)}, u32[]{:S(2)}, u32[]{:S(2)}) collective-permute-start(f32[18,2,32,128]{3,2,1,0:T(8,128)S(1)} %pad_maximum_fusion.2), channel_id=1, source_target_pairs={{1,0},{2,1},{3,2},{5,4},{6,5},{7,6},{9,8},{10,9},{11,10},{13,12},{... | collective-permute-start | bytes 1769480 | tf_op jit(solution)/shard_map/ppermute | solution.py:243
  25.7 6.6 %collective-permute-start = (f32[18,2,32,128]{3,2,1,0:T(8,128)S(1)}, f32[18,2,32,128]{3,2,1,0:T(8,128)}, u32[]{:S(2)}, u32[]{:S(2)}) collective-permute-start(f32[18,2,32,128]{3,2,1,0:T(8,128)S(1)} %pad_maximum_fusion.1), channel_id=1, source_target_pairs={{0,1},{1,2},{2,3},{4,5},{5,6},{6,7},{8,9},{9,10},{10,11},{12,13},{... | collective-permute-start | bytes 1769480 | tf_op jit(solution)/shard_map/ppermute | solution.py:238
  32.2 0.0 all-to-all-done.1
  32.3 0.0 copy-start.4
  32.3 0.0 copy-done.11
  32.3 1.2 %broadcast_in_dim.43 = f32[32,80,128]{2,1,0:T(8,128)} broadcast(f32[80,128]{1,0:T(8,128)S(1)} %bitcast.53), dimensions={1,2} | broadcast | bytes 1351680 | tf_op jit(solution)/shard_map/broadcast_in_dim | solution.py:247
  33.5 0.0 copy-start.12
  33.5 0.0 copy-start.13
  33.5 0.0 copy-start.10
  33.5 0.0 copy-done.4
  33.5 7.7 %all-to-all-start = ((f32[32,80,128]{2,1,0:T(8,128)}), f32[32,80,128]{2,1,0:T(8,128)}, u32[]{:S(2)}, u32[]{:S(2)}) async-start(f32[32,80,128]{2,1,0:T(8,128)} %broadcast_in_dim.43), calls=%async_computation | async-start | bytes 2621440 | tf_op jit(solution)/shard_map/all_to_all | solution.py:248
  41.1 0.0 copy-done.12
  41.2 0.0 copy-done.13
  41.2 1.3 %scatter_custom_fusion = f32[49152]{0:T(1024)} fusion(s32[16]{0:T(128)S(1)} %fusion.2, f32[16]{0:T(128)S(1)} %convert_bitcast_fusion.1, f32[]{:T(128)} %constant.10.clone.1), kind=kCustom, calls=%fused_computation.8 | custom fusion | flops 16 | bytes 196612 | tf_op jit(solution)/shard_map/scatter-add | solution.py:257
  42.5 0.1 slice.82
  42.6 0.1 slice.79
  42.7 0.0 copy-done.10
  42.7 0.1 broadcast_compare_fusion
  42.9 1.1 %broadcast_select_fusion.refs_5_.refs_7_ = f32[4,12,32,128]{3,2,1,0:T(8,128)} fusion(f32[4,12,32]{2,1,0:T(8,128)S(1)} %pad_maximum_fusion.3, pred[12,32,128]{2,1,0:T(8,128)(4,1)S(1)} %broadcast_compare_fusion), kind=kLoop, calls=%fused_computation.6 | loop fusion | flops 196608 | bytes 841728 | tf_op jit(solution)/shard_map/jit(_where)/select_n | solution.py:299
  44.0 0.0 copy-start.7
  44.0 0.0 collective-permute-done.1
  44.0 0.8 copy-done.9
  44.8 0.0 collective-permute-done
  44.8 2.5 %pad_maximum_fusion.refs_1_ = f32[18,12,32,128]{3,2,1,0:T(8,128)S(1)} fusion(f32[18,2,32,128]{3,2,1,0:T(8,128)} %copy-done.9, f32[9,8,32,128]{3,2,1,0:T(8,128)} %bitcast.47, f32[9,8,32,128]{3,2,1,0:T(8,128)} %bitcast.44, f32[18,2,32,128]{3,2,1,0:T(8,128)} %collective-permute-done), kind=kLoop, calls=%fused_computation.1 | loop fusion | flops 2654208 | bytes 7077888 | tf_op jit(solution)/shard_map/concatenate | solution.py:306
  47.3 11.0 %all-to-all-done = f32[32,80,128]{2,1,0:T(8,128)} async-done(((f32[32,80,128]{2,1,0:T(8,128)}), f32[32,80,128]{2,1,0:T(8,128)}, u32[]{:S(2)}, u32[]{:S(2)}) %all-to-all-start) | async-done | bytes 1310752 | tf_op jit(solution)/shard_map/all_to_all | solution.py:248
  58.3 0.0 copy-done.7
  58.3 0.0 copy-start
  58.3 1.1 %copy-done = f32[4,12,32,128]{3,2,1,0:T(8,128)S(1)} copy-done((f32[4,12,32,128]{3,2,1,0:T(8,128)S(1)}, f32[4,12,32,128]{3,2,1,0:T(8,128)}, u32[]{:S(2)}) %copy-start) | copy-done | bytes 786456
  59.4 0.0 copy-start.2
  59.4 0.9 copy-done.2
  60.4 0.0 copy-start.5
  60.4 1.0 copy-done.5
  61.4 0.0 copy-start.1
  61.4 5.6 %phase.2 = (f32[18,12,32,128]{3,2,1,0:T(8,128)S(1)}, f32[10,8,32,128]{3,2,1,0:T(8,128)S(1)}, f32[10,12,32,128]{3,2,1,0:T(8,128)S(1)}, f32[18,2,32,128]{3,2,1,0:T(8,128)S(1)}, f32[18,2,32,128]{3,2,1,0:T(8,128)S(1)}) custom-call(f32[4]{0:T(128)S(1)} %copy-done.7, f32[18,12,32,128]{3,2,1,0:T(8,128)S(1)} %pad_maximum_fusion.refs_1_, ...), custom_call_target="tpu_custom_call", output_to_operand_aliasing={{0}: (1, {})} | custom-call | flops 13107200 | bytes 655360 | tf_op jit(solution)/shard_map/phase/pallas_call | solution.py:224
  67.0 4.9 %collective-permute-start.4 = (f32[18,2,32,128]{3,2,1,0:T(8,128)S(1)}, f32[18,2,32,128]{3,2,1,0:T(8,128)S(1)}, u32[]{:S(2)}, u32[]{:S(2)}) collective-permute-start(f32[18,2,32,128]{3,2,1,0:T(8,128)S(1)} %get-tuple-element.11), channel_id=1, source_target_pairs={{0,1},{1,2},{2,3},{4,5},{5,6},{6,7},{8,9},{9,10},{10,11},{12,13},{... | collective-permute-start | bytes 1769480 | tf_op jit(solution)/shard_map/ppermute | solution.py:238
  71.9 1.9 %collective-permute-start.5 = (f32[18,2,32,128]{3,2,1,0:T(8,128)S(1)}, f32[18,2,32,128]{3,2,1,0:T(8,128)S(1)}, u32[]{:S(2)}, u32[]{:S(2)}) collective-permute-start(f32[18,2,32,128]{3,2,1,0:T(8,128)S(1)} %get-tuple-element.12), channel_id=1, source_target_pairs={{1,0},{2,1},{3,2},{5,4},{6,5},{7,6},{9,8},{10,9},{11,10},{13,12},{... | collective-permute-start | bytes 1769480 | tf_op jit(solution)/shard_map/ppermute | solution.py:243
  73.8 4.9 %collective-permute-done.4.refs_2_ = f32[18,2,32,128]{3,2,1,0:T(8,128)S(1)} collective-permute-done((f32[18,2,32,128]{3,2,1,0:T(8,128)S(1)}, f32[18,2,32,128]{3,2,1,0:T(8,128)S(1)}, u32[]{:S(2)}, u32[]{:S(2)}) %collective-permute-start.4) | collective-permute-done | bytes 589856 | tf_op jit(solution)/shard_map/ppermute | solution.py:238
  78.7 5.9 %collective-permute-done.5.refs_3_ = f32[18,2,32,128]{3,2,1,0:T(8,128)S(1)} collective-permute-done((f32[18,2,32,128]{3,2,1,0:T(8,128)S(1)}, f32[18,2,32,128]{3,2,1,0:T(8,128)S(1)}, u32[]{:S(2)}, u32[]{:S(2)}) %collective-permute-start.5) | collective-permute-done | bytes 589856 | tf_op jit(solution)/shard_map/ppermute | solution.py:243
  84.6 0.0 copy-done.1
  84.6 0.0 copy-done.3
  84.6 4.4 %phase.3 = (f32[18,12,32,128]{3,2,1,0:T(8,128)S(1)}, f32[10,8,32,128]{3,2,1,0:T(8,128)S(1)}, f32[2560,128]{1,0:T(8,128)S(1)}) custom-call(f32[4]{0:T(128)S(1)} %copy-done.7, f32[18,12,32,128]{3,2,1,0:T(8,128)S(1)} %get-tuple-element.10.refs_1_, f32[18,2,32,128]{3,2,1,0:T(8,128)S(1)} %collective-permute-done.4.refs_2_, ...), custom_call_target="tpu_custom_call", output_to_operand_aliasing={{0}: (1, {}), {1}: (5, {})} | custom-call | flops 13107200 | bytes 655360 | tf_op jit(solution)/shard_map/phase/pallas_call | solution.py:224
  89.0 0.0 copy-start.6
  89.0 1.1 copy-done.6
  90.1 4.8 %all-to-all-start.2 = ((f32[32,80,128]{2,1,0:T(8,128)}), f32[32,80,128]{2,1,0:T(8,128)}, u32[]{:S(2)}, u32[]{:S(2)}) async-start(f32[32,80,128]{2,1,0:T(8,128)} %bitcast.43), calls=%async_computation.2 | async-start | bytes 2621440 | tf_op jit(solution)/shard_map/all_to_all | solution.py:326
  94.9 1.7 %slice_bitcast_fusion = (f32[1,9,8,32,128]{4,3,2,1,0:T(8,128)}, f32[1,9,8,32,128]{4,3,2,1,0:T(8,128)}) fusion(f32[18,12,32,128]{3,2,1,0:T(8,128)S(1)} %get-tuple-element.15), kind=kLoop, calls=%fused_computation.2 | loop fusion | bytes 4718592 | tf_op jit(solution)/shard_map/broadcast_in_dim | solution.py:331
  96.6 11.1 %all-to-all-done.2 = f32[32,80,128]{2,1,0:T(8,128)} async-done(((f32[32,80,128]{2,1,0:T(8,128)}), f32[32,80,128]{2,1,0:T(8,128)}, u32[]{:S(2)}, u32[]{:S(2)}) %all-to-all-start.2) | async-done | bytes 1310752 | tf_op jit(solution)/shard_map/all_to_all | solution.py:326
  107.6 1.4 %reduce_sum.9 = f32[80,128]{1,0:T(8,128)S(1)} reduce(f32[32,80,128]{2,1,0:T(8,128)} %all-to-all-done.2, f32[]{:T(128)} %constant.10.clone.1), dimensions={0}, to_apply=%region_1.2 | reduce | flops 317440 | bytes 1351684 | tf_op jit(solution)/shard_map/reduce_sum | solution.py:328
  109.0 0.6 broadcast_multiply_fusion
  (20 shorter events, 0.2 us)
Async XLA Ops:
  0.6 21.8 %copy-start.8 = (f32[1,9,8,32,128]{4,3,2,1,0:T(8,128)S(1)}, f32[1,9,8,32,128]{4,3,2,1,0:T(8,128)}, u32[]{:S(2)}) copy-start(f32[1,9,8,32,128]{4,3,2,1,0:T(8,128)} %param.8) | copy-start | bytes 3538948
  3.9 8.1 %collective-permute-start.3 = (f32[14,128]{1,0:T(8,128)S(1)}, f32[14,128]{1,0:T(8,128)S(1)}, u32[]{:S(2)}, u32[]{:S(2)}) collective-permute-start(f32[14,128]{1,0:T(8,128)S(1)} %pad_maximum_fusion.7), channel_id=1, source_target_pairs={{1,0},{2,1},{3,2},{5,4},{6,5},{7,6},{9,8},{10,9},{11,10},{13,12},{... | collective-permute-start | bytes 21512 | tf_op jit(solution)/shard_map/ppermute | solution.py:243
  7.3 5.4 %collective-permute-start.2 = (f32[14,128]{1,0:T(8,128)S(1)}, f32[14,128]{1,0:T(8,128)S(1)}, u32[]{:S(2)}, u32[]{:S(2)}) collective-permute-start(f32[14,128]{1,0:T(8,128)S(1)} %pad_maximum_fusion.6), channel_id=1, source_target_pairs={{0,1},{1,2},{2,3},{4,5},{5,6},{6,7},{8,9},{9,10},{10,11},{12,13},{... | collective-permute-start | bytes 21512 | tf_op jit(solution)/shard_map/ppermute | solution.py:238
  13.5 18.7 %all-to-all-start.1 = ((f32[32,24,128]{2,1,0:T(8,128)}), f32[32,24,128]{2,1,0:T(8,128)S(1)}, u32[]{:S(2)}, u32[]{:S(2)}) async-start(f32[32,24,128]{2,1,0:T(8,128)} %broadcast_in_dim.45), calls=%async_computation.1 | async-start | bytes 786432 | tf_op jit(solution)/shard_map/all_to_all | solution.py:248
  23.6 8.7 %copy-start.11 = (f32[10,8,1,128]{3,2,1,0:T(1,128)S(1)}, f32[10,8,1,128]{3,2,1,0:T(1,128)}, u32[]{:S(2)}) copy-start(f32[10,8,1,128]{3,2,1,0:T(1,128)} %param.10) | copy-start | bytes 122884
  23.7 20.3 %collective-permute-start.1 = (f32[18,2,32,128]{3,2,1,0:T(8,128)S(1)}, f32[18,2,32,128]{3,2,1,0:T(8,128)S(1)}, u32[]{:S(2)}, u32[]{:S(2)}) collective-permute-start(f32[18,2,32,128]{3,2,1,0:T(8,128)S(1)} %pad_maximum_fusion.2), channel_id=1, source_target_pairs={{1,0},{2,1},{3,2},{5,4},{6,5},{7,6},{9,8},{10,9},{11,10},{13,12},{... | collective-permute-start | bytes 1769480 | tf_op jit(solution)/shard_map/ppermute | solution.py:243
  25.7 19.2 %collective-permute-start = (f32[18,2,32,128]{3,2,1,0:T(8,128)S(1)}, f32[18,2,32,128]{3,2,1,0:T(8,128)}, u32[]{:S(2)}, u32[]{:S(2)}) collective-permute-start(f32[18,2,32,128]{3,2,1,0:T(8,128)S(1)} %pad_maximum_fusion.1), channel_id=1, source_target_pairs={{0,1},{1,2},{2,3},{4,5},{5,6},{6,7},{8,9},{9,10},{10,11},{12,13},{... | collective-permute-start | bytes 1769480 | tf_op jit(solution)/shard_map/ppermute | solution.py:238
  32.3 1.2 %copy-start.4 = (f32[32,24,128]{2,1,0:T(8,128)}, f32[32,24,128]{2,1,0:T(8,128)S(1)}, u32[]{:S(2)}) copy-start(f32[32,24,128]{2,1,0:T(8,128)S(1)} %all-to-all-done.1) | copy-start | bytes 1179652
  33.5 7.7 %copy-start.12 = (s32[1,16]{1,0:T(1,128)S(1)}, s32[1,16]{1,0:T(1,128)}, u32[]{:S(2)}) copy-start(s32[1,16]{1,0:T(1,128)} %param.12) | copy-start | bytes 196
  33.5 7.7 %copy-start.13 = (s32[1,16]{1,0:T(1,128)S(1)}, s32[1,16]{1,0:T(1,128)}, u32[]{:S(2)}) copy-start(s32[1,16]{1,0:T(1,128)} %param.13) | copy-start | bytes 196
  33.5 9.2 %copy-start.10 = (f32[1,4,8,32]{3,2,1,0:T(8,128)S(1)}, f32[1,4,8,32]{3,2,1,0:T(8,128)}, u32[]{:S(2)}) copy-start(f32[1,4,8,32]{3,2,1,0:T(8,128)} %param.15) | copy-start | bytes 12292
  33.5 24.8 %all-to-all-start = ((f32[32,80,128]{2,1,0:T(8,128)}), f32[32,80,128]{2,1,0:T(8,128)}, u32[]{:S(2)}, u32[]{:S(2)}) async-start(f32[32,80,128]{2,1,0:T(8,128)} %broadcast_in_dim.43), calls=%async_computation | async-start | bytes 2621440 | tf_op jit(solution)/shard_map/all_to_all | solution.py:248
  44.0 14.3 %copy-start.7 = (f32[4]{0:T(128)S(1)}, f32[4]{0:T(128)}, u32[]{:S(2)}) copy-start(f32[4]{0:T(128)} %refs_0_.3) | copy-start | bytes 52
  44.0 0.8 copy-start.9
  58.3 1.1 %copy-start = (f32[4,12,32,128]{3,2,1,0:T(8,128)S(1)}, f32[4,12,32,128]{3,2,1,0:T(8,128)}, u32[]{:S(2)}) copy-start(f32[4,12,32,128]{3,2,1,0:T(8,128)} %broadcast_select_fusion.refs_5_.refs_7_) | copy-start | bytes 2359300
  59.4 0.9 copy-start.2
  60.4 1.0 copy-start.5
  61.4 23.2 %copy-start.1 = (f32[4,12,32,128]{3,2,1,0:T(8,128)S(1)}, f32[4,12,32,128]{3,2,1,0:T(8,128)}, u32[]{:S(2)}) copy-start(f32[4,12,32,128]{3,2,1,0:T(8,128)} %broadcast_select_fusion.refs_5_.refs_7_) | copy-start | bytes 2359300
  61.4 23.2 %copy-start.3 = (f32[49152]{0:T(1024)S(1)}, f32[49152]{0:T(1024)}, u32[]{:S(2)}) copy-start(f32[49152]{0:T(1024)} %scatter_custom_fusion) | copy-start | bytes 589828
  67.0 11.7 %collective-permute-start.4 = (f32[18,2,32,128]{3,2,1,0:T(8,128)S(1)}, f32[18,2,32,128]{3,2,1,0:T(8,128)S(1)}, u32[]{:S(2)}, u32[]{:S(2)}) collective-permute-start(f32[18,2,32,128]{3,2,1,0:T(8,128)S(1)} %get-tuple-element.11), channel_id=1, source_target_pairs={{0,1},{1,2},{2,3},{4,5},{5,6},{6,7},{8,9},{9,10},{10,11},{12,13},{... | collective-permute-start | bytes 1769480 | tf_op jit(solution)/shard_map/ppermute | solution.py:238
  71.9 12.7 %collective-permute-start.5 = (f32[18,2,32,128]{3,2,1,0:T(8,128)S(1)}, f32[18,2,32,128]{3,2,1,0:T(8,128)S(1)}, u32[]{:S(2)}, u32[]{:S(2)}) collective-permute-start(f32[18,2,32,128]{3,2,1,0:T(8,128)S(1)} %get-tuple-element.12), channel_id=1, source_target_pairs={{1,0},{2,1},{3,2},{5,4},{6,5},{7,6},{9,8},{10,9},{11,10},{13,12},{... | collective-permute-start | bytes 1769480 | tf_op jit(solution)/shard_map/ppermute | solution.py:243
  89.0 1.1 copy-start.6
  90.1 17.6 %all-to-all-start.2 = ((f32[32,80,128]{2,1,0:T(8,128)}), f32[32,80,128]{2,1,0:T(8,128)}, u32[]{:S(2)}, u32[]{:S(2)}) async-start(f32[32,80,128]{2,1,0:T(8,128)} %bitcast.43), calls=%async_computation.2 | async-start | bytes 2621440 | tf_op jit(solution)/shard_map/all_to_all | solution.py:326

commit v2 on v1

v2 whole, which is shorter than its diff:
```python
import functools

import jax
import jax.numpy as jnp
from jax import lax
from jax.experimental import pallas as pl
from jax.experimental.pallas import tpu as pltpu
from jax.sharding import PartitionSpec as P

STEPS = 4
DEPTH = 2
OWN = 8
LENGTH = OWN + 2 * DEPTH
VX, VY, VZ, SXX, SYY, SZZ, SYZ, SXZ, SXY = range(9)
step_size = 0.25
VMEM = pltpu.VMEM
ROWS = 104

BOTH = (SXX, SXY, SXZ)
UP = [(VX, OWN - 2), (VY, OWN - 1), (VZ, OWN - 1)]
UP += [(f, OWN - 2) for f in BOTH] + [(f, OWN - 1) for f in range(SXX, SXY + 1)]
DOWN = [(VX, 0), (VY, 1), (VZ, 1)] + [(f, j) for f in range(SXX, SXY + 1) for j in (0, 1)]
UP_FIRST = UP + [(VX, OWN - 1)]
DOWN_FIRST = DOWN + [(VY, 0), (VZ, 0)]


def sizes(first):
    up, down = (UP_FIRST, DOWN_FIRST) if first else (UP, DOWN)
    return up, down, 2 * max(len(up), len(down))


def is_odd():
    return lax.rem(lax.axis_index("slab"), 2) == 1


def fill_payloads(first, state, cross, chip, data=None):
    up, down, base = sizes(first)

    def fill(target, planes, layer):
        for s in range(2):
            for n, (f, j) in enumerate(planes):
                target[s * len(planes) + n] = state[9 * s + f, DEPTH + j]
        if data is not None:
            for n in range(STEPS // DEPTH):
                target[base + n] = data[n * DEPTH, layer]

    @pl.when(is_odd())
    def _():
        fill(cross, up, OWN - 1)
        fill(chip, down, 0)

    @pl.when(jnp.logical_not(is_odd()))
    def _():
        fill(cross, down, 0)
        fill(chip, up, OWN - 1)


RIM = (((VY, 0), (VZ, 0)), ((VX, LENGTH - 1), (9 + VX, LENGTH - 1)))


def drain_payloads(first, state, cross, chip):
    up, down, base = sizes(first)

    def drain(source, planes, shift, at):
        for s in range(2):
            for n, (f, j) in enumerate(planes):
                state[9 * s + f, DEPTH + j + shift] = source[s * len(planes) + n]
        if first:
            for n, place in enumerate(RIM[at]):
                state[place] = source[base + n]

    @pl.when(is_odd())
    def _():
        drain(chip, up, -OWN, 0)
        drain(cross, down, OWN, 1)

    @pl.when(jnp.logical_not(is_odd()))
    def _():
        drain(cross, up, -OWN, 0)
        drain(chip, down, OWN, 1)


def edges_kernel(materials, own, far, near, sem):
    copy = pltpu.make_async_copy(materials, own, sem)
    copy.start()
    copy.wait()

    def take(target, layer):
        for m in range(10):
            target[pl.ds(DEPTH * m, DEPTH), :] = own[pl.ds(OWN * m + layer, DEPTH), :]

    @pl.when(is_odd())
    def _():
        take(far, OWN - DEPTH)
        take(near, 0)

    @pl.when(jnp.logical_not(is_odd()))
    def _():
        take(far, 0)
        take(near, OWN - DEPTH)


def spread_kernel(own, cross, chip, out, block, sem):
    block[pl.ds(0, 10 * OWN), :] = own[...]
    block[pl.ds(10 * OWN, ROWS - 10 * OWN), :] = jnp.zeros((ROWS - 10 * OWN, own.shape[1]), jnp.float32)
    side = DEPTH + 9

    def put(source, base, inner):
        block[pl.ds(base, DEPTH), :] = source[pl.ds(0, DEPTH), :]
        for m in range(9):
            block[pl.ds(base + DEPTH + m, 1), :] = source[pl.ds(DEPTH * (1 + m) + inner, 1), :]

    @pl.when(is_odd())
    def _():
        put(chip, 10 * OWN, DEPTH - 1)
        put(cross, 10 * OWN + side, 0)

    @pl.when(jnp.logical_not(is_odd()))
    def _():
        put(cross, 10 * OWN, DEPTH - 1)
        put(chip, 10 * OWN + side, 0)

    copies = [pltpu.make_async_copy(block, out.at[j], sem.at[j]) for j in range(out.shape[0])]
    for copy in copies:
        copy.start()
    for copy in copies:
        copy.wait()


def stage_kernel(forward, adjoint, data, state, cross, chip, sems):
    inner = pl.ds(DEPTH, OWN)
    copies = [
        pltpu.make_async_copy(part.at[f], state.at[9 * s + f, inner], sems.at[9 * s + f])
        for s, part in enumerate((forward, adjoint))
        for f in range(9)
    ]
    for copy in copies:
        copy.start()
    for copy in copies:
        copy.wait()
    fill_payloads(True, state, cross, chip, data)


def join_kernel(state_in, cross, chip, state):
    drain_payloads(True, state, cross, chip)


def draw_image(encoding, cells, image):
    layers, y_rows, z_rows = image.shape
    image[...] = jnp.zeros(image.shape, jnp.float32)
    lane = lax.broadcasted_iota(jnp.int32, (1, z_rows), 1)
    first_x = lax.axis_index("slab") * OWN - DEPTH
    for n in range(cells.shape[1]):
        cell = cells[0, n]
        x = cell // (y_rows * z_rows) - first_x
        inside = jnp.logical_and(x >= 0, x < layers)
        x = jnp.where(inside, x, 0)
        y = lax.rem(cell // z_rows, y_rows)
        sign = jnp.where(inside, 2 * encoding[0, n] - 1, 0).astype(jnp.float32)
        spot = jnp.where(lane == lax.rem(cell, z_rows), sign, 0.0)
        image[x, pl.ds(y, 1), :] = image[x, pl.ds(y, 1), :] + spot


def phase_kernel(first, y_rows, z_rows, *refs):
    refs = list(refs)
    if first:
        wavelet, encoding, cells, _, gathered, data_in, state, acc, mats, image, cross, chip, rows_ref, data, sems = refs
    else:
        wavelet, _, _, cross_in, chip_in, mats, image, data_in, state, acc, packed, rows_ref, data, sems = refs

    chunks = y_rows // 8
    scale = float(y_rows * STEPS) ** (-0.5)
    row = lax.broadcasted_iota(jnp.int32, (8, z_rows), 0)
    lane = lax.broadcasted_iota(jnp.int32, (8, z_rows), 1)
    row_first, row_last = row == 0, row == 7
    lane_first, lane_last = lane == 0, lane == z_rows - 1
    nought = jnp.zeros((8, z_rows), jnp.float32)

    def rows_of(c):
        return pl.ds(8 * c, 8)

    if first:
        copies = [
            pltpu.make_async_copy(gathered.at[c], rows_ref.at[c], sems.at[c]) for c in range(chunks)
        ]
        for copy in copies:
            copy.start()
    start = 0 if first else DEPTH
    data_copy = pltpu.make_async_copy(data_in.at[pl.ds(start, DEPTH)], data, sems.at[chunks])
    data_copy.start()
    if not first:
        drain_payloads(False, state, cross_in, chip_in)
    if first:
        draw_image(encoding, cells, image)
        side = DEPTH + 9
        for c in range(chunks):
            copies[c].wait()

            def take(r):
                return step_size * rows_ref[c, pl.ds(r, 8, stride=ROWS), :]

            for r in range(10 * OWN):
                mats[r // OWN, DEPTH + r % OWN, rows_of(c), :] = take(r)
            for base, buoy_at, stiff_at in ((80, 0, DEPTH - 1), (80 + side, DEPTH + OWN, DEPTH + OWN)):
                for j in range(DEPTH):
                    mats[0, buoy_at + j, rows_of(c), :] = take(base + j)
                for m in range(9):
                    mats[1 + m, stiff_at, rows_of(c), :] = take(base + DEPTH + m)

    def at(f, i, c):
        return state[f, i, rows_of(c), :]

    def up_y(f, i, c, a):
        b = at(f, i, c + 1) if c + 1 < chunks else nought
        return pltpu.roll(jnp.where(row_first, b, a), 7, 0) - a

    def down_y(f, i, c, a):
        b = at(f, i, c - 1) if c > 0 else nought
        return a - pltpu.roll(jnp.where(row_last, b, a), 1, 0)

    def up_z(a):
        return pltpu.roll(jnp.where(lane_first, 0.0, a), z_rows - 1, 1) - a

    def down_z(a):
        return a - pltpu.roll(jnp.where(lane_last, 0.0, a), 1, 1)

    def force(s, i, c, which):
        sxy, sxz = at(s + SXY, i, c), at(s + SXZ, i, c)
        out = [None] * 3
        if 0 in which:
            up_x = at(s + SXX, i + 1, c) - at(s + SXX, i, c)
            out[0] = up_x + down_y(s + SXY, i, c, sxy) + down_z(sxz)
        if 1 in which:
            syz = at(s + SYZ, i, c)
            syy, szz = at(s + SYY, i, c), at(s + SZZ, i, c)
            down_sxy = sxy - at(s + SXY, i - 1, c)
            down_sxz = sxz - at(s + SXZ, i - 1, c)
            out[1] = down_sxy + up_y(s + SYY, i, c, syy) + down_z(syz)
            out[2] = down_sxz + down_y(s + SYZ, i, c, syz) + up_z(szz)
        return out

    def velocity_plane(i, which, slot=None, fresh=False):
        for c in range(chunks):
            buoyancy = mats[0, i, rows_of(c), :]
            both = [force(s, i, c, which) for s in (0, 9)]
            old = [[at(s + d, i, c) for d in range(3)] for s in (0, 9)]
            for d in which:
                for n, s in enumerate((0, 9)):
                    state[s + d, i, rows_of(c), :] = old[n][d] + buoyancy * both[n][d]
            if slot is not None:
                term = both[0][0] * old[1][0] + both[0][1] * old[1][1] + both[0][2] * old[1][2]
                if not fresh:
                    term = acc[0, slot, rows_of(c), :] + term
                acc[0, slot, rows_of(c), :] = term

    def strain(s, i, c):
        vx, vy, vz = at(s + VX, i, c), at(s + VY, i, c), at(s + VZ, i, c)
        return [
            vx - at(s + VX, i - 1, c),
            down_y(s + VY, i, c, vy),
            down_z(vz),
            up_z(vy) + up_y(s + VZ, i, c, vz),
            up_z(vx) + (at(s + VZ, i + 1, c) - vz),
            up_y(s + VX, i, c, vx) + (at(s + VY, i + 1, c) - vy),
        ]

    def stress_chunk(i, c, step, slot=None, fresh=False, final=False, rim=None):
        m = [None] + [mats[k, i, rows_of(c), :] for k in range(1, 10)]
        both = []
        for s in (0, 9):
            e = strain(s, i, c)
            both.append(e)
            if s == 0:
                inject = wavelet[step] * image[i, rows_of(c), :]
            elif rim is None:
                inject = data[step - start, i - DEPTH, rows_of(c), :]
            else:
                inject = at(*RIM[rim][step // DEPTH], c)
            rates = [
                m[1] * e[0] + m[2] * e[1] + m[3] * e[2],
                m[2] * e[0] + m[4] * e[1] + m[5] * e[2],
                m[3] * e[0] + m[5] * e[1] + m[6] * e[2] + inject,
                m[7] * e[3],
                m[8] * e[4],
                m[9] * e[5],
            ]
            for f, rate in enumerate(rates):
                state[s + SXX + f, i, rows_of(c), :] = at(s + SXX + f, i, c) + rate
        if slot is None:
            return
        f, a = both
        terms = [
            f[0] * a[0],
            f[0] * a[1] + f[1] * a[0],
            f[0] * a[2] + f[2] * a[0],
            f[1] * a[1],
            f[1] * a[2] + f[2] * a[1],
            f[2] * a[2],
            f[3] * a[3],
            f[4] * a[4],
            f[5] * a[5],
        ]
        for n, term in enumerate(terms):
            if not fresh:
                term = acc[1 + n, slot, rows_of(c), :] + term
            if final:
                rows_ref[c, pl.ds((1 + n) * OWN + slot, 8, stride=10 * OWN), :] = scale * term
            else:
                acc[1 + n, slot, rows_of(c), :] = term
        if final:
            rows_ref[c, pl.ds(slot, 8, stride=10 * OWN), :] = scale * acc[0, slot, rows_of(c), :]

    inner, low, high = DEPTH + OWN, DEPTH - 1, DEPTH + OWN
    for at_step in range(DEPTH):
        step = at_step if first else DEPTH + at_step
        fresh = first and at_step == 0
        final = not first and at_step == DEPTH - 1
        velocity_plane(at_step, (0,))
        if at_step == 0:
            velocity_plane(low, (0, 1, 2))

        def velocity_own(x, carry):
            velocity_plane(DEPTH + x, (0, 1, 2), x, fresh)
            return carry

        lax.fori_loop(0, OWN, velocity_own, 0)
        if at_step == 0:
            velocity_plane(high, (0, 1, 2))
        velocity_plane(LENGTH - 1 - at_step, (1, 2))
        if at_step == 0:
            data_copy.wait()
            for c in range(chunks):
                stress_chunk(low, c, step, rim=0)
                stress_chunk(high, c, step, rim=1)
        if not final:

            def stress_own(x, carry):
                for c in range(chunks):
                    stress_chunk(DEPTH + x, c, step, x, fresh)
                return carry

            lax.fori_loop(0, OWN, stress_own, 0)
            continue
        copies = []
        for c in range(chunks):

            def stress_last(x, carry):
                for n in range(4):
                    stress_chunk(DEPTH + 4 * x + n, c, step, 4 * x + n, fresh, True)
                return carry

            lax.fori_loop(0, OWN // 4, stress_last, 0)
            copy = pltpu.make_async_copy(rows_ref.at[c], packed.at[c], sems.at[c])
            copy.start()
            copies.append(copy)
        for copy in copies:
            copy.wait()

    if first:
        fill_payloads(False, state, cross, chip)


def in_vmem(x):
    return pltpu.with_memory_space_constraint(x, VMEM)


def in_hbm(x):
    return pltpu.with_memory_space_constraint(x, pltpu.HBM)


WHOLE = pl.BlockSpec(memory_space=VMEM)
SCALARS = pl.BlockSpec(memory_space=pltpu.SMEM)
IN_HBM = pl.BlockSpec(memory_space=pltpu.HBM)


def estimate(flops, moved):
    return pl.CostEstimate(flops=flops, bytes_accessed=moved, transcendentals=0)


def run_phase(first, scalars, state, middle, data):
    y_rows, z_rows = state.shape[2:]
    chunks = y_rows // 8
    outs = [VMEM(state.shape, jnp.float32), VMEM((10, OWN, y_rows, z_rows), jnp.float32)]
    specs = [SCALARS] * len(scalars) + [WHOLE]
    aliases = {len(scalars): 0}
    if first:
        (gathered,) = middle
        middle = [in_hbm(gathered.reshape(chunks, 8 * ROWS, z_rows))]
        specs += [IN_HBM]
        outs += [VMEM((10, LENGTH, y_rows, z_rows), jnp.float32), VMEM((LENGTH, y_rows, z_rows), jnp.float32)]
        outs += [VMEM((sizes(False)[2], y_rows, z_rows), jnp.float32)] * 2
        out_specs = [WHOLE] * len(outs)
        rows = VMEM((chunks, 8 * ROWS, z_rows), jnp.float32)
    else:
        middle = [in_vmem(x) for x in middle]
        specs += [WHOLE] * len(middle)
        aliases[len(scalars) + 1] = 1
        outs.append(pltpu.HBM((chunks, 8 * 10 * OWN, z_rows), jnp.float32))
        out_specs = [WHOLE, WHOLE, IN_HBM]
        rows = VMEM((chunks, 8 * 10 * OWN, z_rows), jnp.float32)
    cells = (OWN + 2) * y_rows * z_rows * DEPTH
    return pl.pallas_call(
        functools.partial(phase_kernel, first, y_rows, z_rows),
        out_shape=tuple(outs),
        in_specs=specs + [IN_HBM],
        out_specs=tuple(out_specs),
        scratch_shapes=[
            rows,
            VMEM((DEPTH, OWN, y_rows, z_rows), jnp.float32),
            pltpu.SemaphoreType.DMA((chunks + 1,)),
        ],
        input_output_aliases=aliases,
        cost_estimate=estimate(160 * cells, 100 * cells),
        compiler_params=pltpu.CompilerParams(vmem_limit_bytes=6 << 20),
        name="phase_first" if first else "phase_last",
    )(*scalars, in_vmem(state), *middle, in_hbm(data))


def swap_across(value):
    peers = lax.axis_size("slab")
    return lax.ppermute(value, "slab", [p for i in range(1, peers - 1, 2) for p in ((i, i + 1), (i + 1, i))])


def swap_on_chip(value):
    peers = lax.axis_size("slab")
    return lax.ppermute(value, "slab", [p for i in range(0, peers, 2) for p in ((i, i + 1), (i + 1, i))])


def body(
    forward_state,
    adjoint_state,
    materials,
    wavelet,
    encoding,
    source_cells,
    receiver_depth,
    receiver_data,
):
    _, comps, own, y_rows, z_rows = forward_state.shape
    shots = lax.axis_size("shot")
    small = pltpu.CompilerParams(vmem_limit_bytes=2 << 20)

    own_rows, far, near = pl.pallas_call(
        edges_kernel,
        out_shape=(
            VMEM((10 * own, z_rows), jnp.float32),
            VMEM((10 * DEPTH, z_rows), jnp.float32),
            VMEM((10 * DEPTH, z_rows), jnp.float32),
        ),
        in_specs=[IN_HBM],
        out_specs=(WHOLE,) * 3,
        scratch_shapes=[pltpu.SemaphoreType.DMA],
        compiler_params=small,
        name="edges",
    )(in_hbm(materials.reshape(10 * own, z_rows)))
    far, near = swap_across(far), swap_on_chip(near)
    copies = pl.pallas_call(
        spread_kernel,
        out_shape=pltpu.HBM((shots, ROWS, z_rows), jnp.float32),
        in_specs=[WHOLE] * 3,
        out_specs=IN_HBM,
        scratch_shapes=[VMEM((ROWS, z_rows), jnp.float32), pltpu.SemaphoreType.DMA((shots,))],
        cost_estimate=estimate(1000, 4 * shots * ROWS * z_rows),
        compiler_params=small,
        name="spread",
    )(in_vmem(own_rows), in_vmem(far), in_vmem(near))
    gathered = lax.all_to_all(copies, "shot", split_axis=0, concat_axis=0, tiled=True)

    z_at = lax.broadcasted_iota(jnp.int32, (own, y_rows, z_rows), 2)
    probe = z_at == receiver_depth[:, :, None]
    data = jnp.where(probe[None], receiver_data[0][:, :, :, None], 0.0)

    payload = VMEM((sizes(True)[2] + STEPS // DEPTH, y_rows, z_rows), jnp.float32)
    whole_state = VMEM((2 * comps, LENGTH, y_rows, z_rows), jnp.float32)
    moved = 8 * comps * own * y_rows * z_rows
    state, cross, chip = pl.pallas_call(
        stage_kernel,
        out_shape=(whole_state, payload, payload),
        in_specs=[IN_HBM, IN_HBM, WHOLE],
        out_specs=(WHOLE,) * 3,
        scratch_shapes=[pltpu.SemaphoreType.DMA((2 * comps,))],
        cost_estimate=estimate(1000, moved),
        compiler_params=small,
        name="stage",
    )(in_hbm(forward_state[0]), in_hbm(adjoint_state[0]), in_vmem(data))
    cross, chip = swap_across(cross), swap_on_chip(chip)
    state = pl.pallas_call(
        join_kernel,
        out_shape=whole_state,
        in_specs=[WHOLE] * 3,
        out_specs=WHOLE,
        input_output_aliases={0: 0},
        cost_estimate=estimate(1000, moved),
        compiler_params=small,
        name="join",
    )(in_vmem(state), in_vmem(cross), in_vmem(chip))

    outs = run_phase(True, (wavelet, encoding, source_cells), state, [gathered], data)
    state, acc, mats, image, cross, chip = outs
    cross, chip = swap_across(cross), swap_on_chip(chip)
    outs = run_phase(False, (wavelet,), state, [acc, cross, chip, mats, image], data)
    state, _, packed = outs

    tiles = lax.all_to_all(packed.reshape(y_rows, 10 * own, z_rows), "shot", 0, 0, tiled=True)
    gradient = jnp.sum(tiles, axis=0).reshape(10, own, 1, z_rows)
    forward_out = state[None, :comps, DEPTH : DEPTH + own]
    adjoint_out = state[None, comps:, DEPTH : DEPTH + own]
    return forward_out, adjoint_out, gradient


def solution(mesh):
    state_spec = P("shot", None, "slab", None, None)
    return jax.shard_map(
        body,
        mesh=mesh,
        in_specs=(
            state_spec,
            state_spec,
            P(None, "slab", "shot", None),
            P(),
            P("shot", None),
            P("shot", None),
            P("slab", None),
            P("shot", None, "slab", None),
        ),
        out_specs=(state_spec, state_spec, P(None, "slab", "shot", None)),
        check_vma=False,
    )
```

time: 111 us -> 98.4 us (0.89)
  starting transfers between devices: 44.7 us -> 33.1 us
  waiting for transfers between devices: 33.6 us -> 44.2 us
  local copies, waits for them, and re-layouts: 11.8 us -> 1.73 us
  other arithmetic: 8.72 us -> 2.31 us
  Pallas kernels: 9.99 us -> 15.7 us
    ppermute x6, waiting for transfers between devices: 11.5 us -> 27.7 us  [the longest x3 27.7 us: swap_across(): lax.ppermute(value, 'slab', [p for i in range(1, peers - 1, 2) for p in (...]
    ppermute x6, starting transfers between devices: 23.3 us -> 14.7 us  [the longest x3 14.5 us: swap_across(): lax.ppermute(value, 'slab', [p for i in range(1, peers - 1, 2) for p in (...]
    pallas_call x2 -> x6, Pallas kernels: 9.99 us -> 15.7 us  [the longest x2 11.2 us: run_phase(): pl.pallas_call(functools.partial(phase_kernel, first, y_rows, z_rows), ou...]
    all_to_all x3 -> x2, waiting for transfers between devices: 22 us -> 16.5 us  [the longest x1 14 us: body(): lax.all_to_all(packed.reshape(y_rows, 10 * own, z_rows), 'shot', 0, 0, ti...]
    unnamed x30 -> x12, local copies, waits for them, and re-layouts: 4.97 us -> 0.03 us
    all_to_all x3 -> x2, starting transfers between devices: 21.4 us -> 18.4 us  [the longest x1 9.37 us: body(): lax.all_to_all(packed.reshape(y_rows, 10 * own, z_rows), 'shot', 0, 0, ti...]
    concatenate x7 -> x0, other arithmetic: 2.62 us -> none  [the longest x1 2.49 us: body(): jnp.concatenate([halo_lo, jnp.concatenate(both, axis=0), halo_hi], axis=1)]
    slice x8 -> x0, local copies, waits for them, and re-layouts: 2.2 us -> none  [the longest x1 1.16 us: body(): part[:, own - k:]]
  transfers between devices with their start and end apart: 9 -> 8, of which waited for: 5 -> 5; matrix products, arithmetic and copies ran while one was open for 9% -> 2% of each run, Pallas kernels for 0% -> 2%
where the time goes in v2:
time: 98.4 us; the launch traced here: 97.9 us
  waiting for transfers between devices  44.2 us (45%)
  starting transfers between devices  33.1 us (34%)
  Pallas kernels  15.7 us (16%)
  other arithmetic  2.31 us (2%)
  local copies, waits for them, and re-layouts  1.73 us (2%)
    ppermute x3, waiting for transfers between devices, swap_across(): lax.ppermute(value, 'slab', [p for i in range(1, peers - 1, 2) for p in (...  27.7 us
    ppermute x3, starting transfers between devices, swap_across(): lax.ppermute(value, 'slab', [p for i in range(1, peers - 1, 2) for p in (...  14.5 us
    all_to_all x1, waiting for transfers between devices, body(): lax.all_to_all(packed.reshape(y_rows, 10 * own, z_rows), 'shot', 0, 0, ti...  14 us
    pallas_call x2, Pallas kernels, run_phase(): pl.pallas_call(functools.partial(phase_kernel, first, y_rows, z_rows), ou...  11.2 us
    all_to_all x1, starting transfers between devices, body(): lax.all_to_all(packed.reshape(y_rows, 10 * own, z_rows), 'shot', 0, 0, ti...  9.37 us
    all_to_all x1, starting transfers between devices, body(): lax.all_to_all(copies, 'shot', split_axis=0, concat_axis=0, tiled=True)  9.04 us
    all_to_all x1, waiting for transfers between devices, body(): lax.all_to_all(copies, 'shot', split_axis=0, concat_axis=0, tiled=True)  2.5 us
    pallas_call x1, Pallas kernels, body(): pl.pallas_call(stage_kernel, out_shape=(whole_state, payload, payload), i...  2.08 us
  transfers between devices with their start and end apart: 8, of which 5 were waited for; matrix products, arithmetic and copies ran while one was open for 2% of the time, Pallas kernels for 2%

profile of v2, /device:TPU:1, one launch (start us, length us, event | category | flops | bytes accessed | tf_op | source)
XLA Modules:
  0.0 97.9 jit_solution(7753739398014362944)
XLA Ops:
  0.6 0.8 edges.1
  1.4 6.0 %collective-permute-start.2 = (f32[20,128]{1,0:T(8,128)S(1)}, f32[20,128]{1,0:T(8,128)S(1)}, u32[]{:S(2)}, u32[]{:S(2)}) collective-permute-start(f32[20,128]{1,0:T(8,128)S(1)} %get-tuple-element.21), channel_id=1, source_target_pairs={{1,2},{2,1},{5,6},{6,5},{9,10},{10,9},{13,14},{14,13},{17,18},{18,... | collective-permute-start | bytes 30728 | tf_op jit(solution)/shard_map/ppermute | solution.py:421
  7.5 0.1 collective-permute-start.3
  7.6 1.3 %collective-permute-done.2.cross = f32[20,128]{1,0:T(8,128)S(1)} collective-permute-done((f32[20,128]{1,0:T(8,128)S(1)}, f32[20,128]{1,0:T(8,128)S(1)}, u32[]{:S(2)}, u32[]{:S(2)}) %collective-permute-start.2) | collective-permute-done | bytes 10272 | tf_op jit(solution)/shard_map/ppermute | solution.py:421
  8.8 0.0 collective-permute-done.3.chip
  8.8 1.5 %spread.1 = f32[32,104,128]{2,1,0:T(8,128)} custom-call(f32[80,128]{1,0:T(8,128)S(1)} %get-tuple-element.20.own, f32[20,128]{1,0:T(8,128)S(1)} %collective-permute-done.2.cross, f32[20,128]{1,0:T(8,128)S(1)} %collective-permute-done.3.chip), custom_call_target="tpu_custom_call" | custom-call | flops 1000 | bytes 1703936 | tf_op jit(solution)/shard_map/spread/pallas_call | solution.py:457
  10.3 0.0 copy-start.5
  10.4 0.0 copy-start.4
  10.4 9.0 %all-to-all-start = ((f32[32,104,128]{2,1,0:T(8,128)}), f32[32,104,128]{2,1,0:T(8,128)}, u32[]{:S(2)}, u32[]{:S(2)}) async-start(f32[32,104,128]{2,1,0:T(8,128)} %spread.1), calls=%async_computation | async-start | bytes 3407872 | tf_op jit(solution)/shard_map/all_to_all | solution.py:467
  19.4 0.0 copy-done.5
  19.4 0.1 iota_compare_fusion
  19.5 0.0 copy-done.4
  19.5 0.2 broadcast_select_fusion.data.refs_5_.refs_7_
  19.7 0.0 copy-start
  19.8 2.1 %stage.1 = (f32[18,12,32,128]{3,2,1,0:T(8,128)S(1)}, f32[36,32,128]{2,1,0:T(8,128)S(1)}, f32[36,32,128]{2,1,0:T(8,128)S(1)}) custom-call(f32[9,8,32,128]{3,2,1,0:T(8,128)} %bitcast.12, f32[9,8,32,128]{3,2,1,0:T(8,128)} %bitcast.13, f32[4,8,32,128]{3,2,1,0:T(8,128)S(1)} %broadcast_select_fusion.data.refs_5_.refs_7_), custom_call_target="tpu_custom_call" | custom-call | flops 1000 | bytes 2359296 | tf_op jit(solution)/shard_map/stage/pallas_call | solution.py:476
  21.9 0.0 copy-done
  21.9 5.2 %collective-permute-start = (f32[36,32,128]{2,1,0:T(8,128)S(1)}, f32[36,32,128]{2,1,0:T(8,128)S(1)}, u32[]{:S(2)}, u32[]{:S(2)}) collective-permute-start(f32[36,32,128]{2,1,0:T(8,128)S(1)} %get-tuple-element.18), channel_id=1, source_target_pairs={{1,2},{2,1},{5,6},{6,5},{9,10},{10,9},{13,14},{14,13},{17,18},{18,... | collective-permute-start | bytes 1769480 | tf_op jit(solution)/shard_map/ppermute | solution.py:421
  27.1 0.1 collective-permute-start.1
  27.2 18.1 %collective-permute-done.cross = f32[36,32,128]{2,1,0:T(8,128)S(1)} collective-permute-done((f32[36,32,128]{2,1,0:T(8,128)S(1)}, f32[36,32,128]{2,1,0:T(8,128)S(1)}, u32[]{:S(2)}, u32[]{:S(2)}) %collective-permute-start) | collective-permute-done | bytes 589856 | tf_op jit(solution)/shard_map/ppermute | solution.py:421
  45.2 0.0 collective-permute-done.1.chip
  45.2 0.0 copy-start.1
  45.2 0.0 copy-start.2
  45.3 0.0 copy-start.3
  45.3 0.1 join.1.refs_3_
  45.4 2.5 %all-to-all-done = f32[32,104,128]{2,1,0:T(8,128)} async-done(((f32[32,104,128]{2,1,0:T(8,128)}), f32[32,104,128]{2,1,0:T(8,128)}, u32[]{:S(2)}, u32[]{:S(2)}) %all-to-all-start) | async-done | bytes 1703968 | tf_op jit(solution)/shard_map/all_to_all | solution.py:467
  47.9 0.0 copy-done.1
  47.9 0.0 copy-done.2
  47.9 0.0 copy-done.3
  47.9 5.8 %phase_first.1 = (f32[18,12,32,128]{3,2,1,0:T(8,128)S(1)}, f32[10,8,32,128]{3,2,1,0:T(8,128)S(1)}, f32[10,12,32,128]{3,2,1,0:T(8,128)S(1)}, f32[12,32,128]{2,1,0...) custom-call(f32[4]{0:T(128)S(1)} %copy-done.1, ...), custom_call_target="tpu_custom_call", output_to_operand_aliasing={{0}: (3, {})} | custom-call | flops 13107200 | bytes 8192000 | tf_op jit(solution)/shard_map/phase_first/pallas_call | solution.py:402
  53.7 3.2 %collective-permute-start.4 = (f32[30,32,128]{2,1,0:T(8,128)S(1)}, f32[30,32,128]{2,1,0:T(8,128)S(1)}, u32[]{:S(2)}, u32[]{:S(2)}) collective-permute-start(f32[30,32,128]{2,1,0:T(8,128)S(1)} %get-tuple-element.25), channel_id=1, source_target_pairs={{1,2},{2,1},{5,6},{6,5},{9,10},{10,9},{13,14},{14,13},{17,18},{18,... | collective-permute-start | bytes 1474568 | tf_op jit(solution)/shard_map/ppermute | solution.py:421
  56.9 0.1 collective-permute-start.5
  57.0 8.3 %collective-permute-done.4.refs_3_ = f32[30,32,128]{2,1,0:T(8,128)S(1)} collective-permute-done((f32[30,32,128]{2,1,0:T(8,128)S(1)}, f32[30,32,128]{2,1,0:T(8,128)S(1)}, u32[]{:S(2)}, u32[]{:S(2)}) %collective-permute-start.4) | collective-permute-done | bytes 491552 | tf_op jit(solution)/shard_map/ppermute | solution.py:421
  65.3 0.0 collective-permute-done.5.refs_4_
  65.3 5.4 %phase_last.1 = (f32[18,12,32,128]{3,2,1,0:T(8,128)S(1)}, f32[10,8,32,128]{3,2,1,0:T(8,128)S(1)}, f32[4,640,128]{2,1,0:T(8,128)}) custom-call(f32[4]{0:T(128)S(1)} %copy-done.1, f32[18,12,32,128]{3,2,1,0:T(8,128)S(1)} %get-tuple-element.23.refs_1_, f32[10,8,32,128]{3,2,1,0:T(8,128)S(1)} %get-tuple-element.24.refs_2_, ...), custom_call_target="tpu_custom_call", output_to_operand_aliasing={{0}: (1, {}), {1}: (2, {})} | custom-call | flops 13107200 | bytes 8192000 | tf_op jit(solution)/shard_map/phase_last/pallas_call | solution.py:402
  70.8 9.4 %all-to-all-start.1 = ((f32[32,80,128]{2,1,0:T(8,128)}), f32[32,80,128]{2,1,0:T(8,128)}, u32[]{:S(2)}, u32[]{:S(2)}) async-start(f32[32,80,128]{2,1,0:T(8,128)} %bitcast.11), calls=%async_computation.1 | async-start | bytes 2621440 | tf_op jit(solution)/shard_map/all_to_all | solution.py:504
  80.2 1.7 %slice_bitcast_fusion = (f32[1,9,8,32,128]{4,3,2,1,0:T(8,128)}, f32[1,9,8,32,128]{4,3,2,1,0:T(8,128)}) fusion(f32[18,12,32,128]{3,2,1,0:T(8,128)S(1)} %get-tuple-element.29), kind=kLoop, calls=%fused_computation | loop fusion | bytes 4718592 | tf_op jit(solution)/shard_map/broadcast_in_dim | solution.py:507
  81.9 14.0 %all-to-all-done.1 = f32[32,80,128]{2,1,0:T(8,128)} async-done(((f32[32,80,128]{2,1,0:T(8,128)}), f32[32,80,128]{2,1,0:T(8,128)}, u32[]{:S(2)}, u32[]{:S(2)}) %all-to-all-start.1) | async-done | bytes 1310752 | tf_op jit(solution)/shard_map/all_to_all | solution.py:504
  95.9 2.0 %reduce_sum.9 = f32[80,128]{1,0:T(8,128)} reduce(f32[32,80,128]{2,1,0:T(8,128)} %all-to-all-done.1, f32[]{:T(128)} %constant.0.clone.1), dimensions={0}, to_apply=%region_0.1 | reduce | flops 317440 | bytes 1351684 | tf_op jit(solution)/shard_map/reduce_sum | solution.py:505
Async XLA Ops:
  1.4 7.4 %collective-permute-start.2 = (f32[20,128]{1,0:T(8,128)S(1)}, f32[20,128]{1,0:T(8,128)S(1)}, u32[]{:S(2)}, u32[]{:S(2)}) collective-permute-start(f32[20,128]{1,0:T(8,128)S(1)} %get-tuple-element.21), channel_id=1, source_target_pairs={{1,2},{2,1},{5,6},{6,5},{9,10},{10,9},{13,14},{14,13},{17,18},{18,... | collective-permute-start | bytes 30728 | tf_op jit(solution)/shard_map/ppermute | solution.py:421
  7.5 1.4 %collective-permute-start.3 = (f32[20,128]{1,0:T(8,128)S(1)}, f32[20,128]{1,0:T(8,128)S(1)}, u32[]{:S(2)}, u32[]{:S(2)}) collective-permute-start(f32[20,128]{1,0:T(8,128)S(1)} %get-tuple-element.22), channel_id=1, source_target_pairs={{0,1},{1,0},{2,3},{3,2},{4,5},{5,4},{6,7},{7,6},{8,9},{9,8},{10,11... | collective-permute-start | bytes 30728 | tf_op jit(solution)/shard_map/ppermute | solution.py:426
  10.3 9.1 %copy-start.5 = (s32[8,32]{1,0:T(8,128)S(1)}, s32[8,32]{1,0:T(8,128)}, u32[]{:S(2)}) copy-start(s32[8,32]{1,0:T(8,128)} %param.14) | copy-start | bytes 3076
  10.4 9.2 %copy-start.4 = (f32[1,4,8,32]{3,2,1,0:T(8,128)S(1)}, f32[1,4,8,32]{3,2,1,0:T(8,128)}, u32[]{:S(2)}) copy-start(f32[1,4,8,32]{3,2,1,0:T(8,128)} %param.15) | copy-start | bytes 12292
  10.4 37.5 %all-to-all-start = ((f32[32,104,128]{2,1,0:T(8,128)}), f32[32,104,128]{2,1,0:T(8,128)}, u32[]{:S(2)}, u32[]{:S(2)}) async-start(f32[32,104,128]{2,1,0:T(8,128)} %spread.1), calls=%async_computation | async-start | bytes 3407872 | tf_op jit(solution)/shard_map/all_to_all | solution.py:467
  19.7 2.1 %copy-start = (f32[4,8,32,128]{3,2,1,0:T(8,128)}, f32[4,8,32,128]{3,2,1,0:T(8,128)S(1)}, u32[]{:S(2)}) copy-start(f32[4,8,32,128]{3,2,1,0:T(8,128)S(1)} %broadcast_select_fusion.data.refs_5_.refs_7_) | copy-start | bytes 1572868
  21.9 23.4 %collective-permute-start = (f32[36,32,128]{2,1,0:T(8,128)S(1)}, f32[36,32,128]{2,1,0:T(8,128)S(1)}, u32[]{:S(2)}, u32[]{:S(2)}) collective-permute-start(f32[36,32,128]{2,1,0:T(8,128)S(1)} %get-tuple-element.18), channel_id=1, source_target_pairs={{1,2},{2,1},{5,6},{6,5},{9,10},{10,9},{13,14},{14,13},{17,18},{18,... | collective-permute-start | bytes 1769480 | tf_op jit(solution)/shard_map/ppermute | solution.py:421
  27.1 18.2 %collective-permute-start.1 = (f32[36,32,128]{2,1,0:T(8,128)S(1)}, f32[36,32,128]{2,1,0:T(8,128)S(1)}, u32[]{:S(2)}, u32[]{:S(2)}) collective-permute-start(f32[36,32,128]{2,1,0:T(8,128)S(1)} %get-tuple-element.19), channel_id=1, source_target_pairs={{0,1},{1,0},{2,3},{3,2},{4,5},{5,4},{6,7},{7,6},{8,9},{9,8},{10,11... | collective-permute-start | bytes 1769480 | tf_op jit(solution)/shard_map/ppermute | solution.py:426
  45.2 2.6 %copy-start.1 = (f32[4]{0:T(128)S(1)}, f32[4]{0:T(128)}, u32[]{:S(2)}) copy-start(f32[4]{0:T(128)} %refs_0_.3) | copy-start | bytes 52
  45.2 2.6 %copy-start.2 = (s32[1,16]{1,0:T(1,128)S(1)}, s32[1,16]{1,0:T(1,128)}, u32[]{:S(2)}) copy-start(s32[1,16]{1,0:T(1,128)} %refs_1_.1) | copy-start | bytes 196
  45.3 2.6 %copy-start.3 = (s32[1,16]{1,0:T(1,128)S(1)}, s32[1,16]{1,0:T(1,128)}, u32[]{:S(2)}) copy-start(s32[1,16]{1,0:T(1,128)} %refs_2_.1) | copy-start | bytes 196
  53.7 11.7 %collective-permute-start.4 = (f32[30,32,128]{2,1,0:T(8,128)S(1)}, f32[30,32,128]{2,1,0:T(8,128)S(1)}, u32[]{:S(2)}, u32[]{:S(2)}) collective-permute-start(f32[30,32,128]{2,1,0:T(8,128)S(1)} %get-tuple-element.25), channel_id=1, source_target_pairs={{1,2},{2,1},{5,6},{6,5},{9,10},{10,9},{13,14},{14,13},{17,18},{18,... | collective-permute-start | bytes 1474568 | tf_op jit(solution)/shard_map/ppermute | solution.py:421
  56.9 8.4 %collective-permute-start.5 = (f32[30,32,128]{2,1,0:T(8,128)S(1)}, f32[30,32,128]{2,1,0:T(8,128)S(1)}, u32[]{:S(2)}, u32[]{:S(2)}) collective-permute-start(f32[30,32,128]{2,1,0:T(8,128)S(1)} %get-tuple-element.26), channel_id=1, source_target_pairs={{0,1},{1,0},{2,3},{3,2},{4,5},{5,4},{6,7},{7,6},{8,9},{9,8},{10,11... | collective-permute-start | bytes 1474568 | tf_op jit(solution)/shard_map/ppermute | solution.py:426
  70.8 25.1 %all-to-all-start.1 = ((f32[32,80,128]{2,1,0:T(8,128)}), f32[32,80,128]{2,1,0:T(8,128)}, u32[]{:S(2)}, u32[]{:S(2)}) async-start(f32[32,80,128]{2,1,0:T(8,128)} %bitcast.11), calls=%async_computation.1 | async-start | bytes 2621440 | tf_op jit(solution)/shard_map/all_to_all | solution.py:504

commit v3 on v2

--- a/solution.py
+++ b/solution.py
@@ -14,7 +14,8 @@
 VX, VY, VZ, SXX, SYY, SZZ, SYZ, SXZ, SXY = range(9)
 step_size = 0.25
 VMEM = pltpu.VMEM
-ROWS = 104
+ROWS = 10 * OWN
+RIM_ROWS = DEPTH + 9
 
 BOTH = (SXX, SXY, SXZ)
 UP = [(VX, OWN - 2), (VY, OWN - 1), (VZ, OWN - 1)]
@@ -80,51 +81,63 @@
         drain(chip, down, OWN, 1)
 
 
-def edges_kernel(materials, own, far, near, sem):
-    copy = pltpu.make_async_copy(materials, own, sem)
+def spread_kernel(materials, out, block, sem, sems):
+    copy = pltpu.make_async_copy(materials, block, sem)
     copy.start()
     copy.wait()
-
-    def take(target, layer):
-        for m in range(10):
-            target[pl.ds(DEPTH * m, DEPTH), :] = own[pl.ds(OWN * m + layer, DEPTH), :]
-
-    @pl.when(is_odd())
-    def _():
-        take(far, OWN - DEPTH)
-        take(near, 0)
-
-    @pl.when(jnp.logical_not(is_odd()))
-    def _():
-        take(far, 0)
-        take(near, OWN - DEPTH)
-
-
-def spread_kernel(own, cross, chip, out, block, sem):
-    block[pl.ds(0, 10 * OWN), :] = own[...]
-    block[pl.ds(10 * OWN, ROWS - 10 * OWN), :] = jnp.zeros((ROWS - 10 * OWN, own.shape[1]), jnp.float32)
-    side = DEPTH + 9
-
-    def put(source, base, inner):
-        block[pl.ds(base, DEPTH), :] = source[pl.ds(0, DEPTH), :]
-        for m in range(9):
-            block[pl.ds(base + DEPTH + m, 1), :] = source[pl.ds(DEPTH * (1 + m) + inner, 1), :]
-
-    @pl.when(is_odd())
-    def _():
-        put(chip, 10 * OWN, DEPTH - 1)
-        put(cross, 10 * OWN + side, 0)
-
-    @pl.when(jnp.logical_not(is_odd()))
-    def _():
-        put(cross, 10 * OWN, DEPTH - 1)
-        put(chip, 10 * OWN + side, 0)
-
-    copies = [pltpu.make_async_copy(block, out.at[j], sem.at[j]) for j in range(out.shape[0])]
+    copies = [pltpu.make_async_copy(block, out.at[j], sems.at[j]) for j in range(out.shape[0])]
     for copy in copies:
         copy.start()
     for copy in copies:
         copy.wait()
+
+
+def turn_kernel(gathered, mats, cross, chip, rows_ref, sems):
+    chunks = gathered.shape[0]
+    copies = [pltpu.make_async_copy(gathered.at[c], rows_ref.at[c], sems.at[c]) for c in range(chunks)]
+    for copy in copies:
+        copy.start()
+    for c in range(chunks):
+        copies[c].wait()
+        for r in range(ROWS):
+            plane = step_size * rows_ref[c, pl.ds(r, 8, stride=ROWS), :]
+            mats[r // OWN, DEPTH + r % OWN, pl.ds(8 * c, 8), :] = plane
+
+    def fill(target, layers):
+        for n, (m, j) in enumerate(rim_planes(layers)):
+            target[n] = mats[m, DEPTH + j]
+
+    @pl.when(is_odd())
+    def _():
+        fill(cross, (OWN - 2, OWN - 1, OWN - 1))
+        fill(chip, (0, 1, 0))
+
+    @pl.when(jnp.logical_not(is_odd()))
+    def _():
+        fill(cross, (0, 1, 0))
+        fill(chip, (OWN - 2, OWN - 1, OWN - 1))
+
+
+def rim_planes(layers):
+    return [(0, layers[0]), (0, layers[1])] + [(m, layers[2]) for m in range(1, 10)]
+
+
+def drain_rims(mats, cross, chip):
+    def drain(source, layers):
+        for n, (m, j) in enumerate(rim_planes(layers)):
+            mats[m, DEPTH + j] = source[n]
+
+    below, above = (-2, -1, -1), (OWN, OWN + 1, OWN)
+
+    @pl.when(is_odd())
+    def _():
+        drain(chip, below)
+        drain(cross, above)
+
+    @pl.when(jnp.logical_not(is_odd()))
+    def _():
+        drain(cross, below)
+        drain(chip, above)
 
 
 def stage_kernel(forward, adjoint, data, state, cross, chip, sems):
@@ -161,12 +174,14 @@
         image[x, pl.ds(y, 1), :] = image[x, pl.ds(y, 1), :] + spot
 
 
-def phase_kernel(first, y_rows, z_rows, *refs):
-    refs = list(refs)
-    if first:
-        wavelet, encoding, cells, _, gathered, data_in, state, acc, mats, image, cross, chip, rows_ref, data, sems = refs
+def phase_kernel(part, y_rows, z_rows, *refs):
+    first = part != "last"
+    if part == "early":
+        wavelet, encoding, cells, _, mats, data_in, state, acc, image, data, sems = refs
+    elif part == "rest":
+        wavelet, _, _, _, cross_in, chip_in, image, data_in, state, acc, mats, cross, chip, data, sems = refs
     else:
-        wavelet, _, _, cross_in, chip_in, mats, image, data_in, state, acc, packed, rows_ref, data, sems = refs
+        wavelet, _, _, cross_in, chip_in, mats, image, data_in, state, acc, packed, data, rows_ref, sems = refs
 
     chunks = y_rows // 8
     scale = float(y_rows * STEPS) ** (-0.5)
@@ -176,36 +191,18 @@
     lane_first, lane_last = lane == 0, lane == z_rows - 1
     nought = jnp.zeros((8, z_rows), jnp.float32)
 
+    start = 0 if first else DEPTH
+    data_copy = pltpu.make_async_copy(data_in.at[pl.ds(start, DEPTH)], data, sems.at[0])
+    data_copy.start()
+    if part == "early":
+        draw_image(encoding, cells, image)
+    elif part == "rest":
+        drain_rims(mats, cross_in, chip_in)
+    else:
+        drain_payloads(False, state, cross_in, chip_in)
+
     def rows_of(c):
         return pl.ds(8 * c, 8)
-
-    if first:
-        copies = [
-            pltpu.make_async_copy(gathered.at[c], rows_ref.at[c], sems.at[c]) for c in range(chunks)
-        ]
-        for copy in copies:
-            copy.start()
-    start = 0 if first else DEPTH
-    data_copy = pltpu.make_async_copy(data_in.at[pl.ds(start, DEPTH)], data, sems.at[chunks])
-    data_copy.start()
-    if not first:
-        drain_payloads(False, state, cross_in, chip_in)
-    if first:
-        draw_image(encoding, cells, image)
-        side = DEPTH + 9
-        for c in range(chunks):
-            copies[c].wait()
-
-            def take(r):
-                return step_size * rows_ref[c, pl.ds(r, 8, stride=ROWS), :]
-
-            for r in range(10 * OWN):
-                mats[r // OWN, DEPTH + r % OWN, rows_of(c), :] = take(r)
-            for base, buoy_at, stiff_at in ((80, 0, DEPTH - 1), (80 + side, DEPTH + OWN, DEPTH + OWN)):
-                for j in range(DEPTH):
-                    mats[0, buoy_at + j, rows_of(c), :] = take(base + j)
-                for m in range(9):
-                    mats[1 + m, stiff_at, rows_of(c), :] = take(base + DEPTH + m)
 
     def at(f, i, c):
         return state[f, i, rows_of(c), :]
@@ -304,60 +301,99 @@
             if not fresh:
                 term = acc[1 + n, slot, rows_of(c), :] + term
             if final:
-                rows_ref[c, pl.ds((1 + n) * OWN + slot, 8, stride=10 * OWN), :] = scale * term
+                rows_ref[pl.ds(10 * slot + 1 + n + 8 * c * ROWS, 8, stride=ROWS), :] = scale * term
             else:
                 acc[1 + n, slot, rows_of(c), :] = term
         if final:
-            rows_ref[c, pl.ds(slot, 8, stride=10 * OWN), :] = scale * acc[0, slot, rows_of(c), :]
-
-    inner, low, high = DEPTH + OWN, DEPTH - 1, DEPTH + OWN
-    for at_step in range(DEPTH):
-        step = at_step if first else DEPTH + at_step
-        fresh = first and at_step == 0
-        final = not first and at_step == DEPTH - 1
+            term = scale * acc[0, slot, rows_of(c), :]
+            rows_ref[pl.ds(10 * slot + 8 * c * ROWS, 8, stride=ROWS), :] = term
+
+    low, high = DEPTH - 1, DEPTH + OWN
+
+    def velocity_own(fresh):
+        def one(x, carry):
+            velocity_plane(DEPTH + x, (0, 1, 2), x, fresh)
+            return carry
+
+        lax.fori_loop(0, OWN, one, 0)
+
+    def stress_own(step, begin, end, fresh=False, final=False):
+        def one(x, carry):
+            for c in range(chunks):
+                stress_chunk(DEPTH + x, c, step, x, fresh, final)
+            return carry
+
+        lax.fori_loop(begin, end, one, 0)
+
+    def velocity_rims(at_step):
         velocity_plane(at_step, (0,))
         if at_step == 0:
             velocity_plane(low, (0, 1, 2))
-
-        def velocity_own(x, carry):
-            velocity_plane(DEPTH + x, (0, 1, 2), x, fresh)
-            return carry
-
-        lax.fori_loop(0, OWN, velocity_own, 0)
-        if at_step == 0:
             velocity_plane(high, (0, 1, 2))
         velocity_plane(LENGTH - 1 - at_step, (1, 2))
-        if at_step == 0:
-            data_copy.wait()
+
+    def stress_rims(step):
+        for c in range(chunks):
+            stress_chunk(low, c, step, rim=0)
+            stress_chunk(high, c, step, rim=1)
+
+    if part == "early":
+        velocity_own(True)
+        data_copy.wait()
+        stress_own(0, 1, OWN - 1, True)
+    elif part == "rest":
+        velocity_rims(0)
+        data_copy.wait()
+        stress_rims(0)
+
+        def ends(x, carry):
+            slot = x * (OWN - 1)
             for c in range(chunks):
-                stress_chunk(low, c, step, rim=0)
-                stress_chunk(high, c, step, rim=1)
-        if not final:
-
-            def stress_own(x, carry):
-                for c in range(chunks):
-                    stress_chunk(DEPTH + x, c, step, x, fresh)
-                return carry
-
-            lax.fori_loop(0, OWN, stress_own, 0)
-            continue
+                stress_chunk(DEPTH + slot, c, 0, slot, True)
+            return carry
+
+        lax.fori_loop(0, 2, ends, 0)
+        velocity_own(False)
+        velocity_rims(1)
+        stress_own(1, 0, OWN)
+        fill_payloads(False, state, cross, chip)
+    else:
+        velocity_own(False)
+        velocity_rims(0)
+        data_copy.wait()
+        stress_rims(DEPTH)
+        stress_own(DEPTH, 0, OWN)
+        velocity_own(False)
+        velocity_rims(1)
         copies = []
-        for c in range(chunks):
-
-            def stress_last(x, carry):
-                for n in range(4):
-                    stress_chunk(DEPTH + 4 * x + n, c, step, 4 * x + n, fresh, True)
-                return carry
-
-            lax.fori_loop(0, OWN // 4, stress_last, 0)
-            copy = pltpu.make_async_copy(rows_ref.at[c], packed.at[c], sems.at[c])
-            copy.start()
-            copies.append(copy)
+        for n in range(2):
+            stress_own(DEPTH + 1, n * OWN // 2, (n + 1) * OWN // 2, False, True)
+            half = pl.ds(n * ROWS // 2, ROWS // 2)
+            whole = rows_ref.reshape(y_rows, ROWS, z_rows)
+            copies.append(pltpu.make_async_copy(whole.at[:, half], packed.at[:, half], sems.at[1 + n]))
+            copies[-1].start()
         for copy in copies:
             copy.wait()
 
-    if first:
-        fill_payloads(False, state, cross, chip)
+
+def sum_kernel(tiles, out, rows_ref, total, sems):
+    parts = tiles.shape[0] // 8
+    copies = [
+        pltpu.make_async_copy(tiles.at[pl.ds(8 * n, 8)], rows_ref.at[pl.ds(8 * n, 8)], sems.at[n])
+        for n in range(parts)
+    ]
+    for copy in copies:
+        copy.start()
+    for n in range(parts):
+        copies[n].wait()
+        for g in range(ROWS // 8):
+            rows = pl.ds(8 * g, 8)
+            values = [rows_ref[8 * n + j, rows, :] for j in range(8)]
+            while len(values) > 1:
+                values = [a + b for a, b in zip(values[::2], values[1::2])]
+            total[rows, :] = values[0] if n == 0 else total[rows, :] + values[0]
+    for m in range(10):
+        out[pl.ds(OWN * m, OWN), :] = total[pl.ds(m, OWN, stride=10), :]
 
 
 def in_vmem(x):
@@ -377,43 +413,38 @@
     return pl.CostEstimate(flops=flops, bytes_accessed=moved, transcendentals=0)
 
 
-def run_phase(first, scalars, state, middle, data):
+def run_phase(part, scalars, state, middle, data):
     y_rows, z_rows = state.shape[2:]
-    chunks = y_rows // 8
+    count = len(scalars)
     outs = [VMEM(state.shape, jnp.float32), VMEM((10, OWN, y_rows, z_rows), jnp.float32)]
-    specs = [SCALARS] * len(scalars) + [WHOLE]
-    aliases = {len(scalars): 0}
-    if first:
-        (gathered,) = middle
-        middle = [in_hbm(gathered.reshape(chunks, 8 * ROWS, z_rows))]
-        specs += [IN_HBM]
-        outs += [VMEM((10, LENGTH, y_rows, z_rows), jnp.float32), VMEM((LENGTH, y_rows, z_rows), jnp.float32)]
-        outs += [VMEM((sizes(False)[2], y_rows, z_rows), jnp.float32)] * 2
-        out_specs = [WHOLE] * len(outs)
-        rows = VMEM((chunks, 8 * ROWS, z_rows), jnp.float32)
+    aliases = {count: 0}
+    scratch = [VMEM((DEPTH, OWN, y_rows, z_rows), jnp.float32)]
+    payload = VMEM((sizes(False)[2], y_rows, z_rows), jnp.float32)
+    out_specs = [WHOLE, WHOLE]
+    if part == "early":
+        outs += [VMEM((LENGTH, y_rows, z_rows), jnp.float32)]
+        out_specs += [WHOLE]
+    elif part == "rest":
+        outs += [VMEM((10, LENGTH, y_rows, z_rows), jnp.float32), payload, payload]
+        aliases.update({count + 1: 1, count + 2: 2})
+        out_specs += [WHOLE] * 3
     else:
-        middle = [in_vmem(x) for x in middle]
-        specs += [WHOLE] * len(middle)
-        aliases[len(scalars) + 1] = 1
-        outs.append(pltpu.HBM((chunks, 8 * 10 * OWN, z_rows), jnp.float32))
-        out_specs = [WHOLE, WHOLE, IN_HBM]
-        rows = VMEM((chunks, 8 * 10 * OWN, z_rows), jnp.float32)
-    cells = (OWN + 2) * y_rows * z_rows * DEPTH
+        outs += [pltpu.HBM((y_rows, ROWS, z_rows), jnp.float32)]
+        aliases.update({count + 1: 1})
+        scratch += [VMEM((y_rows * ROWS, z_rows), jnp.float32)]
+        out_specs += [IN_HBM]
+    cells = (OWN + 2) * y_rows * z_rows * (2 if part == "last" else 1)
     return pl.pallas_call(
-        functools.partial(phase_kernel, first, y_rows, z_rows),
+        functools.partial(phase_kernel, part, y_rows, z_rows),
         out_shape=tuple(outs),
-        in_specs=specs + [IN_HBM],
+        in_specs=[SCALARS] * count + [WHOLE] * (1 + len(middle)) + [IN_HBM],
         out_specs=tuple(out_specs),
-        scratch_shapes=[
-            rows,
-            VMEM((DEPTH, OWN, y_rows, z_rows), jnp.float32),
-            pltpu.SemaphoreType.DMA((chunks + 1,)),
-        ],
+        scratch_shapes=scratch + [pltpu.SemaphoreType.DMA((3,))],
         input_output_aliases=aliases,
         cost_estimate=estimate(160 * cells, 100 * cells),
-        compiler_params=pltpu.CompilerParams(vmem_limit_bytes=6 << 20),
-        name="phase_first" if first else "phase_last",
-    )(*scalars, in_vmem(state), *middle, in_hbm(data))
+        compiler_params=pltpu.CompilerParams(vmem_limit_bytes=4 << 20),
+        name="steps_" + part,
+    )(*scalars, in_vmem(state), *[in_vmem(x) for x in middle], in_hbm(data))
 
 
 def swap_across(value):
@@ -440,30 +471,20 @@
     shots = lax.axis_size("shot")
     small = pltpu.CompilerParams(vmem_limit_bytes=2 << 20)
 
-    own_rows, far, near = pl.pallas_call(
-        edges_kernel,
-        out_shape=(
-            VMEM((10 * own, z_rows), jnp.float32),
-            VMEM((10 * DEPTH, z_rows), jnp.float32),
-            VMEM((10 * DEPTH, z_rows), jnp.float32),
-        ),
-        in_specs=[IN_HBM],
-        out_specs=(WHOLE,) * 3,
-        scratch_shapes=[pltpu.SemaphoreType.DMA],
-        compiler_params=small,
-        name="edges",
-    )(in_hbm(materials.reshape(10 * own, z_rows)))
-    far, near = swap_across(far), swap_on_chip(near)
     copies = pl.pallas_call(
         spread_kernel,
         out_shape=pltpu.HBM((shots, ROWS, z_rows), jnp.float32),
-        in_specs=[WHOLE] * 3,
+        in_specs=[IN_HBM],
         out_specs=IN_HBM,
-        scratch_shapes=[VMEM((ROWS, z_rows), jnp.float32), pltpu.SemaphoreType.DMA((shots,))],
+        scratch_shapes=[
+            VMEM((ROWS, z_rows), jnp.float32),
+            pltpu.SemaphoreType.DMA,
+            pltpu.SemaphoreType.DMA((shots,)),
+        ],
         cost_estimate=estimate(1000, 4 * shots * ROWS * z_rows),
         compiler_params=small,
         name="spread",
-    )(in_vmem(own_rows), in_vmem(far), in_vmem(near))
+    )(in_hbm(materials.reshape(ROWS, z_rows)))
     gathered = lax.all_to_all(copies, "shot", split_axis=0, concat_axis=0, tiled=True)
 
     z_at = lax.broadcasted_iota(jnp.int32, (own, y_rows, z_rows), 2)
@@ -495,14 +516,44 @@
         name="join",
     )(in_vmem(state), in_vmem(cross), in_vmem(chip))
 
-    outs = run_phase(True, (wavelet, encoding, source_cells), state, [gathered], data)
-    state, acc, mats, image, cross, chip = outs
+    chunks = y_rows // 8
+    rim = VMEM((RIM_ROWS, y_rows, z_rows), jnp.float32)
+    mats, far, near = pl.pallas_call(
+        turn_kernel,
+        out_shape=(VMEM((10, LENGTH, y_rows, z_rows), jnp.float32), rim, rim),
+        in_specs=[IN_HBM],
+        out_specs=(WHOLE,) * 3,
+        scratch_shapes=[
+            VMEM((chunks, 8 * ROWS, z_rows), jnp.float32),
+            pltpu.SemaphoreType.DMA((chunks,)),
+        ],
+        cost_estimate=estimate(1000, 8 * shots * ROWS * z_rows),
+        compiler_params=pltpu.CompilerParams(vmem_limit_bytes=4 << 20),
+        name="turn",
+    )(in_hbm(gathered.reshape(chunks, 8 * ROWS, z_rows)))
+    far, near = swap_across(far), swap_on_chip(near)
+    state, acc, image = run_phase("early", (wavelet, encoding, source_cells), state, [mats], data)
+    outs = run_phase("rest", (wavelet,), state, [acc, mats, far, near, image], data)
+    state, acc, mats, cross, chip = outs
     cross, chip = swap_across(cross), swap_on_chip(chip)
-    outs = run_phase(False, (wavelet,), state, [acc, cross, chip, mats, image], data)
-    state, _, packed = outs
-
-    tiles = lax.all_to_all(packed.reshape(y_rows, 10 * own, z_rows), "shot", 0, 0, tiled=True)
-    gradient = jnp.sum(tiles, axis=0).reshape(10, own, 1, z_rows)
+    state, _, packed = run_phase("last", (wavelet,), state, [acc, cross, chip, mats, image], data)
+
+    tiles = lax.all_to_all(packed, "shot", 0, 0, tiled=True)
+    gradient = pl.pallas_call(
+        sum_kernel,
+        out_shape=jax.ShapeDtypeStruct((ROWS, z_rows), jnp.float32),
+        in_specs=[IN_HBM],
+        out_specs=WHOLE,
+        scratch_shapes=[
+            VMEM((shots, ROWS, z_rows), jnp.float32),
+            VMEM((ROWS, z_rows), jnp.float32),
+            pltpu.SemaphoreType.DMA((shots // 8,)),
+        ],
+        cost_estimate=estimate(shots * ROWS * z_rows, 4 * shots * ROWS * z_rows),
+        compiler_params=pltpu.CompilerParams(vmem_limit_bytes=4 << 20),
+        name="sum",
+    )(in_hbm(tiles))
+    gradient = gradient.reshape(10, own, 1, z_rows)
     forward_out = state[None, :comps, DEPTH : DEPTH + own]
     adjoint_out = state[None, comps:, DEPTH : DEPTH + own]
     return forward_out, adjoint_out, gradient

time: 98.4 us -> 85.7 us (0.87)
  waiting for transfers between devices: 44.2 us -> 29.8 us
  Pallas kernels: 15.7 us -> 21.3 us
  other arithmetic: 2.31 us -> 0.3 us
  starting transfers between devices: 33.1 us -> 31.1 us
    ppermute x3, waiting for transfers between devices: 27.7 us -> 6.96 us  [swap_across(): lax.ppermute(value, 'slab', [p for i in range(1, peers - 1, 2) for p in (...]
    all_to_all x1, waiting for transfers between devices: 2.5 us -> 9.57 us  [body(): lax.all_to_all(copies, 'shot', split_axis=0, concat_axis=0, tiled=True)]
    all_to_all x1, starting transfers between devices: 9.37 us -> 5.09 us  [body(): tiles = lax.all_to_all(packed, 'shot', 0, 0, tiled=True)]
    pallas_call x3 -> x5, Pallas kernels: 12 us -> 14.7 us  [the longest x3 11.3 us: run_phase(): pl.pallas_call(functools.partial(phase_kernel, part, y_rows, z_rows), out...]
    reduce_sum x1 -> x0, other arithmetic: 2.01 us -> none  [body(): gradient = jnp.sum(tiles, axis=0).reshape(10, own, 1, z_rows)]
    ppermute x3, starting transfers between devices: 14.5 us -> 15.9 us  [swap_across(): lax.ppermute(value, 'slab', [p for i in range(1, peers - 1, 2) for p in (...]
    pallas_call x1, Pallas kernels: 0.08 us -> 1.32 us  [body(): pl.pallas_call(join_kernel, out_shape=whole_state, in_specs=[WHOLE] * 3,...]
    pallas_call x1, Pallas kernels: 2.08 us -> 3.09 us  [body(): pl.pallas_call(stage_kernel, out_shape=(whole_state, payload, payload), i...]
  transfers between devices with their start and end apart: 8 -> 8, of which waited for: 5 -> 3; matrix products, arithmetic and copies ran while one was open for 2% -> 2% of each run, Pallas kernels for 2% -> 10%
where the time goes in v3:
time: 85.7 us; the launch traced here: 85.1 us
  starting transfers between devices  31.1 us (36%)
  waiting for transfers between devices  29.8 us (35%)
  Pallas kernels  21.3 us (25%)
  local copies, waits for them, and re-layouts  1.75 us (2%)
  between operations  0.89 us (1%)
    ppermute x3, starting transfers between devices, swap_across(): lax.ppermute(value, 'slab', [p for i in range(1, peers - 1, 2) for p in (...  15.9 us
    all_to_all x1, waiting for transfers between devices, body(): tiles = lax.all_to_all(packed, 'shot', 0, 0, tiled=True)  13.2 us
    pallas_call x3, Pallas kernels, run_phase(): pl.pallas_call(functools.partial(phase_kernel, part, y_rows, z_rows), out...  11.3 us
    all_to_all x1, starting transfers between devices, body(): lax.all_to_all(copies, 'shot', split_axis=0, concat_axis=0, tiled=True)  9.93 us
    all_to_all x1, waiting for transfers between devices, body(): lax.all_to_all(copies, 'shot', split_axis=0, concat_axis=0, tiled=True)  9.57 us
    ppermute x3, waiting for transfers between devices, swap_across(): lax.ppermute(value, 'slab', [p for i in range(1, peers - 1, 2) for p in (...  6.96 us
    all_to_all x1, starting transfers between devices, body(): tiles = lax.all_to_all(packed, 'shot', 0, 0, tiled=True)  5.09 us
    pallas_call x1, Pallas kernels, body(): pl.pallas_call(stage_kernel, out_shape=(whole_state, payload, payload), i...  3.09 us
  transfers between devices with their start and end apart: 8, of which 3 were waited for; matrix products, arithmetic and copies ran while one was open for 2% of the time, Pallas kernels for 10%

profile of v3, /device:TPU:1, one launch (start us, length us, event | category | flops | bytes accessed | tf_op | source)
XLA Modules:
  0.0 85.1 jit_solution(14760199275523495483)
XLA Ops:
  0.6 2.1 %spread.1 = f32[32,80,128]{2,1,0:T(8,128)} custom-call(f32[80,128]{1,0:T(8,128)} %bitcast.14), custom_call_target="tpu_custom_call" | custom-call | flops 1000 | bytes 1310720 | tf_op jit(solution)/shard_map/spread/pallas_call | solution.py:474
  2.8 0.0 copy-start.5
  2.8 0.0 copy-start.4
  2.8 9.9 %all-to-all-start = ((f32[32,80,128]{2,1,0:T(8,128)}), f32[32,80,128]{2,1,0:T(8,128)}, u32[]{:S(2)}, u32[]{:S(2)}) async-start(f32[32,80,128]{2,1,0:T(8,128)} %spread.1), calls=%async_computation | async-start | bytes 2621440 | tf_op jit(solution)/shard_map/all_to_all | solution.py:488
  12.7 0.0 copy-done.5
  12.7 0.1 iota_compare_fusion
  12.8 0.0 copy-done.4
  12.9 0.2 broadcast_select_fusion.data.refs_5_.refs_7_
  13.1 0.0 copy-start
  13.1 3.1 %stage.1 = (f32[18,12,32,128]{3,2,1,0:T(8,128)S(1)}, f32[36,32,128]{2,1,0:T(8,128)}, f32[36,32,128]{2,1,0:T(8,128)}) custom-call(f32[9,8,32,128]{3,2,1,0:T(8,128)} %bitcast.12, f32[9,8,32,128]{3,2,1,0:T(8,128)} %bitcast.13, f32[4,8,32,128]{3,2,1,0:T(8,128)S(1)} %broadcast_select_fusion.data.refs_5_.refs_7_), custom_call_target="tpu_custom_call" | custom-call | flops 1000 | bytes 2359296 | tf_op jit(solution)/shard_map/stage/pallas_call | solution.py:497
  16.2 0.0 copy-done
  16.2 5.2 %collective-permute-start = (f32[36,32,128]{2,1,0:T(8,128)}, f32[36,32,128]{2,1,0:T(8,128)}, u32[]{:S(2)}, u32[]{:S(2)}) collective-permute-start(f32[36,32,128]{2,1,0:T(8,128)} %get-tuple-element.20), channel_id=1, source_target_pairs={{1,2},{2,1},{5,6},{6,5},{9,10},{10,9},{13,14},{14,13},{17,18},{18,... | collective-permute-start | bytes 1769480 | tf_op jit(solution)/shard_map/ppermute | solution.py:452
  21.4 0.1 collective-permute-start.1
  21.5 9.6 %all-to-all-done = f32[32,80,128]{2,1,0:T(8,128)} async-done(((f32[32,80,128]{2,1,0:T(8,128)}), f32[32,80,128]{2,1,0:T(8,128)}, u32[]{:S(2)}, u32[]{:S(2)}) %all-to-all-start) | async-done | bytes 1310752 | tf_op jit(solution)/shard_map/all_to_all | solution.py:488
  31.1 1.5 %turn.1 = (f32[10,12,32,128]{3,2,1,0:T(8,128)S(1)}, f32[11,32,128]{2,1,0:T(8,128)S(1)}, f32[11,32,128]{2,1,0:T(8,128)S(1)}) custom-call(f32[4,640,128]{2,1,0:T(8,128)} %bitcast.4.gathered), custom_call_target="tpu_custom_call" | custom-call | flops 1000 | bytes 2621440 | tf_op jit(solution)/shard_map/turn/pallas_call | solution.py:521
  32.6 6.1 %collective-permute-start.2 = (f32[11,32,128]{2,1,0:T(8,128)S(1)}, f32[11,32,128]{2,1,0:T(8,128)S(1)}, u32[]{:S(2)}, u32[]{:S(2)}) collective-permute-start(f32[11,32,128]{2,1,0:T(8,128)S(1)} %get-tuple-element.25), channel_id=1, source_target_pairs={{1,2},{2,1},{5,6},{6,5},{9,10},{10,9},{13,14},{14,13},{17,18},{18,... | collective-permute-start | bytes 540680 | tf_op jit(solution)/shard_map/ppermute | solution.py:452
  38.6 0.1 collective-permute-start.3
  38.7 0.0 collective-permute-done.cross
  38.7 0.0 collective-permute-done.1.chip
  38.7 0.0 copy-start.1
  38.8 0.0 copy-start.2
  38.8 0.0 copy-start.3
  38.8 1.3 %join.1.refs_3_ = f32[18,12,32,128]{3,2,1,0:T(8,128)S(1)} custom-call(f32[18,12,32,128]{3,2,1,0:T(8,128)S(1)} %get-tuple-element.19.state_in, f32[36,32,128]{2,1,0:T(8,128)} %collective-permute-done.cross, f32[36,32,128]{2,1,0:T(8,128)} %collective-permute-done.1.chip), custom_call_target="tpu_custom_call", output_to_operand_aliasing={{}: (0, {})} | custom-call | flops 1000 | bytes 2359296 | tf_op jit(solution)/shard_map/join/pallas_call | solution.py:508
  40.1 0.0 copy-done.1
  40.1 0.0 copy-done.2
  40.1 0.0 copy-done.3
  40.1 2.2 %steps_early.1 = (f32[18,12,32,128]{3,2,1,0:T(8,128)S(1)}, f32[10,8,32,128]{3,2,1,0:T(8,128)S(1)}, f32[12,32,128]{2,1,0:T(8,128)S(1)}) custom-call(f32[4]{0:T(128)S(1)} %copy-done.1, s32[1,16]{1,0:T(1,128)S(1)} %copy-done.2, s32[1,16]{1,0:T(1,128)S(1)} %copy-done.3, f32[18,12,32,128]{3,2,1,0:T(8,128)S(1)} %join.1.refs_3_, ...), custom_call_target="tpu_custom_call", output_to_operand_aliasing={{0}: (3, {})} | custom-call | flops 6553600 | bytes 4096000 | tf_op jit(solution)/shard_map/steps_early/pallas_call | solution.py:437
  42.3 0.0 collective-permute-done.2.refs_4_
  42.3 0.0 collective-permute-done.3.refs_5_
  42.3 3.7 %steps_rest.1 = (f32[18,12,32,128]{3,2,1,0:T(8,128)S(1)}, f32[10,8,32,128]{3,2,1,0:T(8,128)S(1)}, f32[10,12,32,128]{3,2,1,0:T(8,128)S(1)}, f32[30,32,128]{2,1,0:T(8,128)S(1)}, f32[30,32,128]{2,1,0:T(8,128)S(1)}) custom-call(f32[4]{0:T(128)S(1)} %copy-done.1, ...), custom_call_target="tpu_custom_call", output_to_operand_aliasing={{0}: (1, {}), {1}: (2, {}), {2}: (3, {})} | custom-call | flops 6553600 | bytes 4096000 | tf_op jit(solution)/shard_map/steps_rest/pallas_call | solution.py:437
  46.0 4.6 %collective-permute-start.4 = (f32[30,32,128]{2,1,0:T(8,128)S(1)}, f32[30,32,128]{2,1,0:T(8,128)S(1)}, u32[]{:S(2)}, u32[]{:S(2)}) collective-permute-start(f32[30,32,128]{2,1,0:T(8,128)S(1)} %get-tuple-element.30), channel_id=1, source_target_pairs={{1,2},{2,1},{5,6},{6,5},{9,10},{10,9},{13,14},{14,13},{17,18},{18,... | collective-permute-start | bytes 1474568 | tf_op jit(solution)/shard_map/ppermute | solution.py:452
  50.6 0.1 collective-permute-start.5
  50.7 7.0 %collective-permute-done.4.refs_3_ = f32[30,32,128]{2,1,0:T(8,128)S(1)} collective-permute-done((f32[30,32,128]{2,1,0:T(8,128)S(1)}, f32[30,32,128]{2,1,0:T(8,128)S(1)}, u32[]{:S(2)}, u32[]{:S(2)}) %collective-permute-start.4) | collective-permute-done | bytes 491552 | tf_op jit(solution)/shard_map/ppermute | solution.py:452
  57.7 0.0 collective-permute-done.5.refs_4_
  57.7 5.4 %steps_last.1 = (f32[18,12,32,128]{3,2,1,0:T(8,128)S(1)}, f32[10,8,32,128]{3,2,1,0:T(8,128)S(1)}, f32[32,80,128]{2,1,0:T(8,128)}) custom-call(f32[4]{0:T(128)S(1)} %copy-done.1, f32[18,12,32,128]{3,2,1,0:T(8,128)S(1)} %get-tuple-element.28.refs_1_, f32[10,8,32,128]{3,2,1,0:T(8,128)S(1)} %get-tuple-element.29.refs_2_, ...), custom_call_target="tpu_custom_call", output_to_operand_aliasing={{0}: (1, {}), {1}: (2, {})} | custom-call | flops 13107200 | bytes 8192000 | tf_op jit(solution)/shard_map/steps_last/pallas_call | solution.py:437
  63.1 5.1 %all-to-all-start.1 = ((f32[32,80,128]{2,1,0:T(8,128)}), f32[32,80,128]{2,1,0:T(8,128)}, u32[]{:S(2)}, u32[]{:S(2)}) async-start(f32[32,80,128]{2,1,0:T(8,128)} %get-tuple-element.34), calls=%async_computation.1 | async-start | bytes 2621440 | tf_op jit(solution)/shard_map/all_to_all | solution.py:541
  68.2 1.7 %slice_bitcast_fusion = (f32[1,9,8,32,128]{4,3,2,1,0:T(8,128)}, f32[1,9,8,32,128]{4,3,2,1,0:T(8,128)}) fusion(f32[18,12,32,128]{3,2,1,0:T(8,128)S(1)} %get-tuple-element.33), kind=kLoop, calls=%fused_computation | loop fusion | bytes 4718592 | tf_op jit(solution)/shard_map/broadcast_in_dim | solution.py:558
  69.9 13.2 %all-to-all-done.1.tiles = f32[32,80,128]{2,1,0:T(8,128)} async-done(((f32[32,80,128]{2,1,0:T(8,128)}), f32[32,80,128]{2,1,0:T(8,128)}, u32[]{:S(2)}, u32[]{:S(2)}) %all-to-all-start.1) | async-done | bytes 1310752 | tf_op jit(solution)/shard_map/all_to_all | solution.py:541
  83.2 1.9 %sum.1 = f32[80,128]{1,0:T(8,128)} custom-call(f32[32,80,128]{2,1,0:T(8,128)} %all-to-all-done.1.tiles), custom_call_target="tpu_custom_call" | custom-call | flops 327680 | bytes 1310720 | tf_op jit(solution)/shard_map/sum/pallas_call | solution.py:542
Async XLA Ops:
  2.8 10.0 %copy-start.5 = (s32[8,32]{1,0:T(8,128)S(1)}, s32[8,32]{1,0:T(8,128)}, u32[]{:S(2)}) copy-start(s32[8,32]{1,0:T(8,128)} %param.14) | copy-start | bytes 3076
  2.8 10.1 %copy-start.4 = (f32[1,4,8,32]{3,2,1,0:T(8,128)S(1)}, f32[1,4,8,32]{3,2,1,0:T(8,128)}, u32[]{:S(2)}) copy-start(f32[1,4,8,32]{3,2,1,0:T(8,128)} %param.15) | copy-start | bytes 12292
  2.8 28.3 %all-to-all-start = ((f32[32,80,128]{2,1,0:T(8,128)}), f32[32,80,128]{2,1,0:T(8,128)}, u32[]{:S(2)}, u32[]{:S(2)}) async-start(f32[32,80,128]{2,1,0:T(8,128)} %spread.1), calls=%async_computation | async-start | bytes 2621440 | tf_op jit(solution)/shard_map/all_to_all | solution.py:488
  13.1 3.1 %copy-start = (f32[4,8,32,128]{3,2,1,0:T(8,128)}, f32[4,8,32,128]{3,2,1,0:T(8,128)S(1)}, u32[]{:S(2)}) copy-start(f32[4,8,32,128]{3,2,1,0:T(8,128)S(1)} %broadcast_select_fusion.data.refs_5_.refs_7_) | copy-start | bytes 1572868
  16.2 22.5 %collective-permute-start = (f32[36,32,128]{2,1,0:T(8,128)}, f32[36,32,128]{2,1,0:T(8,128)}, u32[]{:S(2)}, u32[]{:S(2)}) collective-permute-start(f32[36,32,128]{2,1,0:T(8,128)} %get-tuple-element.20), channel_id=1, source_target_pairs={{1,2},{2,1},{5,6},{6,5},{9,10},{10,9},{13,14},{14,13},{17,18},{18,... | collective-permute-start | bytes 1769480 | tf_op jit(solution)/shard_map/ppermute | solution.py:452
  21.4 17.4 %collective-permute-start.1 = (f32[36,32,128]{2,1,0:T(8,128)}, f32[36,32,128]{2,1,0:T(8,128)}, u32[]{:S(2)}, u32[]{:S(2)}) collective-permute-start(f32[36,32,128]{2,1,0:T(8,128)} %get-tuple-element.21), channel_id=1, source_target_pairs={{0,1},{1,0},{2,3},{3,2},{4,5},{5,4},{6,7},{7,6},{8,9},{9,8},{10,11... | collective-permute-start | bytes 1769480 | tf_op jit(solution)/shard_map/ppermute | solution.py:457
  32.6 9.8 %collective-permute-start.2 = (f32[11,32,128]{2,1,0:T(8,128)S(1)}, f32[11,32,128]{2,1,0:T(8,128)S(1)}, u32[]{:S(2)}, u32[]{:S(2)}) collective-permute-start(f32[11,32,128]{2,1,0:T(8,128)S(1)} %get-tuple-element.25), channel_id=1, source_target_pairs={{1,2},{2,1},{5,6},{6,5},{9,10},{10,9},{13,14},{14,13},{17,18},{18,... | collective-permute-start | bytes 540680 | tf_op jit(solution)/shard_map/ppermute | solution.py:452
  38.6 3.7 %collective-permute-start.3 = (f32[11,32,128]{2,1,0:T(8,128)S(1)}, f32[11,32,128]{2,1,0:T(8,128)S(1)}, u32[]{:S(2)}, u32[]{:S(2)}) collective-permute-start(f32[11,32,128]{2,1,0:T(8,128)S(1)} %get-tuple-element.26), channel_id=1, source_target_pairs={{0,1},{1,0},{2,3},{3,2},{4,5},{5,4},{6,7},{7,6},{8,9},{9,8},{10,11... | collective-permute-start | bytes 540680 | tf_op jit(solution)/shard_map/ppermute | solution.py:457
  38.7 1.4 %copy-start.1 = (f32[4]{0:T(128)S(1)}, f32[4]{0:T(128)}, u32[]{:S(2)}) copy-start(f32[4]{0:T(128)} %refs_0_.5) | copy-start | bytes 52
  38.8 1.4 %copy-start.2 = (s32[1,16]{1,0:T(1,128)S(1)}, s32[1,16]{1,0:T(1,128)}, u32[]{:S(2)}) copy-start(s32[1,16]{1,0:T(1,128)} %refs_1_.1) | copy-start | bytes 196
  38.8 1.4 %copy-start.3 = (s32[1,16]{1,0:T(1,128)S(1)}, s32[1,16]{1,0:T(1,128)}, u32[]{:S(2)}) copy-start(s32[1,16]{1,0:T(1,128)} %refs_2_.1) | copy-start | bytes 196
  46.0 11.7 %collective-permute-start.4 = (f32[30,32,128]{2,1,0:T(8,128)S(1)}, f32[30,32,128]{2,1,0:T(8,128)S(1)}, u32[]{:S(2)}, u32[]{:S(2)}) collective-permute-start(f32[30,32,128]{2,1,0:T(8,128)S(1)} %get-tuple-element.30), channel_id=1, source_target_pairs={{1,2},{2,1},{5,6},{6,5},{9,10},{10,9},{13,14},{14,13},{17,18},{18,... | collective-permute-start | bytes 1474568 | tf_op jit(solution)/shard_map/ppermute | solution.py:452
  50.6 7.0 %collective-permute-start.5 = (f32[30,32,128]{2,1,0:T(8,128)S(1)}, f32[30,32,128]{2,1,0:T(8,128)S(1)}, u32[]{:S(2)}, u32[]{:S(2)}) collective-permute-start(f32[30,32,128]{2,1,0:T(8,128)S(1)} %get-tuple-element.31), channel_id=1, source_target_pairs={{0,1},{1,0},{2,3},{3,2},{4,5},{5,4},{6,7},{7,6},{8,9},{9,8},{10,11... | collective-permute-start | bytes 1474568 | tf_op jit(solution)/shard_map/ppermute | solution.py:457
  63.1 20.1 %all-to-all-start.1 = ((f32[32,80,128]{2,1,0:T(8,128)}), f32[32,80,128]{2,1,0:T(8,128)}, u32[]{:S(2)}, u32[]{:S(2)}) async-start(f32[32,80,128]{2,1,0:T(8,128)} %get-tuple-element.34), calls=%async_computation.1 | async-start | bytes 2621440 | tf_op jit(solution)/shard_map/all_to_all | solution.py:541

commit v4 on v3

v4 whole, which is shorter than its diff:
```python
import functools

import jax
import jax.numpy as jnp
from jax import lax
from jax.experimental import pallas as pl
from jax.experimental.pallas import tpu as pltpu
from jax.sharding import PartitionSpec as P

STEPS = 4
DEPTH = STEPS
OWN = 8
LENGTH = OWN + 2 * DEPTH
VX, VY, VZ, SXX, SYY, SZZ, SYZ, SXZ, SXY = range(9)
step_size = 0.25
VMEM = pltpu.VMEM
ROWS = 10 * OWN

UP = [(f, OWN - n, n) for f, n in enumerate((4, 3, 3, 4, 3, 3, 3, 4, 4))]
DOWN = [(f, 0, n) for f, n in enumerate((3, 4, 4, 4, 4, 4, 4, 4, 4))]
RIM_SLOTS = [(t, k) for t in range(STEPS - 1) for k in range(DEPTH - 1 - t)]
RIM_BASE = [0, 3, 5]
RECEIVER_CELLS = 4
PAYLOAD = 2 * sum(n for _, _, n in DOWN) + 1
HALO_COPIES = 4 * len(UP) + 2
RIM_PLANES = DEPTH + 9 * (DEPTH - 1)


def is_odd():
    return lax.rem(lax.axis_index("slab"), 2) == 1


def pieces(planes):
    place, out = 0, []
    for s in range(2):
        for f, first, n in planes:
            out.append((9 * s + f, first, n, place))
            place += n
    return out


def by_parity(odd, even):
    pl.when(is_odd())(odd)
    pl.when(jnp.logical_not(is_odd()))(even)


def spread_kernel(materials, out, block, sem, sems):
    copy = pltpu.make_async_copy(materials, block, sem)
    copy.start()
    copy.wait()
    copies = [pltpu.make_async_copy(block, out.at[j], sems.at[j]) for j in range(out.shape[0])]
    for copy in copies:
        copy.start()
    for copy in copies:
        copy.wait()


def turn_kernel(gathered, forward, adjoint, mats, cross, chip, state, rows_ref, sems):
    chunks = gathered.shape[0]
    copies = [pltpu.make_async_copy(gathered.at[c], rows_ref.at[c], sems.at[c]) for c in range(chunks)]
    for copy in copies:
        copy.start()
    for c in range(chunks):
        copies[c].wait()
        for r in range(ROWS):
            plane = step_size * rows_ref[c, pl.ds(r, 8, stride=ROWS), :]
            mats[r // OWN, DEPTH + r % OWN, pl.ds(8 * c, 8), :] = plane

    copies = [
        pltpu.make_async_copy(part.at[f], state.at[9 * s + f, pl.ds(DEPTH, OWN)], sems.at[chunks + 9 * s + f])
        for s, part in enumerate((forward, adjoint))
        for f in range(9)
    ]
    for copy in copies:
        copy.start()

    def fill(target, upward):
        for n, (m, j) in enumerate(rim_planes()):
            target[n] = mats[m, DEPTH + (OWN - 1 - j if upward else j)]

    def odd():
        fill(cross, True)
        fill(chip, False)

    def even():
        fill(cross, False)
        fill(chip, True)

    by_parity(odd, even)
    for copy in copies:
        copy.wait()


def rim_planes():
    return [(0, j) for j in range(DEPTH)] + [(m, j) for m in range(1, 10) for j in range(DEPTH - 1)]


def drain_rims(mats, cross, chip):
    def drain(source, below):
        for n, (m, j) in enumerate(rim_planes()):
            mats[m, DEPTH - 1 - j if below else DEPTH + OWN + j] = source[n]

    def odd():
        drain(chip, True)
        drain(cross, False)

    def even():
        drain(cross, True)
        drain(chip, False)

    by_parity(odd, even)


def stage_kernel(forward, adjoint, data, cross, chip, own, lines, sems):
    z_rows = data.shape[-1]
    fields = [
        pltpu.make_async_copy(part.at[f], own.at[9 * s + f], sems.at[9 * s + f])
        for s, part in enumerate((forward, adjoint))
        for f in range(9)
    ]
    for copy in fields:
        copy.start()
    for at, upward in enumerate((True, False)):
        line = jnp.zeros(data.shape[2:], jnp.float32)
        for n, (t, k) in enumerate(RIM_SLOTS):
            plane = data[t, OWN - 1 - k if upward else k]
            line = line + (pltpu.roll(plane, RECEIVER_CELLS * n, 1) if n else plane)
        lines[at] = line
    for copy in fields:
        copy.wait()

    def send(target, at, planes):
        copies = [(own.at[f, pl.ds(first, n)], target.at[pl.ds(place, n)]) for f, first, n, place in pieces(planes)]
        copies.append((lines.at[at], target.at[PAYLOAD - 1]))
        return copies

    def run(copies):
        copies = [pltpu.make_async_copy(a, b, sems.at[n]) for n, (a, b) in enumerate(copies)]
        for copy in copies:
            copy.start()
        for copy in copies:
            copy.wait()

    by_parity(
        lambda: run(send(cross, 0, UP) + send(chip, 1, DOWN)),
        lambda: run(send(cross, 1, DOWN) + send(chip, 0, UP)),
    )


def halo_copies(state, lines, below, above, sems):
    out = []
    for source, planes, shift, at in ((below, UP, DEPTH - OWN, 0), (above, DOWN, DEPTH + OWN, 1)):
        pairs = [
            (source.at[pl.ds(place, n)], state.at[f, pl.ds(first + shift, n)]) for f, first, n, place in pieces(planes)
        ]
        pairs.append((source.at[PAYLOAD - 1], lines.at[at]))
        for a, b in pairs:
            out.append(pltpu.make_async_copy(a, b, sems.at[len(out)]))
    return out


def draw_image(encoding, cells, image):
    layers, y_rows, z_rows = image.shape
    image[...] = jnp.zeros(image.shape, jnp.float32)
    lane = lax.broadcasted_iota(jnp.int32, (1, z_rows), 1)
    first_x = lax.axis_index("slab") * OWN - DEPTH
    for n in range(cells.shape[1]):
        cell = cells[0, n]
        x = cell // (y_rows * z_rows) - first_x
        inside = jnp.logical_and(x >= 0, x < layers)
        x = jnp.where(inside, x, 0)
        y = lax.rem(cell // z_rows, y_rows)
        sign = jnp.where(inside, 2 * encoding[0, n] - 1, 0).astype(jnp.float32)
        spot = jnp.where(lane == lax.rem(cell, z_rows), sign, 0.0)
        image[x, pl.ds(y, 1), :] = image[x, pl.ds(y, 1), :] + spot


def phase_kernel(part, y_rows, z_rows, *refs):
    if part == "early":
        wavelet, encoding, cells, _, mats, cross_in, chip_in, data_in, *refs = refs
        state, acc, image, rim_data, data, lines, sems = refs
    else:
        wavelet, _, _, _, cross_in, chip_in, image, rim_data, data, state, acc, mats, forward, adjoint, packed, rows_ref, final_state, sems = refs

    chunks = y_rows // 8
    scale = float(y_rows * STEPS) ** (-0.5)
    row = lax.broadcasted_iota(jnp.int32, (8, z_rows), 0)
    lane = lax.broadcasted_iota(jnp.int32, (8, z_rows), 1)
    row_first, row_last = row == 0, row == 7
    lane_first, lane_last = lane == 0, lane == z_rows - 1
    nought = jnp.zeros((8, z_rows), jnp.float32)

    def rows_of(c):
        return pl.ds(8 * c, 8)

    def at(f, i, c):
        return state[f, i, rows_of(c), :]

    def up_y(f, i, c, a):
        b = at(f, i, c + 1) if c + 1 < chunks else nought
        return pltpu.roll(jnp.where(row_first, b, a), 7, 0) - a

    def down_y(f, i, c, a):
        b = at(f, i, c - 1) if c > 0 else nought
        return a - pltpu.roll(jnp.where(row_last, b, a), 1, 0)

    def up_z(a):
        return pltpu.roll(jnp.where(lane_first, 0.0, a), z_rows - 1, 1) - a

    def down_z(a):
        return a - pltpu.roll(jnp.where(lane_last, 0.0, a), 1, 1)

    def force(s, i, c, which):
        sxy, sxz = at(s + SXY, i, c), at(s + SXZ, i, c)
        out = [None] * 3
        if 0 in which:
            up_x = at(s + SXX, i + 1, c) - at(s + SXX, i, c)
            out[0] = up_x + down_y(s + SXY, i, c, sxy) + down_z(sxz)
        if 1 in which:
            syz = at(s + SYZ, i, c)
            syy, szz = at(s + SYY, i, c), at(s + SZZ, i, c)
            down_sxy = sxy - at(s + SXY, i - 1, c)
            down_sxz = sxz - at(s + SXZ, i - 1, c)
            out[1] = down_sxy + up_y(s + SYY, i, c, syy) + down_z(syz)
            out[2] = down_sxz + down_y(s + SYZ, i, c, syz) + up_z(szz)
        return out

    def velocity_plane(i, which, slot=None, fresh=False, final=False):
        for c in range(chunks):
            buoyancy = mats[0, i, rows_of(c), :]
            both = [force(s, i, c, which) for s in (0, 9)]
            old = [[at(s + d, i, c) for d in range(3)] for s in (0, 9)]
            for d in which:
                for n, s in enumerate((0, 9)):
                    value = old[n][d] + buoyancy * both[n][d]
                    state[s + d, i, rows_of(c), :] = value
                    if final:
                        final_state[s + d, slot, rows_of(c), :] = value
            if slot is not None:
                term = both[0][0] * old[1][0] + both[0][1] * old[1][1] + both[0][2] * old[1][2]
                if not fresh:
                    term = acc[0, slot, rows_of(c), :] + term
                acc[0, slot, rows_of(c), :] = term

    def strain(s, i, c):
        vx, vy, vz = at(s + VX, i, c), at(s + VY, i, c), at(s + VZ, i, c)
        return [
            vx - at(s + VX, i - 1, c),
            down_y(s + VY, i, c, vy),
            down_z(vz),
            up_z(vy) + up_y(s + VZ, i, c, vz),
            up_z(vx) + (at(s + VZ, i + 1, c) - vz),
            up_y(s + VX, i, c, vx) + (at(s + VY, i + 1, c) - vy),
        ]

    def stress_chunk(i, c, step, slot=None, fresh=False, final=False, rim=None):
        m = [None] + [mats[k, i, rows_of(c), :] for k in range(1, 10)]
        both = []
        for s in (0, 9):
            e = strain(s, i, c)
            both.append(e)
            if s == 0:
                inject = wavelet[step] * image[i, rows_of(c), :]
            elif rim is None:
                inject = data[step, i - DEPTH, rows_of(c), :]
            else:
                inject = rim_data[rim[0], rim[1], rows_of(c), :]
            rates = [
                m[1] * e[0] + m[2] * e[1] + m[3] * e[2],
                m[2] * e[0] + m[4] * e[1] + m[5] * e[2],
                m[3] * e[0] + m[5] * e[1] + m[6] * e[2] + inject,
                m[7] * e[3],
                m[8] * e[4],
                m[9] * e[5],
            ]
            for f, rate in enumerate(rates):
                value = at(s + SXX + f, i, c) + rate
                if final:
                    final_state[s + SXX + f, slot, rows_of(c), :] = value
                else:
                    state[s + SXX + f, i, rows_of(c), :] = value
        if slot is None:
            return
        f, a = both
        terms = [
            f[0] * a[0],
            f[0] * a[1] + f[1] * a[0],
            f[0] * a[2] + f[2] * a[0],
            f[1] * a[1],
            f[1] * a[2] + f[2] * a[1],
            f[2] * a[2],
            f[3] * a[3],
            f[4] * a[4],
            f[5] * a[5],
        ]
        for n, term in enumerate(terms):
            if not fresh:
                term = acc[1 + n, slot, rows_of(c), :] + term
            if final:
                rows_ref[pl.ds(10 * slot + 1 + n + 8 * c * ROWS, 8, stride=ROWS), :] = scale * term
            else:
                acc[1 + n, slot, rows_of(c), :] = term
        if final:
            term = scale * acc[0, slot, rows_of(c), :]
            rows_ref[pl.ds(10 * slot + 8 * c * ROWS, 8, stride=ROWS), :] = term

    def over(begins, counts, one):
        (a, b), (n, m) = begins, counts
        if n + m:

            def turn(x, carry):
                one(jnp.where(x < n, a + x, b - n + x) if n and m else (a if n else b) + x)
                return carry

            lax.fori_loop(0, n + m, turn, 0)

    def velocity_own(begins, counts, fresh=False, final=False):
        over(begins, counts, lambda x: velocity_plane(DEPTH + x, (0, 1, 2), x, fresh, final))

    def stress_own(step, begins, counts, fresh=False, final=False):
        def one(x):
            for c in range(chunks):
                stress_chunk(DEPTH + x, c, step, x, fresh, final)

        over(begins, counts, one)

    def velocity_rims(step):
        n = DEPTH - 1 - step
        velocity_plane(step, (0,))
        over((step + 1, DEPTH + OWN), (n, n), lambda i: velocity_plane(i, (0, 1, 2)))
        velocity_plane(LENGTH - 1 - step, (1, 2))

    def stress_rims(step):
        n = DEPTH - 1 - step

        def one(i):
            above = i >= DEPTH + OWN
            distance = jnp.where(above, i - DEPTH - OWN, DEPTH - 1 - i)
            for c in range(chunks):
                stress_chunk(i, c, step, rim=(jnp.where(above, 1, 0), RIM_BASE[step] + distance))

        over((step + 1, DEPTH + OWN), (n, n), one)

    if part == "early":
        data_copy = pltpu.make_async_copy(data_in, data, sems.at[HALO_COPIES])

        def start(below, above):
            for copy in halo_copies(state, lines, below, above, sems):
                copy.start()

        by_parity(lambda: start(chip_in, cross_in), lambda: start(cross_in, chip_in))
        data_copy.start()
        draw_image(encoding, cells, image)
        velocity_own((1, 0), (OWN - 2, 0), True)
        for copy in halo_copies(state, lines, cross_in, chip_in, sems):
            copy.wait()
        data_copy.wait()
        whole_lane = lax.broadcasted_iota(jnp.int32, (y_rows, z_rows), 1)
        for side in range(2):
            for n in range(len(RIM_SLOTS)):
                line = lines[side]
                line = pltpu.roll(line, z_rows - RECEIVER_CELLS * n, 1) if n else line
                rim_data[side, n] = jnp.where(whole_lane < RECEIVER_CELLS, line, 0.0)
        velocity_own((0, OWN - 1), (1, 1), True)
        stress_own(0, (1, 0), (OWN - 2, 0), True)
        velocity_own((2, 0), (OWN - 4, 0))
        stress_own(1, (3, 0), (OWN - 6, 0))
        return
    drain_rims(mats, cross_in, chip_in)
    velocity_rims(0)
    stress_rims(0)
    stress_own(0, (0, OWN - 1), (1, 1), True)
    velocity_rims(1)
    velocity_own((0, OWN - 2), (2, 2))
    stress_rims(1)
    stress_own(1, (0, OWN - 3), (3, 3))
    velocity_rims(2)
    velocity_own((0, 0), (OWN, 0))
    stress_rims(2)
    stress_own(2, (0, 0), (OWN, 0))
    velocity_rims(3)
    velocity_own((0, 0), (OWN, 0), False, True)
    copies = []

    def send(source, target):
        copies.append(pltpu.make_async_copy(source, target, sems.at[len(copies)]))
        copies[-1].start()

    for side, out in enumerate((forward, adjoint)):
        send(final_state.at[pl.ds(9 * side, SXX)], out.at[pl.ds(0, SXX)])
    for n in range(2):
        stress_own(3, (n * OWN // 2, 0), (OWN // 2, 0), False, True)
        half = pl.ds(n * ROWS // 2, ROWS // 2)
        send(rows_ref.reshape(y_rows, ROWS, z_rows).at[:, half], packed.at[:, half])
        layers = pl.ds(n * OWN // 2, OWN // 2)
        for side, out in enumerate((forward, adjoint)):
            send(final_state.at[pl.ds(9 * side + SXX, 6), layers], out.at[pl.ds(SXX, 6), layers])
    for copy in copies:
        copy.wait()


def sum_kernel(tiles, out, rows_ref, total, sems):
    parts = tiles.shape[0] // 8
    copies = [
        pltpu.make_async_copy(tiles.at[pl.ds(8 * n, 8)], rows_ref.at[pl.ds(8 * n, 8)], sems.at[n])
        for n in range(parts)
    ]
    for copy in copies:
        copy.start()
    for n in range(parts):
        copies[n].wait()
        for g in range(ROWS // 8):
            rows = pl.ds(8 * g, 8)
            values = [rows_ref[8 * n + j, rows, :] for j in range(8)]
            while len(values) > 1:
                values = [a + b for a, b in zip(values[::2], values[1::2])]
            total[rows, :] = values[0] if n == 0 else total[rows, :] + values[0]
    for m in range(10):
        out[pl.ds(OWN * m, OWN), :] = total[pl.ds(m, OWN, stride=10), :]


def in_vmem(x):
    return pltpu.with_memory_space_constraint(x, VMEM)


def in_hbm(x):
    return pltpu.with_memory_space_constraint(x, pltpu.HBM)


WHOLE = pl.BlockSpec(memory_space=VMEM)
SCALARS = pl.BlockSpec(memory_space=pltpu.SMEM)
ANYWHERE = pl.BlockSpec(memory_space=pl.ANY)
IN_HBM = pl.BlockSpec(memory_space=pltpu.HBM)


def estimate(flops, moved):
    return pl.CostEstimate(flops=flops, bytes_accessed=moved, transcendentals=0)


def run_phase(part, scalars, state, middle, far):
    y_rows, z_rows = state.shape[2:]
    count = len(scalars)
    outs = [VMEM(state.shape, jnp.float32), VMEM((10, OWN, y_rows, z_rows), jnp.float32)]
    aliases = {count: 0}
    if part == "early":
        outs += [
            VMEM((LENGTH, y_rows, z_rows), jnp.float32),
            VMEM((2, len(RIM_SLOTS), y_rows, z_rows), jnp.float32),
            VMEM((STEPS, OWN, y_rows, z_rows), jnp.float32),
        ]
        out_specs = [WHOLE] * len(outs)
        scratch = [VMEM((2, y_rows, z_rows), jnp.float32), pltpu.SemaphoreType.DMA((HALO_COPIES + 1,))]
    else:
        outs += [
            VMEM((10, LENGTH, y_rows, z_rows), jnp.float32),
            pltpu.HBM((state.shape[0] // 2, OWN, y_rows, z_rows), jnp.float32),
            pltpu.HBM((state.shape[0] // 2, OWN, y_rows, z_rows), jnp.float32),
            pltpu.HBM((y_rows, ROWS, z_rows), jnp.float32),
        ]
        aliases.update({count + 1: 1, count + 2: 2})
        scratch = [
            VMEM((y_rows * ROWS, z_rows), jnp.float32),
            VMEM((state.shape[0], OWN, y_rows, z_rows), jnp.float32),
            pltpu.SemaphoreType.DMA((8,)),
        ]
        out_specs = [WHOLE] * 3 + [IN_HBM] * 3
    cells = 12 * y_rows * z_rows
    return pl.pallas_call(
        functools.partial(phase_kernel, part, y_rows, z_rows),
        out_shape=tuple(outs),
        in_specs=[SCALARS] * count + [WHOLE] * (1 + len(middle)) + [ANYWHERE] * len(far),
        out_specs=tuple(out_specs),
        scratch_shapes=scratch,
        input_output_aliases=aliases,
        cost_estimate=estimate(160 * cells, 100 * cells),
        compiler_params=pltpu.CompilerParams(vmem_limit_bytes=6 << 20),
        name="steps_" + part,
    )(*scalars, in_vmem(state), *[in_vmem(x) for x in middle], *far)


def swap_across(value):
    peers = lax.axis_size("slab")
    return lax.ppermute(value, "slab", [p for i in range(1, peers - 1, 2) for p in ((i, i + 1), (i + 1, i))])


def swap_on_chip(value):
    peers = lax.axis_size("slab")
    return lax.ppermute(value, "slab", [p for i in range(0, peers, 2) for p in ((i, i + 1), (i + 1, i))])


def body(
    forward_state,
    adjoint_state,
    materials,
    wavelet,
    encoding,
    source_cells,
    receiver_depth,
    receiver_data,
):
    _, comps, own, y_rows, z_rows = forward_state.shape
    shots = lax.axis_size("shot")
    small = pltpu.CompilerParams(vmem_limit_bytes=2 << 20)

    copies = pl.pallas_call(
        spread_kernel,
        out_shape=pltpu.HBM((shots, ROWS, z_rows), jnp.float32),
        in_specs=[IN_HBM],
        out_specs=IN_HBM,
        scratch_shapes=[
            VMEM((ROWS, z_rows), jnp.float32),
            pltpu.SemaphoreType.DMA,
            pltpu.SemaphoreType.DMA((shots,)),
        ],
        cost_estimate=estimate(1000, 4 * shots * ROWS * z_rows),
        compiler_params=small,
        name="spread",
    )(in_hbm(materials.reshape(ROWS, z_rows)))
    gathered = lax.all_to_all(copies, "shot", split_axis=0, concat_axis=0, tiled=True)

    z_at = lax.broadcasted_iota(jnp.int32, (own, y_rows, z_rows), 2)
    probe = z_at == receiver_depth[:, :, None]
    data = jnp.where(probe[None], receiver_data[0][:, :, :, None], 0.0)

    payload = pltpu.HBM((PAYLOAD, y_rows, z_rows), jnp.float32)
    moved = 8 * comps * own * y_rows * z_rows
    fields = [in_hbm(forward_state[0]), in_hbm(adjoint_state[0])]
    cross, chip = pl.pallas_call(
        stage_kernel,
        out_shape=(payload, payload),
        in_specs=[IN_HBM, IN_HBM, WHOLE],
        out_specs=(IN_HBM, IN_HBM),
        scratch_shapes=[
            VMEM((2 * comps, own, y_rows, z_rows), jnp.float32),
            VMEM((2, y_rows, z_rows), jnp.float32),
            pltpu.SemaphoreType.DMA((4 * comps + 2,)),
        ],
        cost_estimate=estimate(1000, moved),
        compiler_params=pltpu.CompilerParams(vmem_limit_bytes=4 << 20),
        name="stage",
    )(*fields, in_vmem(data))
    cross, chip = swap_across(cross), swap_on_chip(chip)

    chunks = y_rows // 8
    rim = VMEM((RIM_PLANES, y_rows, z_rows), jnp.float32)
    mats, far, near, state = pl.pallas_call(
        turn_kernel,
        out_shape=(
            VMEM((10, LENGTH, y_rows, z_rows), jnp.float32),
            rim,
            rim,
            VMEM((2 * comps, LENGTH, y_rows, z_rows), jnp.float32),
        ),
        in_specs=[ANYWHERE, IN_HBM, IN_HBM],
        out_specs=(WHOLE,) * 4,
        scratch_shapes=[
            VMEM((chunks, 8 * ROWS, z_rows), jnp.float32),
            pltpu.SemaphoreType.DMA((chunks + 2 * comps,)),
        ],
        cost_estimate=estimate(1000, 8 * shots * ROWS * z_rows),
        compiler_params=pltpu.CompilerParams(vmem_limit_bytes=4 << 20),
        name="turn",
    )(gathered.reshape(chunks, 8 * ROWS, z_rows), *fields)
    far, near = swap_across(far), swap_on_chip(near)
    scalars = (wavelet, encoding, source_cells)
    state, acc, image, rim_data, data = run_phase("early", scalars, state, [mats], [cross, chip, data])
    middle = [acc, mats, far, near, image, rim_data, data]
    _, _, _, forward_out, adjoint_out, packed = run_phase("rest", (wavelet,), state, middle, [])

    tiles = lax.all_to_all(packed, "shot", 0, 0, tiled=True)
    gradient = pl.pallas_call(
        sum_kernel,
        out_shape=jax.ShapeDtypeStruct((ROWS, z_rows), jnp.float32),
        in_specs=[ANYWHERE],
        out_specs=WHOLE,
        scratch_shapes=[
            VMEM((shots, ROWS, z_rows), jnp.float32),
            VMEM((ROWS, z_rows), jnp.float32),
            pltpu.SemaphoreType.DMA((shots // 8,)),
        ],
        cost_estimate=estimate(shots * ROWS * z_rows, 4 * shots * ROWS * z_rows),
        compiler_params=pltpu.CompilerParams(vmem_limit_bytes=4 << 20),
        name="sum",
    )(tiles)
    gradient = gradient.reshape(10, own, 1, z_rows)
    return forward_out[None], adjoint_out[None], gradient


def solution(mesh):
    state_spec = P("shot", None, "slab", None, None)
    return jax.shard_map(
        body,
        mesh=mesh,
        in_specs=(
            state_spec,
            state_spec,
            P(None, "slab", "shot", None),
            P(),
            P("shot", None),
            P("shot", None),
            P("slab", None),
            P("shot", None, "slab", None),
        ),
        out_specs=(state_spec, state_spec, P(None, "slab", "shot", None)),
        check_vma=False,
    )
```

time: 85.7 us -> 83.1 us (0.970)
  blocking collectives: 0 us -> 23.5 us
  waiting for transfers between devices: 29.8 us -> 12.7 us
  starting transfers between devices: 31.1 us -> 21.2 us
  Pallas kernels: 21.3 us -> 24.1 us
  local copies, waits for them, and re-layouts: 1.75 us -> 0.02 us
    all_to_all x0 -> x1, blocking collectives: none -> 23.5 us  [body(): tiles = lax.all_to_all(packed, 'shot', 0, 0, tiled=True)]
    all_to_all x1 -> x0, waiting for transfers between devices: 13.2 us -> none  [body(): tiles = lax.all_to_all(packed, 'shot', 0, 0, tiled=True)]
    all_to_all x1 -> x0, starting transfers between devices: 5.09 us -> none  [body(): tiles = lax.all_to_all(packed, 'shot', 0, 0, tiled=True)]
    ppermute x3 -> x2, starting transfers between devices: 15.9 us -> 11.3 us  [swap_across(): lax.ppermute(value, 'slab', [p for i in range(1, peers - 1, 2) for p in (...]
    ppermute x3 -> x2, waiting for transfers between devices: 6.96 us -> 3.3 us  [swap_across(): lax.ppermute(value, 'slab', [p for i in range(1, peers - 1, 2) for p in (...]
    pallas_call x3 -> x2, Pallas kernels: 11.3 us -> 14.8 us  [run_phase(): pl.pallas_call(functools.partial(phase_kernel, part, y_rows, z_rows), out...]
    broadcast_in_dim x1 -> x0, local copies, waits for them, and re-layouts: 1.71 us -> none  [body(): adjoint_out = state[None, comps:, DEPTH:DEPTH + own]]
    pallas_call x1, Pallas kernels: 1.51 us -> 2.64 us  [body(): pl.pallas_call(turn_kernel, out_shape=(VMEM((10, LENGTH, y_rows, z_rows),...]
  transfers between devices with their start and end apart: 8 -> 5, of which waited for: 3 -> 3; matrix products, arithmetic and copies ran while one was open for 2% -> 0% of each run, Pallas kernels for 10% -> 13%
where the time goes in v4:
time: 83.1 us; the launch traced here: 82.6 us
  Pallas kernels  24.1 us (29%)
  blocking collectives  23.5 us (28%)
  starting transfers between devices  21.2 us (26%)
  waiting for transfers between devices  12.7 us (15%)
    all_to_all x1, blocking collectives, body(): tiles = lax.all_to_all(packed, 'shot', 0, 0, tiled=True)  23.5 us
    pallas_call x2, Pallas kernels, run_phase(): pl.pallas_call(functools.partial(phase_kernel, part, y_rows, z_rows), out...  14.8 us
    ppermute x2, starting transfers between devices, swap_across(): lax.ppermute(value, 'slab', [p for i in range(1, peers - 1, 2) for p in (...  11.3 us
    all_to_all x1, starting transfers between devices, body(): lax.all_to_all(copies, 'shot', split_axis=0, concat_axis=0, tiled=True)  9.81 us
    all_to_all x1, waiting for transfers between devices, body(): lax.all_to_all(copies, 'shot', split_axis=0, concat_axis=0, tiled=True)  9.36 us
    pallas_call x1, Pallas kernels, body(): pl.pallas_call(stage_kernel, out_shape=(payload, payload), in_specs=[IN_H...  3.33 us
    ppermute x2, waiting for transfers between devices, swap_across(): lax.ppermute(value, 'slab', [p for i in range(1, peers - 1, 2) for p in (...  3.3 us
    pallas_call x1, Pallas kernels, body(): pl.pallas_call(turn_kernel, out_shape=(VMEM((10, LENGTH, y_rows, z_rows),...  2.64 us
  transfers between devices with their start and end apart: 5, of which 3 were waited for; matrix products, arithmetic and copies ran while one was open for 0% of the time, Pallas kernels for 13%

profile of v4, /device:TPU:1, one launch (start us, length us, event | category | flops | bytes accessed | tf_op | source)
XLA Modules:
  0.0 82.6 jit_solution(16873567920925356720)
XLA Ops:
  0.6 2.1 %spread.1 = f32[32,80,128]{2,1,0:T(8,128)} custom-call(f32[80,128]{1,0:T(8,128)} %bitcast.15), custom_call_target="tpu_custom_call" | custom-call | flops 1000 | bytes 1310720 | tf_op jit(solution)/shard_map/spread/pallas_call | solution.py:505
  2.8 0.0 copy-start.4
  2.8 0.0 copy-start.3
  2.8 9.8 %all-to-all-start = ((f32[32,80,128]{2,1,0:T(8,128)}), f32[32,80,128]{2,1,0:T(8,128)S(1)}, u32[]{:S(2)}, u32[]{:S(2)}) async-start(f32[32,80,128]{2,1,0:T(8,128)} %spread.1), calls=%async_computation | async-start | bytes 2621440 | tf_op jit(solution)/shard_map/all_to_all | solution.py:519
  12.6 0.0 copy-done.4
  12.6 0.1 iota_compare_fusion
  12.7 0.0 copy-done.3
  12.8 0.2 broadcast_select_fusion.data.refs_7_
  13.0 3.3 %stage.1 = (f32[71,32,128]{2,1,0:T(8,128)}, f32[71,32,128]{2,1,0:T(8,128)}) custom-call(f32[9,8,32,128]{3,2,1,0:T(8,128)} %bitcast.11, f32[9,8,32,128]{3,2,1,0:T(8,128)} %bitcast.13, f32[4,8,32,128]{3,2,1,0:T(8,128)S(1)} %broadcast_select_fusion.data.refs_7_), custom_call_target="tpu_custom_call" | custom-call | flops 1000 | bytes 2359296 | tf_op jit(solution)/shard_map/stage/pallas_call | solution.py:528
  16.3 5.2 %collective-permute-start = (f32[71,32,128]{2,1,0:T(8,128)}, f32[71,32,128]{2,1,0:T(8,128)S(1)}, u32[]{:S(2)}, u32[]{:S(2)}) collective-permute-start(f32[71,32,128]{2,1,0:T(8,128)} %get-tuple-element.19), channel_id=1, source_target_pairs={{1,2},{2,1},{5,6},{6,5},{9,10},{10,9},{13,14},{14,13},{17,18},{18,... | collective-permute-start | bytes 3489800 | tf_op jit(solution)/shard_map/ppermute | solution.py:483
  21.5 0.1 collective-permute-start.1
  21.6 9.4 %all-to-all-done = f32[32,80,128]{2,1,0:T(8,128)S(1)} async-done(((f32[32,80,128]{2,1,0:T(8,128)}), f32[32,80,128]{2,1,0:T(8,128)S(1)}, u32[]{:S(2)}, u32[]{:S(2)}) %all-to-all-start) | async-done | bytes 1310752 | tf_op jit(solution)/shard_map/all_to_all | solution.py:519
  31.0 0.0 copy-start
  31.0 0.0 copy-start.1
  31.0 0.0 copy-start.2
  31.0 2.6 %turn.1 = (f32[10,16,32,128]{3,2,1,0:T(8,128)S(1)}, f32[31,32,128]{2,1,0:T(8,128)S(1)}, f32[31,32,128]{2,1,0:T(8,128)S(1)}, f32[18,16,32,128]{3,2,1,0:T(8,128)S(1)}) custom-call(f32[4,640,128]{2,1,0:T(8,128)S(1)} %bitcast.10, f32[9,8,32,128]{3,2,1,0:T(8,128)} %bitcast.12, f32[9,8,32,128]{3,2,1,0:T(8,128)} %bitcast.14), custom_call_target="tpu_custom_call" | custom-call | flops 1000 | bytes 2621440 | tf_op jit(solution)/shard_map/turn/pallas_call | solution.py:546
  33.6 6.1 %collective-permute-start.2 = (f32[31,32,128]{2,1,0:T(8,128)S(1)}, f32[31,32,128]{2,1,0:T(8,128)S(1)}, u32[]{:S(2)}, u32[]{:S(2)}) collective-permute-start(f32[31,32,128]{2,1,0:T(8,128)S(1)} %get-tuple-element.23), channel_id=1, source_target_pairs={{1,2},{2,1},{5,6},{6,5},{9,10},{10,9},{13,14},{14,13},{17,18},{18,... | collective-permute-start | bytes 1523720 | tf_op jit(solution)/shard_map/ppermute | solution.py:483
  39.7 0.1 collective-permute-start.3
  39.8 2.7 %collective-permute-done.refs_5_ = f32[71,32,128]{2,1,0:T(8,128)S(1)} collective-permute-done((f32[71,32,128]{2,1,0:T(8,128)}, f32[71,32,128]{2,1,0:T(8,128)S(1)}, u32[]{:S(2)}, u32[]{:S(2)}) %collective-permute-start) | collective-permute-done | bytes 1163296 | tf_op jit(solution)/shard_map/ppermute | solution.py:483
  42.5 0.0 collective-permute-done.1.refs_6_
  42.5 0.0 copy-done
  42.5 0.0 copy-done.1
  42.5 0.0 copy-done.2
  42.5 4.8 %steps_early.1 = (f32[18,16,32,128]{3,2,1,0:T(8,128)S(1)}, f32[10,8,32,128]{3,2,1,0:T(8,128)S(1)}, f32[16,32,128]{2,1,0:T(8,128)S(1)}, f32[2,6,32,128]{3,2,1,0:T(8,128)S(1)}, f32[4,8,32,128]{3,2,1,0:T(8,128)S(1)}) custom-call(f32[4]{0:T(128)S(1)} %copy-done, s32[1,16]{1,0:T(1,128)S(1)} %copy-done.1, ...), custom_call_target="tpu_custom_call", output_to_operand_aliasing={{0}: (3, {})} | custom-call | flops 7864320 | bytes 4915200 | tf_op jit(solution)/shard_map/steps_early/pallas_call | solution.py:468
  47.4 0.6 collective-permute-done.2.refs_4_
  47.9 0.0 collective-permute-done.3.refs_5_
  48.0 10.0 %steps_rest.1 = (f32[18,16,32,128]{3,2,1,0:T(8,128)S(1)}, f32[10,8,32,128]{3,2,1,0:T(8,128)S(1)}, f32[10,16,32,128]{3,2,1,0:T(8,128)S(1)}, f32[9,8,32,128]{3,2,1...) custom-call(f32[4]{0:T(128)S(1)} %copy-done, ...), custom_call_target="tpu_custom_call", output_to_operand_aliasing={{0}: (1, {}), {1}: (2, {}), {2}: (3, {})} | custom-call | flops 7864320 | bytes 4915200 | tf_op jit(solution)/shard_map/steps_rest/pallas_call | solution.py:468
  57.9 23.5 %all_to_all.10.tiles = f32[32,80,128]{2,1,0:T(8,128)S(1)} all-to-all(f32[32,80,128]{2,1,0:T(8,128)} %get-tuple-element.30), channel_id=1, replica_groups=mesh['shot'=32,'slab'=4] {'shot'}, dimensions={0} | all-to-all | bytes 2621440 | tf_op jit(solution)/shard_map/all_to_all | solution.py:570
  81.4 1.1 %sum.1 = f32[80,128]{1,0:T(8,128)} custom-call(f32[32,80,128]{2,1,0:T(8,128)S(1)} %all_to_all.10.tiles), custom_call_target="tpu_custom_call" | custom-call | flops 327680 | bytes 1310720 | tf_op jit(solution)/shard_map/sum/pallas_call | solution.py:571
Async XLA Ops:
  2.8 9.8 %copy-start.4 = (s32[8,32]{1,0:T(8,128)S(1)}, s32[8,32]{1,0:T(8,128)}, u32[]{:S(2)}) copy-start(s32[8,32]{1,0:T(8,128)} %param.14) | copy-start | bytes 3076
  2.8 10.0 %copy-start.3 = (f32[1,4,8,32]{3,2,1,0:T(8,128)S(1)}, f32[1,4,8,32]{3,2,1,0:T(8,128)}, u32[]{:S(2)}) copy-start(f32[1,4,8,32]{3,2,1,0:T(8,128)} %param.15) | copy-start | bytes 12292
  2.8 28.2 %all-to-all-start = ((f32[32,80,128]{2,1,0:T(8,128)}), f32[32,80,128]{2,1,0:T(8,128)S(1)}, u32[]{:S(2)}, u32[]{:S(2)}) async-start(f32[32,80,128]{2,1,0:T(8,128)} %spread.1), calls=%async_computation | async-start | bytes 2621440 | tf_op jit(solution)/shard_map/all_to_all | solution.py:519
  16.3 26.2 %collective-permute-start = (f32[71,32,128]{2,1,0:T(8,128)}, f32[71,32,128]{2,1,0:T(8,128)S(1)}, u32[]{:S(2)}, u32[]{:S(2)}) collective-permute-start(f32[71,32,128]{2,1,0:T(8,128)} %get-tuple-element.19), channel_id=1, source_target_pairs={{1,2},{2,1},{5,6},{6,5},{9,10},{10,9},{13,14},{14,13},{17,18},{18,... | collective-permute-start | bytes 3489800 | tf_op jit(solution)/shard_map/ppermute | solution.py:483
  21.5 21.0 %collective-permute-start.1 = (f32[71,32,128]{2,1,0:T(8,128)}, f32[71,32,128]{2,1,0:T(8,128)}, u32[]{:S(2)}, u32[]{:S(2)}) collective-permute-start(f32[71,32,128]{2,1,0:T(8,128)} %get-tuple-element.20), channel_id=1, source_target_pairs={{0,1},{1,0},{2,3},{3,2},{4,5},{5,4},{6,7},{7,6},{8,9},{9,8},{10,11... | collective-permute-start | bytes 3489800 | tf_op jit(solution)/shard_map/ppermute | solution.py:488
  31.0 11.5 %copy-start = (f32[4]{0:T(128)S(1)}, f32[4]{0:T(128)}, u32[]{:S(2)}) copy-start(f32[4]{0:T(128)} %refs_0_.3) | copy-start | bytes 52
  31.0 11.5 %copy-start.1 = (s32[1,16]{1,0:T(1,128)S(1)}, s32[1,16]{1,0:T(1,128)}, u32[]{:S(2)}) copy-start(s32[1,16]{1,0:T(1,128)} %refs_1_.1) | copy-start | bytes 196
  31.0 11.6 %copy-start.2 = (s32[1,16]{1,0:T(1,128)S(1)}, s32[1,16]{1,0:T(1,128)}, u32[]{:S(2)}) copy-start(s32[1,16]{1,0:T(1,128)} %refs_2_.1) | copy-start | bytes 196
  33.6 14.3 %collective-permute-start.2 = (f32[31,32,128]{2,1,0:T(8,128)S(1)}, f32[31,32,128]{2,1,0:T(8,128)S(1)}, u32[]{:S(2)}, u32[]{:S(2)}) collective-permute-start(f32[31,32,128]{2,1,0:T(8,128)S(1)} %get-tuple-element.23), channel_id=1, source_target_pairs={{1,2},{2,1},{5,6},{6,5},{9,10},{10,9},{13,14},{14,13},{17,18},{18,... | collective-permute-start | bytes 1523720 | tf_op jit(solution)/shard_map/ppermute | solution.py:483
  39.7 8.3 %collective-permute-start.3 = (f32[31,32,128]{2,1,0:T(8,128)S(1)}, f32[31,32,128]{2,1,0:T(8,128)S(1)}, u32[]{:S(2)}, u32[]{:S(2)}) collective-permute-start(f32[31,32,128]{2,1,0:T(8,128)S(1)} %get-tuple-element.24), channel_id=1, source_target_pairs={{0,1},{1,0},{2,3},{3,2},{4,5},{5,4},{6,7},{7,6},{8,9},{9,8},{10,11... | collective-permute-start | bytes 1523720 | tf_op jit(solution)/shard_map/ppermute | solution.py:488
